TPU v7x, 32 devices: a whole 2x2x4 slice. The times are simulated.
32 devices in a mesh: ctx: 8 (over z, x), fsdp: 4 (over y, core).
Axes of the slice: x: 2, y: 2, z: 4, core: 2. Of those that a mesh axis runs over, the one named last changes fastest.
Arguments:
- tokens: bfloat16 [4, 1024, 768], P('fsdp', 'ctx'), may hold values from -6 to 6
- block_order: int32 [4, 16], P('fsdp'), may hold values from 0 to 15, each once within a row
- attn_gain: bfloat16 [1, 768], P(None, ('ctx', 'fsdp')), may hold values from 0.5 to 1.5
- attn_shift: bfloat16 [1, 768], P(None, ('ctx', 'fsdp')), may hold values from -3 to 3
- w_qkv: bfloat16 [1, 768, 2304], P(None, ('ctx', 'fsdp')), may hold values from -2 to 2, as said below
- query_bias: bfloat16 [1, 768], P(None, ('ctx', 'fsdp')), may hold values from -3 to 3
- value_bias: bfloat16 [1, 768], P(None, ('ctx', 'fsdp')), may hold values from -0.59765625 to 0.59765625
- w_out: bfloat16 [1, 768, 768], P(None, ('ctx', 'fsdp')), may hold values from -1.75 to 1.75
- out_bias: bfloat16 [1, 768], P(None, ('ctx', 'fsdp')), may hold values from -4 to 4
- mlp_gain: bfloat16 [1, 768], P(None, ('ctx', 'fsdp')), may hold values from 0.5 to 1.5
- mlp_shift: bfloat16 [1, 768], P(None, ('ctx', 'fsdp')), may hold values from -3 to 3
- w_fc: bfloat16 [1, 768, 3072], P(None, ('ctx', 'fsdp')), may hold values from -0.21875 to 0.21875
- fc_bias: bfloat16 [1, 3072], P(None, ('ctx', 'fsdp')), may hold values from -3 to 3
- w_proj: bfloat16 [1, 3072, 768], P(None, ('ctx', 'fsdp')), may hold values from -0.109375 to 0.109375
- proj_bias: bfloat16 [1, 768], P(None, ('ctx', 'fsdp')), may hold values from -4 to 4
- cotangent: float32 [4, 1024, 768], P('fsdp', 'ctx'), may hold values from -6 to 6
Outputs:
- block_out: bfloat16 [4, 1024, 768], P('fsdp', 'ctx')
- input_grad: float32 [4, 1024, 768], P('fsdp', 'ctx')
- grad_attn_gain: float32 [1, 768], P(None, ('ctx', 'fsdp'))
- grad_attn_shift: float32 [1, 768], P(None, ('ctx', 'fsdp'))
- grad_w_qkv: float32 [1, 768, 2304], P(None, ('ctx', 'fsdp'))
- grad_query_bias: float32 [1, 768], P(None, ('ctx', 'fsdp'))
- grad_value_bias: float32 [1, 768], P(None, ('ctx', 'fsdp'))
- grad_w_out: float32 [1, 768, 768], P(None, ('ctx', 'fsdp'))
- grad_out_bias: float32 [1, 768], P(None, ('ctx', 'fsdp'))
- grad_mlp_gain: float32 [1, 768], P(None, ('ctx', 'fsdp'))
- grad_mlp_shift: float32 [1, 768], P(None, ('ctx', 'fsdp'))
- grad_w_fc: float32 [1, 768, 3072], P(None, ('ctx', 'fsdp'))
- grad_fc_bias: float32 [1, 3072], P(None, ('ctx', 'fsdp'))
- grad_w_proj: float32 [1, 3072, 768], P(None, ('ctx', 'fsdp'))
- grad_proj_bias: float32 [1, 768], P(None, ('ctx', 'fsdp'))
Inputs may be any that keep to these rules, and one draw needn't show every extreme that they name: `block_order`: each row is a permutation: every one of the 16 position blocks of a sequence is stored exactly once. `w_qkv`: entries are of order 768 ** -0.5.
All inputs are finite; a program needn't handle non-finite values.
Results may differ from a plain program's by a relative error of at most 0.02.
Values may be sent and summed in bfloat16 or wider, within the bound.
No kernel may reach another device: no remote copies, remote signals or barrier semaphores. Data moves between devices by JAX's collectives and lax.ppermute only.
A program may use at most 192 MiB of HBM per device.

v0:
```python
import functools

import jax
import jax.numpy as jnp
from jax import lax
from jax.experimental import pallas as pl
from jax.experimental.pallas import tpu as pltpu
from jax.sharding import PartitionSpec as P


D = 768
HEADS = 12
HEAD_DIM = 64


EPSILON = 1e-05
GELU_SCALE = 0.7978845608028654
GELU_CUBIC = 0.044715


def gelu_value(value):
    return 0.5 * value * (1.0 + jnp.tanh(GELU_SCALE * (value + GELU_CUBIC * value * value * value)))


def gelu_slope(value):
    tangent = jnp.tanh(GELU_SCALE * (value + GELU_CUBIC * value * value * value))
    return 0.5 * (1.0 + tangent) + 0.5 * value * (1.0 - tangent * tangent) * GELU_SCALE * (
        1.0 + 3.0 * GELU_CUBIC * value * value
    )


def true_positions(order, first, count, half):
    rows = first + jnp.arange(count, dtype=jnp.int32)
    blocks = rows // half
    table = blocks[:, None] == jnp.arange(order.shape[0], dtype=jnp.int32)[None, :]
    return jnp.sum(jnp.where(table, order[None, :], 0), axis=1) * half + rows % half


def norm_forward(state, gain, shift):
    centre = state - jnp.mean(state, axis=-1, keepdims=True)
    inverse = lax.rsqrt(jnp.mean(centre * centre, axis=-1, keepdims=True) + EPSILON)
    normed = centre * inverse
    return (normed * gain.astype(jnp.float32) + shift.astype(jnp.float32), normed, inverse)


def norm_backward(grad_out, normed, inverse, gain):
    scaled = grad_out * gain.astype(jnp.float32)
    return inverse * (
        scaled
        - jnp.mean(scaled, axis=-1, keepdims=True)
        - normed * jnp.mean(scaled * normed, axis=-1, keepdims=True)
    )


BF = jnp.bfloat16
F32 = jnp.float32
EXT = 128
AXES = ("ctx", "fsdp")


class Grid:
    def __init__(self, mesh):
        ctx, fsdp = mesh.shape["ctx"], mesh.shape["fsdp"]
        self.z = 4
        self.x = ctx // self.z
        self.y = fsdp // 2
        self.n = ctx * fsdp
        assert self.x == self.y and self.x * self.z == ctx

    def here(self):
        c, f = lax.axis_index("ctx"), lax.axis_index("fsdp")
        return c // self.x, c % self.x, f // 2, f % 2

    def index(self, z, x, y, k):
        return ((z % self.z * self.x + x % self.x) * self.y + y % self.y) * 2 + k % 2

    def send(self, value, move):
        pairs = [
            (self.index(z, x, y, k), self.index(*move(z, x, y, k)))
            for z in range(self.z)
            for x in range(self.x)
            for y in range(self.y)
            for k in range(2)
        ]
        return lax.ppermute(value, AXES, pairs)

    def core(self, value):
        return self.send(value, lambda z, x, y, k: (z, x, y, 1 - k))

    def along_z(self, value, step):
        return self.send(value, lambda z, x, y, k: (z + step, x, y, k))

    def along_x(self, value, step):
        return self.send(value, lambda z, x, y, k: (z, x + step, y, k))

    def first(self, value, step):
        return self.send(value, lambda z, x, y, k: (z, x + step, y, k) if k == 0 else (z, x, y + step, k))

    def second(self, value, step):
        return self.send(value, lambda z, x, y, k: (z, x, y + step, k) if k == 0 else (z, x + step, y, k))

    def z_far(self, value):
        return self.send(value, lambda z, x, y, k: (z, x, y, k) if k == 0 else (z + 1, x, y, k))

    def z_near(self, value):
        return self.send(value, lambda z, x, y, k: (z + 2, x, y, k) if k == 0 else (z + 3, x, y, k))


def gather(grid, shard, widths):
    rows, _ = shard.shape
    core = grid.here()[3]
    other = grid.core(shard)
    pair = jnp.where(core == 0, jnp.stack([shard, other]), jnp.stack([other, shard]))
    base = jnp.stack([grid.z_far(pair), grid.z_near(pair)])
    reached = {}
    for i in range(grid.x):
        reached[i, 0] = base if i == 0 else grid.first(base, i)
        for j in range(1, grid.y):
            reached[i, j] = grid.second(reached[i, 0], j)
    own = [reached[i, j] for i in range(grid.x) for j in range(grid.y)]
    parts = own + [grid.core(part) for part in own]
    offsets = [sum(widths[:at]) for at in range(len(widths))]
    X, Y, Z = grid.x, grid.y, grid.z

    def kernel(*refs):
        ins, outs, sem = refs[: len(parts)], refs[len(parts) : -1], refs[-1]
        z, x, y, k = grid.here()
        copies = []
        for at, part in enumerate(ins):
            route = k if at < len(own) else 1 - k
            i, j = (at % len(own)) // Y, (at % len(own)) % Y
            dx = jnp.where(route == 0, i, j)
            dy = jnp.where(route == 0, j, i)
            sx, sy = (x - dx + X) % X, (y - dy + Y) % Y
            for near in range(2):
                sz = (z - 2 * near - route + Z) % Z
                place = (sz * X + sx) * Y + sy
                for out, low, width in zip(outs, offsets, widths):
                    copies.append(
                        pltpu.make_async_copy(
                            part.at[near, :, :, pl.ds(low, width)],
                            out.at[place],
                            sem.at[len(copies)],
                        )
                    )
        for copy in copies:
            copy.start()
        for copy in copies:
            copy.wait()

    whole = pl.pallas_call(
        kernel,
        in_specs=[pl.BlockSpec(memory_space=pl.ANY)] * len(parts),
        out_specs=[pl.BlockSpec(memory_space=pltpu.VMEM)] * len(widths),
        out_shape=[jax.ShapeDtypeStruct((grid.n // 2, 2, rows, width), shard.dtype) for width in widths],
        scratch_shapes=[pltpu.SemaphoreType.DMA((len(parts) * 2 * len(widths),))],
        compiler_params=pltpu.CompilerParams(vmem_limit_bytes=16 * 1024 * 1024),
    )(*parts)
    return [item.reshape(grid.n * rows, width) for item, width in zip(whole, widths)]


def add_parts(terms, lead, blocks):
    rows, width = terms[0][0].shape[-2:]

    def kernel(*refs):
        total = refs[0][...].astype(F32)
        for ref in refs[1:-1]:
            total = total + ref[...].astype(F32)
        refs[-1][...] = total.astype(BF)

    return pl.pallas_call(
        kernel,
        grid=(blocks,),
        in_specs=[pl.BlockSpec((None, lead, rows, width), where) for _, where in terms],
        out_specs=pl.BlockSpec((None, lead, rows, width), lambda g: (g, 0, 0, 0)),
        out_shape=jax.ShapeDtypeStruct((blocks, lead, rows, width), BF),
        compiler_params=pltpu.CompilerParams(vmem_limit_bytes=24 * 1024 * 1024),
    )(*[array for array, _ in terms])


def scatter(grid, pairs, extra=()):
    n = grid.n
    X, Y, Z = grid.x, grid.y, grid.z
    rows = pairs[0][0].shape[1] // n
    chunk = 2 * Y * rows
    widths = [right.shape[1] for _, right in pairs]
    offsets = [sum(widths[:at]) for at in range(len(widths))]
    lefts = [left for left, _ in pairs]
    rights = [right for _, right in pairs]
    total = sum(widths) + (EXT if extra else 0)
    inputs = 2 * len(pairs) + len(extra)

    def kernel(*refs):
        left_refs, right_refs, line_refs = refs[: len(pairs)], refs[len(pairs) : 2 * len(pairs)], refs[2 * len(pairs) : inputs]
        outs, turned = refs[inputs : inputs + 2 * X], refs[inputs + 2 * X :]
        z, x, y, k = grid.here()
        for left, turn in zip(left_refs, turned):
            turn[...] = left[...].T
        if line_refs:
            lines, tail = turned[len(pairs) :]
            lines[...] = jnp.zeros(lines.shape, F32)
            at = 0
            for line in line_refs:
                lines[at : at + line.shape[0], :] = line[...]
                at += line.shape[0]
            tail[...] = lines[...].T
        for other in range(2):
            route = k if other == 0 else 1 - k

            def step(at, carry):
                near, dx = at // X, at % X
                tz, tx = (z + 2 * near + route) % Z, (x + dx) % X
                low_row = (tz * X + tx) * chunk
                if rows % 8 == 0:
                    low_row = pl.multiple_of(low_row, chunk)
                made = [
                    product(left[pl.ds(low_row, chunk), :], right[...], ((1,), (0,)))
                    for left, right in zip(turned, right_refs)
                ]
                ends = [tail[pl.ds(low_row, chunk), :]] if line_refs else []

                def store(out, ty, spot):
                    for core in range(2):
                        at = 2 * ty + core
                        span = slice(at * rows, (at + 1) * rows)
                        for value, low, width in zip(made, offsets, widths):
                            out[spot, 2 * near + core, :, low : low + width] = value[span].astype(BF)
                        for value in ends:
                            out[spot, 2 * near + core, :, sum(widths) :] = value[span].astype(BF)

                for ty in range(Y):
                    dy = (ty - y + Y) % Y
                    i = jnp.where(route == 0, dx, dy)
                    j = jnp.where(route == 0, dy, dx)
                    for at in range(X):
                        pl.when(i == at)(functools.partial(store, outs[other * X + at], ty, j))
                return carry

            lax.fori_loop(0, 2 * X, step, 0)

    shape = jax.ShapeDtypeStruct((Y, 4, rows, total), BF)
    vmem = pl.BlockSpec(memory_space=pltpu.VMEM)
    scratch = [pltpu.VMEM((left.shape[1], left.shape[0]), BF) for left in lefts]
    if extra:
        scratch += [pltpu.VMEM((EXT, n * rows), F32), pltpu.VMEM((n * rows, EXT), F32)]
    made = pl.pallas_call(
        kernel,
        in_specs=[vmem] * inputs,
        out_specs=[vmem] * (2 * X),
        out_shape=[shape] * (2 * X),
        scratch_shapes=scratch,
        compiler_params=pltpu.CompilerParams(vmem_limit_bytes=24 * 1024 * 1024),
    )(*lefts, *rights, *extra)
    mine, theirs = made[:X], made[X:]
    came = [None] * X
    for i in list(range(1, X)) + [0]:
        came[i] = grid.core(theirs[i])
    got = []
    for i in range(1, X):
        one = add_parts([(item, lambda g: (g, 0, 0, 0)) for item in (mine[i], came[i])], 4, Y)
        got.append(grid.first(one, i))

    def pick(j):
        return lambda g: (j, g, 0, 0)

    held = [mine[0], came[0]] + got
    final = [(item, 0) for item in held]
    for j in range(1, Y):
        two = add_parts([(item, pick(j)) for item in held], 2, 2).reshape(1, 4, rows, total)
        final.append((grid.second(two, j), 0))
    half = [add_parts([(item, lambda g, near=near: (0, near, 0, 0)) for item, _ in final], 2, 1)[0] for near in range(2)]
    four = grid.z_far(half[0]).astype(F32) + grid.z_near(half[1]).astype(F32)
    core = grid.here()[3]
    kept = jnp.where(core == 0, four[0], four[1])
    sent = jnp.where(core == 0, four[1], four[0]).astype(BF)
    return kept + grid.core(sent).astype(F32)


def product(left, right, dims):
    return lax.dot_general(left, right, (dims, ((), ())), preferred_element_type=F32)


def simple(kernel, ins, outs):
    vmem = pl.BlockSpec(memory_space=pltpu.VMEM)
    return pl.pallas_call(
        kernel,
        in_specs=[vmem] * len(ins),
        out_specs=[vmem] * len(outs),
        out_shape=[jax.ShapeDtypeStruct(shape, kind) for shape, kind in outs],
        compiler_params=pltpu.CompilerParams(vmem_limit_bytes=24 * 1024 * 1024),
    )(*ins)


def split_groups(grid, value, bias, sets):
    count, Z = value.shape[0], grid.z
    group = D // Z

    def kernel(*refs):
        outs = refs[-Z:]
        z = grid.here()[0]

        def write(first):
            for dz in range(Z):
                for part in range(sets):
                    low = part * D + (first + dz) % Z * group
                    item = refs[0][:, low : low + group]
                    if bias is not None:
                        item = item + refs[1][:, low : low + group]
                    outs[dz][:, part * group : (part + 1) * group] = item.astype(BF)

        for first in range(Z):
            pl.when(z == first)(functools.partial(write, first))

    ins = [value] if bias is None else [value, bias]
    return simple(kernel, ins, [((count, sets * group), BF)] * Z)


def join_groups(grid, pieces, sets):
    count, Z = pieces[0].shape[0], grid.z
    group = D // Z

    def kernel(*refs):
        out, sums = refs[Z:]
        z = grid.here()[0]

        def write(first):
            for dz in range(Z):
                for part in range(sets):
                    low = part * D + (first + dz) % Z * group
                    item = refs[dz][:, part * group : (part + 1) * group]
                    out[:, low : low + group] = item
                    sums[:, low : low + group] = jnp.sum(item.astype(F32), axis=0, keepdims=True)

        for first in range(Z):
            pl.when(z == first)(functools.partial(write, first))

    return simple(kernel, pieces, [((count, sets * D), BF), ((1, sets * D), F32)])


def attend(pieces, keys, query_pos, key_pos, heads):
    Z, step = len(pieces), pieces[0].shape[0]
    group = heads * HEAD_DIM
    scale = HEAD_DIM ** (-0.5)

    def kernel(*refs):
        piece_refs, key_refs = refs[:Z], refs[Z : Z + len(keys)]
        row_ref, col_ref, mixed_ref, lse_ref = refs[Z + len(keys) : Z + len(keys) + 4]
        sent = refs[Z + len(keys) + 4 :]
        for head in range(heads):
            low = head * HEAD_DIM
            cols = slice(low, low + HEAD_DIM)
            k = jnp.concatenate([ref[:, cols] for ref in key_refs], axis=0)
            v = jnp.concatenate([ref[:, group + low : group + low + HEAD_DIM] for ref in key_refs], axis=0)
            for at in range(Z):
                rows = slice(at * step, (at + 1) * step)
                q = piece_refs[at][:, cols]
                allowed = row_ref[rows] >= col_ref[...]
                scores = jnp.where(allowed, product(q, k, ((1,), (1,))) * scale, -jnp.inf)
                top = jnp.max(scores, axis=1, keepdims=True)
                probs = jnp.exp(scores - top)
                total = jnp.sum(probs, axis=1, keepdims=True)
                mixed = product(probs.astype(BF), v, ((1,), (0,))) / total
                mixed_ref[rows, cols] = mixed
                sent[at][:, cols] = mixed.astype(BF)
                lse_ref[rows, head : head + 1] = top + jnp.log(total)

    outs = [((Z * step, group), F32), ((Z * step, heads), F32)] + [((step, group), BF)] * Z
    made = simple(kernel, [*pieces, *keys, query_pos[:, None], key_pos[None]], outs)
    return made[0], made[1], made[2:]


def attend_back(pieces, keys, query_pos, key_pos, mixed, lse, grads, heads):
    Z, step = len(pieces), pieces[0].shape[0]
    group = heads * HEAD_DIM
    scale = HEAD_DIM ** (-0.5)
    own = keys[0].shape[0]
    far = len(keys)

    def kernel(*refs):
        piece_refs, key_refs = refs[:Z], refs[Z : Z + far]
        row_ref, col_ref, mixed_ref, lse_ref = refs[Z + far : Z + far + 4]
        grad_refs = refs[Z + far + 4 : 2 * Z + far + 4]
        dq_ref, own_ref = refs[2 * Z + far + 4 : 2 * Z + far + 6]
        far_refs = refs[2 * Z + far + 6 :]
        for head in range(heads):
            low = head * HEAD_DIM
            cols = slice(low, low + HEAD_DIM)
            later = slice(group + low, group + low + HEAD_DIM)
            k = jnp.concatenate([ref[:, cols] for ref in key_refs], axis=0)
            v = jnp.concatenate([ref[:, later] for ref in key_refs], axis=0)
            dk = jnp.zeros((own * far, HEAD_DIM), F32)
            dv = jnp.zeros((own * far, HEAD_DIM), F32)
            for at in range(Z):
                rows = slice(at * step, (at + 1) * step)
                q = piece_refs[at][:, cols]
                g = grad_refs[at][:, cols]
                delta = jnp.sum(g.astype(F32) * mixed_ref[rows, cols], axis=1, keepdims=True)
                allowed = row_ref[rows] >= col_ref[...]
                scores = product(q, k, ((1,), (1,))) * scale
                soft = jnp.where(allowed, jnp.exp(scores - lse_ref[rows, head : head + 1]), 0.0)
                inner = product(g, v, ((1,), (1,)))
                slope = (soft * (inner - delta)).astype(BF)
                dq_ref[rows, cols] = (product(slope, k, ((1,), (0,))) * scale).astype(BF)
                dk = dk + product(slope, q, ((0,), (0,)))
                dv = dv + product(soft.astype(BF), g, ((0,), (0,)))
            dk = dk * scale
            own_ref[:, cols] = dk[:own]
            own_ref[:, later] = dv[:own]
            for at, ref in enumerate(far_refs):
                piece = slice((at + 1) * own, (at + 2) * own)
                ref[:, cols] = dk[piece].astype(BF)
                ref[:, later] = dv[piece].astype(BF)

    outs = [((Z * step, group), BF), ((own, 2 * group), F32)] + [((own, 2 * group), BF)] * (far - 1)
    ins = [*pieces, *keys, query_pos[:, None], key_pos[None], mixed, lse, *grads]
    made = simple(kernel, ins, outs)
    return made[0], made[1], made[2:]


def return_pieces(grad_q, own, came, Z):
    step, group = grad_q.shape[0] // Z, grad_q.shape[1]

    def kernel(*refs):
        outs = refs[-Z:]
        for at, out in enumerate(outs):
            rows = slice(at * step, (at + 1) * step)
            out[:, :group] = refs[0][rows]
            total = refs[1][rows]
            for ref in refs[2:-Z]:
                total = total + ref[rows].astype(F32)
            out[:, group:] = total.astype(BF)

    return simple(kernel, [grad_q, own, *came], [((step, 3 * group), BF)] * Z)


def pack_first(w_qkv, lines, spare, rows):
    width = w_qkv.shape[1]
    used = len(lines) + spare.shape[1] // rows

    def kernel(*refs):
        out = refs[-1]
        out[:, :width] = refs[0][...]
        items = [ref[...] for ref in refs[2:-1]]
        items += [refs[1][:, at * rows : (at + 1) * rows] for at in range(used - len(lines))]
        stacked = jnp.concatenate([item.astype(F32) for item in items] + [jnp.zeros((EXT - used, rows), F32)], axis=0)
        across = lax.broadcasted_iota(jnp.int32, (rows, rows), 0) == lax.broadcasted_iota(jnp.int32, (rows, rows), 1)
        out[:, width:] = product(across.astype(BF), stacked.astype(BF), ((1,), (1,))).astype(BF)

    return simple(kernel, [w_qkv, spare, *lines], [((rows, width + EXT), BF)])[0]


def local_step(
    grid,
    tokens,
    block_order,
    attn_gain,
    attn_shift,
    w_qkv,
    query_bias,
    value_bias,
    w_out,
    out_bias,
    mlp_gain,
    mlp_shift,
    w_fc,
    fc_bias,
    w_proj,
    proj_bias,
    cotangent,
):
    count = tokens.shape[1]
    half = count // 2
    order = block_order[0]
    Z, X = grid.z, grid.x
    z, x, _, _ = grid.here()
    group = D // Z
    heads = HEADS // Z

    rows = w_qkv.shape[1]
    small = [attn_gain, attn_shift, query_bias, value_bias, out_bias, mlp_gain, mlp_shift, proj_bias]
    used = 8 + fc_bias.shape[1] // rows
    w_joint, extra = gather(grid, pack_first(w_qkv[0], small, fc_bias, rows), [3 * D, EXT])
    w_mix, w_up = gather(grid, jnp.concatenate([w_out[0], w_fc[0]], axis=1), [D, w_fc.shape[2]])
    (w_down,) = gather(grid, w_proj[0], [D])
    extra = extra[:, :used].T
    gain_one, shift_one, bias_query, bias_value, bias_mix, gain_two, shift_two, bias_down = [extra[i] for i in range(8)]
    bias_up = jnp.transpose(extra[8:].reshape(used - 8, grid.n, rows), (1, 0, 2)).reshape(-1)

    def positions(dz, dx):
        owner = (z - dz + Z) % Z * X + (x - dx + X) % X
        return true_positions(order, owner * count, count, half)

    query_pos = jnp.concatenate([positions(dz, 0) for dz in range(Z)])
    key_pos = jnp.concatenate([positions(dz, dx) for dx in range(X) for dz in range(Z)])

    def spread(pieces):
        return [pieces[0]] + [grid.along_z(pieces[dz], dz) for dz in range(1, Z)]

    def collect(pieces):
        return [pieces[0]] + [grid.along_z(pieces[dz], -dz) for dz in range(1, Z)]

    state = tokens[0].astype(F32)
    normed_in, normed_one, inverse_one = norm_forward(state, gain_one, shift_one)
    first = normed_in.astype(BF)
    joint = jnp.dot(first, w_joint, preferred_element_type=F32)
    joint_bias = jnp.concatenate([bias_query, jnp.zeros_like(bias_query), bias_value]).astype(F32)[None]
    packed = spread(split_groups(grid, joint, joint_bias, 3))
    own_keys = jnp.concatenate([piece[:, group:] for piece in packed])
    all_keys = [own_keys] + [grid.along_x(own_keys, dx) for dx in range(1, X)]
    mixed_local, log_total, mixed_send = attend(packed, all_keys, query_pos, key_pos, heads)
    mixed_round, _ = join_groups(grid, collect(mixed_send), 1)

    middle = state + jnp.dot(mixed_round, w_mix, preferred_element_type=F32) + bias_mix.astype(F32)
    normed_mid, normed_two, inverse_two = norm_forward(middle, gain_two, shift_two)
    second = normed_mid.astype(BF)
    pre = jnp.dot(second, w_up, preferred_element_type=F32) + bias_up.astype(F32)
    hidden = gelu_value(pre).astype(BF)
    result = middle + jnp.dot(hidden, w_down, preferred_element_type=F32) + bias_down.astype(F32)
    block_out = result.astype(BF)[None]

    grad_state = cotangent[0]
    grad_proj_bias = jnp.sum(grad_state, axis=0)
    grad_round = grad_state.astype(BF)
    shard_proj = scatter(grid, [(hidden, grad_round)])
    grad_pre = jnp.einsum("td,fd->tf", grad_round, w_down, preferred_element_type=F32) * gelu_slope(pre)
    grad_fc_bias = jnp.sum(grad_pre, axis=0)
    grad_pre_round = grad_pre.astype(BF)
    grad_second = jnp.einsum("tf,df->td", grad_pre_round, w_up, preferred_element_type=F32)
    grad_mlp_gain = jnp.sum(grad_second * normed_two, axis=0)
    grad_mlp_shift = jnp.sum(grad_second, axis=0)
    grad_middle = grad_state + norm_backward(grad_second, normed_two, inverse_two, gain_two)
    grad_out_bias = jnp.sum(grad_middle, axis=0)
    middle_round = grad_middle.astype(BF)
    shard_mid = scatter(grid, [(mixed_round, middle_round), (second, grad_pre_round)])
    grad_mixed = jnp.einsum("td,cd->tc", middle_round, w_mix, preferred_element_type=F32).astype(BF)

    grad_local = spread(split_groups(grid, grad_mixed, None, 1))
    grad_q, grad_own, grad_far = attend_back(
        packed, all_keys, query_pos, key_pos, mixed_local, log_total, grad_local, heads
    )
    came = [grid.along_x(grad_far[dx - 1], -dx) for dx in range(1, X)]
    back = collect(return_pieces(grad_q, grad_own, came, Z))
    grad_joint, joint_sums = join_groups(grid, back, 3)
    grad_query_bias = joint_sums[:, :D]
    grad_value_bias = joint_sums[:, 2 * D :]
    grad_first = jnp.einsum("te,de->td", grad_joint, w_joint, preferred_element_type=F32)
    grad_attn_gain = jnp.sum(grad_first * normed_one, axis=0)
    grad_attn_shift = jnp.sum(grad_first, axis=0)
    grad_in = grad_middle + norm_backward(grad_first, normed_one, inverse_one, gain_one)

    vectors = [
        grad_attn_gain,
        grad_attn_shift,
        grad_query_bias,
        grad_value_bias,
        grad_out_bias,
        grad_mlp_gain,
        grad_mlp_shift,
        grad_proj_bias,
    ]
    vectors = [item.reshape(1, D) for item in vectors]
    vectors.append(jnp.transpose(grad_fc_bias.reshape(grid.n, used - 8, rows), (1, 0, 2)).reshape(used - 8, D))
    shard_first = scatter(grid, [(first, grad_joint)], vectors)
    shard_qkv, ends = shard_first[:, : 3 * D], shard_first[:, 3 * D :]
    small = [ends[:, i][None] for i in range(8)]
    return (
        block_out,
        grad_in[None],
        small[0],
        small[1],
        shard_qkv[None],
        small[2],
        small[3],
        shard_mid[None, :, :D],
        small[4],
        small[5],
        small[6],
        shard_mid[None, :, D:],
        ends[:, 8:used].T.reshape(1, -1),
        shard_proj[None],
        small[7],
    )


def solution(mesh):
    grid = Grid(mesh)

    def local(*args):
        return local_step(grid, *args)

    placed = (
        P("fsdp", "ctx", None),
        P("fsdp", None),
        P(None, ("ctx", "fsdp")),
        P(None, ("ctx", "fsdp")),
        P(None, ("ctx", "fsdp"), None),
        P(None, ("ctx", "fsdp")),
        P(None, ("ctx", "fsdp")),
        P(None, ("ctx", "fsdp"), None),
        P(None, ("ctx", "fsdp")),
        P(None, ("ctx", "fsdp")),
        P(None, ("ctx", "fsdp")),
        P(None, ("ctx", "fsdp"), None),
        P(None, ("ctx", "fsdp")),
        P(None, ("ctx", "fsdp"), None),
        P(None, ("ctx", "fsdp")),
        P("fsdp", "ctx", None),
    )
    return jax.shard_map(
        local,
        mesh=mesh,
        in_specs=placed,
        out_specs=(
            P("fsdp", "ctx", None),
            P("fsdp", "ctx", None),
            P(None, ("ctx", "fsdp")),
            P(None, ("ctx", "fsdp")),
            P(None, ("ctx", "fsdp"), None),
            P(None, ("ctx", "fsdp")),
            P(None, ("ctx", "fsdp")),
            P(None, ("ctx", "fsdp"), None),
            P(None, ("ctx", "fsdp")),
            P(None, ("ctx", "fsdp")),
            P(None, ("ctx", "fsdp")),
            P(None, ("ctx", "fsdp"), None),
            P(None, ("ctx", "fsdp")),
            P(None, ("ctx", "fsdp"), None),
            P(None, ("ctx", "fsdp")),
        ),
        check_vma=False,
    )
```

profile of v0, /device:TPU:0, one launch (start us, length us, event | category | flops | bytes accessed | tf_op | source)
XLA Modules:
  0.0 314.6 jit_solution(18095421186861831605)
XLA Ops:
  12.1 3.7 %collective-permute-start.2 = (bf16[2,24,2432]{2,1,0:T(8,128)(2,1)S(1)}, bf16[2,24,2432]{2,1,0:T(8,128)(2,1)S(1)}, u32[]{:S(2)}, u32[]{:S(2)}) collective-permute-start(bf16[2,24,2432]{2,1,0:T(8,128)(2,1)S(1)} %maximum_select_fusion.2), channel_id=1, source_target_pairs={{0,16},{1,25},{2,18},{3,27},{4,20},{5,29},{6,22},{7,31},{8,24},{9,... | collective-permute-start | bytes 700424 | tf_op jit(solution)/shard_map/ppermute | solution.py:85
  17.6 9.6 %collective-permute-done.2 = bf16[2,24,2432]{2,1,0:T(8,128)(2,1)S(1)} collective-permute-done((bf16[2,24,2432]{2,1,0:T(8,128)(2,1)S(1)}, bf16[2,24,2432]{2,1,0:T(8,128)(2,1)S(1)}, u32[]{:S(2)}, u32[]{:S(2)}) %collective-permute-start.2) | collective-permute-done | bytes 233504 | tf_op jit(solution)/shard_map/ppermute | solution.py:85
  29.7 3.0 collective-permute-start.19
  33.3 16.7 %collective-permute-done.29 = bf16[2,96,768]{2,1,0:T(8,128)(2,1)S(1)} collective-permute-done((bf16[2,96,768]{2,1,0:T(8,128)(2,1)S(1)}, bf16[2,96,768]{2,1,0:T(8,128)(2,1)S(1)}, u32[]{:S(2)}, u32[]{:S(2)}) %collective-permute-start.29) | collective-permute-done | bytes 294944 | tf_op jit(solution)/shard_map/ppermute | solution.py:85
  53.9 6.9 %collective-permute-done.19 = bf16[2,24,3840]{2,1,0:T(8,128)(2,1)S(1)} collective-permute-done((bf16[2,24,3840]{2,1,0:T(8,128)(2,1)S(1)}, bf16[2,24,3840]{2,1,0:T(8,128)(2,1)S(1)}, u32[]{:S(2)}, u32[]{:S(2)}) %collective-permute-start.19) | collective-permute-done | bytes 368672 | tf_op jit(solution)/shard_map/ppermute | solution.py:85
  82.5 13.5 %collective-permute-done.21.refs_2_ = bf16[2,2,24,3840]{3,2,1,0:T(8,128)(2,1)} collective-permute-done((bf16[2,2,24,3840]{3,2,1,0:T(8,128)(2,1)}, bf16[2,2,24,3840]{3,2,1,0:T(8,128)(2,1)}, u32[]{:S(2)}, u32[]{:S(2)}) %collective-permute-start.21) | collective-permute-done | bytes 737312 | tf_op jit(solution)/shard_map/ppermute | solution.py:85
  98.3 2.9 collective-permute-start.12
  101.2 7.1 %collective-permute-done.11.refs_2_ = bf16[128,576]{1,0:T(8,128)(2,1)} collective-permute-done((bf16[128,576]{1,0:T(8,128)(2,1)S(1)}, bf16[128,576]{1,0:T(8,128)(2,1)}, u32[]{:S(2)}, u32[]{:S(2)}) %collective-permute-start.11) | collective-permute-done | bytes 147488 | tf_op jit(solution)/shard_map/ppermute | solution.py:85
  116.8 8.1 %collective-permute-done.13.refs_5_ = bf16[512,384]{1,0:T(8,128)(2,1)S(1)} collective-permute-done((bf16[512,384]{1,0:T(8,128)(2,1)S(1)}, bf16[512,384]{1,0:T(8,128)(2,1)S(1)}, u32[]{:S(2)}, u32[]{:S(2)}) %collective-permute-start.13) | collective-permute-done | bytes 393248 | tf_op jit(solution)/shard_map/ppermute | solution.py:85
  126.3 6.3 %shard_map.274 = (f32[512,192]{1,0:T(8,128)S(1)}, f32[512,3]{1,0:T(8,128)S(1)}, bf16[128,192]{1,0:T(8,128)(2,1)S(1)}, bf16[128,192]{1,0:T(8,128)(2,1)S(1)}, bf16...) custom-call(bf16[128,576]{1,0:T(8,128)(2,1)S(1)} %copy-done.14, bf16[128,576]{1,0:T(8,128)(2,1)} %collective-permute-done.10.refs_1_, ...), custom_call_target="tpu_custom_call" | custom-call | tf_op jit(solution)/shard_map/pallas_call | solution.py:285
  136.4 4.3 %collective-permute-start.14 = (bf16[128,192]{1,0:T(8,128)(2,1)S(1)}, bf16[128,192]{1,0:T(8,128)(2,1)S(1)}, u32[]{:S(2)}, u32[]{:S(2)}) collective-permute-start(bf16[128,192]{1,0:T(8,128)(2,1)S(1)} %get-tuple-element.62), channel_id=1, source_target_pairs={{0,24},{1,25},{2,26},{3,27},{4,28},{5,29},{6,30},{7,31},{8,0},{9,1... | collective-permute-start | bytes 147464 | tf_op jit(solution)/shard_map/ppermute | solution.py:85
  144.6 5.3 %collective-permute-done.15.refs_2_ = bf16[128,192]{1,0:T(8,128)(2,1)S(1)} collective-permute-done((bf16[128,192]{1,0:T(8,128)(2,1)S(1)}, bf16[128,192]{1,0:T(8,128)(2,1)S(1)}, u32[]{:S(2)}, u32[]{:S(2)}) %collective-permute-start.15) | collective-permute-done | bytes 49184 | tf_op jit(solution)/shard_map/ppermute | solution.py:85
  162.3 3.1 shard_map.276
  174.6 3.8 %collective-permute-start.38 = (bf16[128,192]{1,0:T(8,128)(2,1)S(1)}, bf16[128,192]{1,0:T(8,128)(2,1)S(1)}, u32[]{:S(2)}, u32[]{:S(2)}) collective-permute-start(bf16[128,192]{1,0:T(8,128)(2,1)S(1)} %get-tuple-element.72), channel_id=1, source_target_pairs={{0,16},{1,17},{2,18},{3,19},{4,20},{5,21},{6,22},{7,23},{8,24},{9,... | collective-permute-start | bytes 147464 | tf_op jit(solution)/shard_map/ppermute | solution.py:85
  182.8 7.0 %shard_map.279 = (bf16[512,192]{1,0:T(8,128)(2,1)S(1)}, f32[512,384]{1,0:T(8,128)S(1)}, bf16[512,384]{1,0:T(8,128)(2,1)S(1)}) custom-call(bf16[128,576]{1,0:T(8,128)(2,1)S(1)} %copy-done.15, bf16[128,576]{1,0:T(8,128)(2,1)} %collective-permute-done.10.refs_1_, bf16[128,576]{1,0:T(8,128)(2,1)} %collective-permute-done.11.refs_2_, ...), custom_call_target="tpu_custom_call" | custom-call | tf_op jit(solution)/shard_map/pallas_call | solution.py:285
  190.3 7.3 %collective-permute-done.40.refs_2_ = bf16[512,384]{1,0:T(8,128)(2,1)S(1)} collective-permute-done((bf16[512,384]{1,0:T(8,128)(2,1)S(1)}, bf16[512,384]{1,0:T(8,128)(2,1)S(1)}, u32[]{:S(2)}, u32[]{:S(2)}) %collective-permute-start.40) | collective-permute-done | bytes 393248 | tf_op jit(solution)/shard_map/ppermute | solution.py:85
  199.3 3.8 %collective-permute-start.41 = (bf16[128,576]{1,0:T(8,128)(2,1)}, bf16[128,576]{1,0:T(8,128)(2,1)}, u32[]{:S(2)}, u32[]{:S(2)}) collective-permute-start(bf16[128,576]{1,0:T(8,128)(2,1)} %get-tuple-element.78), channel_id=1, source_target_pairs={{0,24},{1,25},{2,26},{3,27},{4,28},{5,29},{6,30},{7,31},{8,0},{9,1... | collective-permute-start | bytes 442376 | tf_op jit(solution)/shard_map/ppermute | solution.py:85
  211.3 3.2 %shard_map.292 = (bf16[2,4,96,768]{3,2,1,0:T(8,128)(2,1)S(1)}, bf16[2,4,96,768]{3,2,1,0:T(8,128)(2,1)S(1)}, bf16[2,4,96,768]{3,2,1,0:T(8,128)(2,1)S(1)}, bf16[2,4,96,768]{3,2,1,0:T(8,128)(2,1)S(1)}) custom-call(bf16[128,3072]{1,0:T(8,128)(2,1)S(1)} %copy-done.5, bf16[128,768]{1,0:T(8,128)(2,1)S(1)} %copy-done.20), custom_call_target="tpu_custom_call" | custom-call | tf_op jit(solution)/shard_map/pallas_call | solution.py:246
  222.6 3.6 %shard_map.287 = (bf16[2,4,24,3840]{3,2,1,0:T(8,128)(2,1)S(1)}, bf16[2,4,24,3840]{3,2,1,0:T(8,128)(2,1)S(1)}, bf16[2,4,24,3840]{3,2,1,0:T(8,128)(2,1)S(1)}, bf16[2,4,24,3840]{3,2,1,0:T(8,128)(2,1)S(1)}) custom-call(bf16[128,768]{1,0:T(8,128)(2,1)S(1)} %copy-done.17, bf16[128,768]{1,0:T(8,128)(2,1)S(1)} %copy-done.19, bf16[128,768]{1,0:T(8,128)(2,1)S(1)} %copy-done.10, ...), custom_call_target="tpu_custom_call" | custom-call | tf_op jit(solution)/shard_map/pallas_call | solution.py:246
  231.3 9.4 %collective-permute-done.46.refs_2_ = bf16[2,4,24,2432]{3,2,1,0:T(8,128)(2,1)S(1)} collective-permute-done((bf16[2,4,24,2432]{3,2,1,0:T(8,128)(2,1)S(1)}, bf16[2,4,24,2432]{3,2,1,0:T(8,128)(2,1)S(1)}, u32[]{:S(2)}, u32[]{:S(2)}) %collective-permute-start.46) | collective-permute-done | bytes 933920 | tf_op jit(solution)/shard_map/ppermute | solution.py:85
  243.4 14.9 %collective-permute-done.60.refs_2_ = bf16[2,4,96,768]{3,2,1,0:T(8,128)(2,1)S(1)} collective-permute-done((bf16[2,4,96,768]{3,2,1,0:T(8,128)(2,1)S(1)}, bf16[2,4,96,768]{3,2,1,0:T(8,128)(2,1)S(1)}, u32[]{:S(2)}, u32[]{:S(2)}) %collective-permute-start.60) | collective-permute-done | bytes 1179680 | tf_op jit(solution)/shard_map/ppermute | solution.py:85
  263.0 11.8 %collective-permute-done.61.refs_3_ = bf16[1,4,96,768]{3,2,1,0:T(8,128)(2,1)S(1)} collective-permute-done((bf16[1,4,96,768]{3,2,1,0:T(8,128)(2,1)S(1)}, bf16[1,4,96,768]{3,2,1,0:T(8,128)(2,1)S(1)}, u32[]{:S(2)}, u32[]{:S(2)}) %collective-permute-start.61) | collective-permute-done | bytes 589856 | tf_op jit(solution)/shard_map/ppermute | solution.py:85
  281.0 10.0 %collective-permute-done.63 = bf16[2,96,768]{2,1,0:T(8,128)(2,1)S(1)} collective-permute-done((bf16[2,96,768]{2,1,0:T(8,128)(2,1)S(1)}, bf16[2,96,768]{2,1,0:T(8,128)(2,1)S(1)}, u32[]{:S(2)}, u32[]{:S(2)}) %collective-permute-start.63) | collective-permute-done | bytes 294944 | tf_op jit(solution)/shard_map/ppermute | solution.py:85
  298.0 13.6 %collective-permute-done.56 = bf16[2,24,3840]{2,1,0:T(8,128)(2,1)S(1)} collective-permute-done((bf16[2,24,3840]{2,1,0:T(8,128)(2,1)S(1)}, bf16[2,24,3840]{2,1,0:T(8,128)(2,1)S(1)}, u32[]{:S(2)}, u32[]{:S(2)}) %collective-permute-start.56) | collective-permute-done | bytes 368672 | tf_op jit(solution)/shard_map/ppermute | solution.py:85
  (373 shorter events, 133.9 us)
Async XLA Ops:
  8.2 20.7 %collective-permute-start.27 = (bf16[96,768]{1,0:T(8,128)(2,1)}, bf16[96,768]{1,0:T(8,128)(2,1)S(1)}, u32[]{:S(2)}, u32[]{:S(2)}) collective-permute-start(bf16[96,768]{1,0:T(8,128)(2,1)} %bitcast.173), channel_id=1, source_target_pairs={{0,1},{1,0},{2,3},{3,2},{4,5},{5,4},{6,7},{7,6},{8,9},{9,8},{10,11... | collective-permute-start | bytes 442376 | tf_op jit(solution)/shard_map/ppermute | solution.py:85
  9.1 20.5 %collective-permute-start.17 = (bf16[24,3840]{1,0:T(8,128)(2,1)S(1)}, bf16[24,3840]{1,0:T(8,128)(2,1)S(1)}, u32[]{:S(2)}, u32[]{:S(2)}) collective-permute-start(bf16[24,3840]{1,0:T(8,128)(2,1)S(1)} %get-tuple-element.141), channel_id=1, source_target_pairs={{0,1},{1,0},{2,3},{3,2},{4,5},{5,4},{6,7},{7,6},{8,9},{9,8},{10,11... | collective-permute-start | bytes 552968 | tf_op jit(solution)/shard_map/ppermute | solution.py:85
  27.3 24.2 %collective-permute-start.4 = (bf16[2,2,24,2432]{3,2,1,0:T(8,128)(2,1)S(1)}, bf16[2,2,24,2432]{3,2,1,0:T(8,128)(2,1)S(1)}, u32[]{:S(2)}, u32[]{:S(2)}) collective-permute-start(bf16[2,2,24,2432]{3,2,1,0:T(8,128)(2,1)S(1)} %pad_maximum_fusion.2.refs_0_), channel_id=1, source_target_pairs={{0,4},{1,3},{2,6},{3,1},{4,0},{5,7},{6,2},{7,5},{8,12},{9,11},{10,... | collective-permute-start | bytes 1400840 | tf_op jit(solution)/shard_map/ppermute | solution.py:85
  28.9 21.1 %collective-permute-start.29 = (bf16[2,96,768]{2,1,0:T(8,128)(2,1)S(1)}, bf16[2,96,768]{2,1,0:T(8,128)(2,1)S(1)}, u32[]{:S(2)}, u32[]{:S(2)}) collective-permute-start(bf16[2,96,768]{2,1,0:T(8,128)(2,1)S(1)} %maximum_select_fusion.1), channel_id=1, source_target_pairs={{0,16},{1,25},{2,18},{3,27},{4,20},{5,29},{6,22},{7,31},{8,24},{9,... | collective-permute-start | bytes 884744 | tf_op jit(solution)/shard_map/ppermute | solution.py:85
  28.9 24.1 %collective-permute-start.28 = (bf16[2,96,768]{2,1,0:T(8,128)(2,1)S(1)}, bf16[2,96,768]{2,1,0:T(8,128)(2,1)S(1)}, u32[]{:S(2)}, u32[]{:S(2)}) collective-permute-start(bf16[2,96,768]{2,1,0:T(8,128)(2,1)S(1)} %maximum_select_fusion.1), channel_id=1, source_target_pairs={{0,0},{1,9},{2,2},{3,11},{4,4},{5,13},{6,6},{7,15},{8,8},{9,17},{1... | collective-permute-start | bytes 884744 | tf_op jit(solution)/shard_map/ppermute | solution.py:85
  29.7 31.2 %collective-permute-start.19 = (bf16[2,24,3840]{2,1,0:T(8,128)(2,1)S(1)}, bf16[2,24,3840]{2,1,0:T(8,128)(2,1)S(1)}, u32[]{:S(2)}, u32[]{:S(2)}) collective-permute-start(bf16[2,24,3840]{2,1,0:T(8,128)(2,1)S(1)} %maximum_select_fusion), channel_id=1, source_target_pairs={{0,16},{1,25},{2,18},{3,27},{4,20},{5,29},{6,22},{7,31},{8,24},{9,... | collective-permute-start | bytes 1105928 | tf_op jit(solution)/shard_map/ppermute | solution.py:85
  32.6 28.2 %collective-permute-start.18 = (bf16[2,24,3840]{2,1,0:T(8,128)(2,1)S(1)}, bf16[2,24,3840]{2,1,0:T(8,128)(2,1)S(1)}, u32[]{:S(2)}, u32[]{:S(2)}) collective-permute-start(bf16[2,24,3840]{2,1,0:T(8,128)(2,1)S(1)} %maximum_select_fusion), channel_id=1, source_target_pairs={{0,0},{1,9},{2,2},{3,11},{4,4},{5,13},{6,6},{7,15},{8,8},{9,17},{1... | collective-permute-start | bytes 1105928 | tf_op jit(solution)/shard_map/ppermute | solution.py:85
  65.0 33.3 %collective-permute-start.30 = (bf16[2,2,96,768]{3,2,1,0:T(8,128)(2,1)}, bf16[2,2,96,768]{3,2,1,0:T(8,128)(2,1)}, u32[]{:S(2)}, u32[]{:S(2)}) collective-permute-start(bf16[2,2,96,768]{3,2,1,0:T(8,128)(2,1)} %pad_maximum_fusion.1.refs_0_), channel_id=1, source_target_pairs={{0,2},{1,5},{2,0},{3,7},{4,6},{5,1},{6,4},{7,3},{8,10},{9,13},{10,... | collective-permute-start | bytes 1769480 | tf_op jit(solution)/shard_map/ppermute | solution.py:85
  66.5 29.5 %collective-permute-start.21 = (bf16[2,2,24,3840]{3,2,1,0:T(8,128)(2,1)}, bf16[2,2,24,3840]{3,2,1,0:T(8,128)(2,1)}, u32[]{:S(2)}, u32[]{:S(2)}) collective-permute-start(bf16[2,2,24,3840]{3,2,1,0:T(8,128)(2,1)} %pad_maximum_fusion.refs_0_), channel_id=1, source_target_pairs={{0,4},{1,3},{2,6},{3,1},{4,0},{5,7},{6,2},{7,5},{8,12},{9,11},{10,... | collective-permute-start | bytes 2211848 | tf_op jit(solution)/shard_map/ppermute | solution.py:85
  68.0 45.8 %collective-permute-start.20 = (bf16[2,2,24,3840]{3,2,1,0:T(8,128)(2,1)}, bf16[2,2,24,3840]{3,2,1,0:T(8,128)(2,1)}, u32[]{:S(2)}, u32[]{:S(2)}) collective-permute-start(bf16[2,2,24,3840]{3,2,1,0:T(8,128)(2,1)} %pad_maximum_fusion.refs_0_), channel_id=1, source_target_pairs={{0,2},{1,5},{2,0},{3,7},{4,6},{5,1},{6,4},{7,3},{8,10},{9,13},{10,... | collective-permute-start | bytes 2211848 | tf_op jit(solution)/shard_map/ppermute | solution.py:85
  77.2 21.1 %collective-permute-start.10 = (bf16[128,576]{1,0:T(8,128)(2,1)S(1)}, bf16[128,576]{1,0:T(8,128)(2,1)}, u32[]{:S(2)}, u32[]{:S(2)}) collective-permute-start(bf16[128,576]{1,0:T(8,128)(2,1)S(1)} %get-tuple-element.58), channel_id=1, source_target_pairs={{0,8},{1,9},{2,10},{3,11},{4,12},{5,13},{6,14},{7,15},{8,16},{9,17... | collective-permute-start | bytes 442376 | tf_op jit(solution)/shard_map/ppermute | solution.py:85
  80.2 34.8 %collective-permute-start.32 = (bf16[2,2,96,768]{3,2,1,0:T(8,128)(2,1)}, bf16[2,2,96,768]{3,2,1,0:T(8,128)(2,1)}, u32[]{:S(2)}, u32[]{:S(2)}) collective-permute-start(bf16[2,2,96,768]{3,2,1,0:T(8,128)(2,1)} %collective-permute-done.31.refs_2_), channel_id=1, source_target_pairs={{0,2},{1,5},{2,0},{3,7},{4,6},{5,1},{6,4},{7,3},{8,10},{9,13},{10,... | collective-permute-start | bytes 1769480 | tf_op jit(solution)/shard_map/ppermute | solution.py:85
  96.0 20.4 %collective-permute-start.22 = (bf16[2,2,24,3840]{3,2,1,0:T(8,128)(2,1)}, bf16[2,2,24,3840]{3,2,1,0:T(8,128)(2,1)}, u32[]{:S(2)}, u32[]{:S(2)}) collective-permute-start(bf16[2,2,24,3840]{3,2,1,0:T(8,128)(2,1)} %collective-permute-done.21.refs_2_), channel_id=1, source_target_pairs={{0,2},{1,5},{2,0},{3,7},{4,6},{5,1},{6,4},{7,3},{8,10},{9,13},{10,... | collective-permute-start | bytes 2211848 | tf_op jit(solution)/shard_map/ppermute | solution.py:85
  115.0 20.6 %collective-permute-start.36 = (bf16[2,2,96,768]{3,2,1,0:T(8,128)(2,1)}, bf16[2,2,96,768]{3,2,1,0:T(8,128)(2,1)S(1)}, u32[]{:S(2)}, u32[]{:S(2)}) collective-permute-start(bf16[2,2,96,768]{3,2,1,0:T(8,128)(2,1)} %collective-permute-done.32.refs_3_), channel_id=1, source_target_pairs={{0,1},{1,0},{2,3},{3,2},{4,5},{5,4},{6,7},{7,6},{8,9},{9,8},{10,11... | collective-permute-start | bytes 1769480 | tf_op jit(solution)/shard_map/ppermute | solution.py:85
  115.7 46.5 %collective-permute-start.23 = (bf16[2,2,24,3840]{3,2,1,0:T(8,128)(2,1)}, bf16[2,2,24,3840]{3,2,1,0:T(8,128)(2,1)}, u32[]{:S(2)}, u32[]{:S(2)}) collective-permute-start(bf16[2,2,24,3840]{3,2,1,0:T(8,128)(2,1)} %pad_maximum_fusion.refs_0_), channel_id=1, source_target_pairs={{0,1},{1,0},{2,3},{3,2},{4,5},{5,4},{6,7},{7,6},{8,9},{9,8},{10,11... | collective-permute-start | bytes 2211848 | tf_op jit(solution)/shard_map/ppermute | solution.py:85
  116.3 46.0 %collective-permute-start.25 = (bf16[2,2,24,3840]{3,2,1,0:T(8,128)(2,1)}, bf16[2,2,24,3840]{3,2,1,0:T(8,128)(2,1)}, u32[]{:S(2)}, u32[]{:S(2)}) collective-permute-start(bf16[2,2,24,3840]{3,2,1,0:T(8,128)(2,1)} %collective-permute-done.21.refs_2_), channel_id=1, source_target_pairs={{0,1},{1,0},{2,3},{3,2},{4,5},{5,4},{6,7},{7,6},{8,9},{9,8},{10,11... | collective-permute-start | bytes 2211848 | tf_op jit(solution)/shard_map/ppermute | solution.py:85
  116.4 45.9 %collective-permute-start.24 = (bf16[2,2,24,3840]{3,2,1,0:T(8,128)(2,1)}, bf16[2,2,24,3840]{3,2,1,0:T(8,128)(2,1)}, u32[]{:S(2)}, u32[]{:S(2)}) collective-permute-start(bf16[2,2,24,3840]{3,2,1,0:T(8,128)(2,1)} %collective-permute-done.20.refs_1_), channel_id=1, source_target_pairs={{0,1},{1,0},{2,3},{3,2},{4,5},{5,4},{6,7},{7,6},{8,9},{9,8},{10,11... | collective-permute-start | bytes 2211848 | tf_op jit(solution)/shard_map/ppermute | solution.py:85
  125.0 37.3 %collective-permute-start.26 = (bf16[2,2,24,3840]{3,2,1,0:T(8,128)(2,1)}, bf16[2,2,24,3840]{3,2,1,0:T(8,128)(2,1)}, u32[]{:S(2)}, u32[]{:S(2)}) collective-permute-start(bf16[2,2,24,3840]{3,2,1,0:T(8,128)(2,1)} %collective-permute-done.22.refs_3_), channel_id=1, source_target_pairs={{0,1},{1,0},{2,3},{3,2},{4,5},{5,4},{6,7},{7,6},{8,9},{9,8},{10,11... | collective-permute-start | bytes 2211848 | tf_op jit(solution)/shard_map/ppermute | solution.py:85
  227.8 30.4 %collective-permute-start.60 = (bf16[2,4,96,768]{3,2,1,0:T(8,128)(2,1)S(1)}, bf16[2,4,96,768]{3,2,1,0:T(8,128)(2,1)S(1)}, u32[]{:S(2)}, u32[]{:S(2)}) collective-permute-start(bf16[2,4,96,768]{3,2,1,0:T(8,128)(2,1)S(1)} %shard_map.293), channel_id=1, source_target_pairs={{0,4},{1,3},{2,6},{3,1},{4,0},{5,7},{6,2},{7,5},{8,12},{9,11},{10,... | collective-permute-start | bytes 3538952 | tf_op jit(solution)/shard_map/ppermute | solution.py:85
  229.5 48.0 %collective-permute-start.51 = (bf16[2,4,24,3840]{3,2,1,0:T(8,128)(2,1)S(1)}, bf16[2,4,24,3840]{3,2,1,0:T(8,128)(2,1)S(1)}, u32[]{:S(2)}, u32[]{:S(2)}) collective-permute-start(bf16[2,4,24,3840]{3,2,1,0:T(8,128)(2,1)S(1)} %get-tuple-element.88), channel_id=1, source_target_pairs={{0,1},{1,0},{2,3},{3,2},{4,5},{5,4},{6,7},{7,6},{8,9},{9,8},{10,11... | collective-permute-start | bytes 4423688 | tf_op jit(solution)/shard_map/ppermute | solution.py:85
  230.8 49.6 %collective-permute-start.53 = (bf16[2,4,24,3840]{3,2,1,0:T(8,128)(2,1)S(1)}, bf16[2,4,24,3840]{3,2,1,0:T(8,128)(2,1)S(1)}, u32[]{:S(2)}, u32[]{:S(2)}) collective-permute-start(bf16[2,4,24,3840]{3,2,1,0:T(8,128)(2,1)S(1)} %shard_map.288), channel_id=1, source_target_pairs={{0,4},{1,3},{2,6},{3,1},{4,0},{5,7},{6,2},{7,5},{8,12},{9,11},{10,... | collective-permute-start | bytes 4423688 | tf_op jit(solution)/shard_map/ppermute | solution.py:85
  258.8 22.0 %collective-permute-start.49 = (bf16[2,24,2432]{2,1,0:T(8,128)(2,1)S(1)}, bf16[2,24,2432]{2,1,0:T(8,128)(2,1)S(1)}, u32[]{:S(2)}, u32[]{:S(2)}) collective-permute-start(bf16[2,24,2432]{2,1,0:T(8,128)(2,1)S(1)} %bitcast.157), channel_id=1, source_target_pairs={{0,16},{1,25},{2,18},{3,27},{4,20},{5,29},{6,22},{7,31},{8,24},{9,... | collective-permute-start | bytes 700424 | tf_op jit(solution)/shard_map/ppermute | solution.py:85
  261.3 19.5 %collective-permute-start.48 = (bf16[2,24,2432]{2,1,0:T(8,128)(2,1)S(1)}, bf16[2,24,2432]{2,1,0:T(8,128)(2,1)S(1)}, u32[]{:S(2)}, u32[]{:S(2)}) collective-permute-start(bf16[2,24,2432]{2,1,0:T(8,128)(2,1)S(1)} %bitcast.158), channel_id=1, source_target_pairs={{0,0},{1,9},{2,2},{3,11},{4,4},{5,13},{6,6},{7,15},{8,8},{9,17},{1... | collective-permute-start | bytes 700424 | tf_op jit(solution)/shard_map/ppermute | solution.py:85
  291.1 20.7 %collective-permute-start.64 = (bf16[96,768]{1,0:T(8,128)(2,1)S(1)}, bf16[96,768]{1,0:T(8,128)(2,1)S(1)}, u32[]{:S(2)}, u32[]{:S(2)}) collective-permute-start(bf16[96,768]{1,0:T(8,128)(2,1)S(1)} %fusion.41), channel_id=1, source_target_pairs={{0,1},{1,0},{2,3},{3,2},{4,5},{5,4},{6,7},{7,6},{8,9},{9,8},{10,11... | collective-permute-start | bytes 442376 | tf_op jit(solution)/shard_map/ppermute | solution.py:85
  (117 other events, 824.5 us)
where the time goes:
time: 316 us; the launch traced here: 315 us
  waiting for transfers between devices  147 us (47%)
  starting transfers between devices  58.9 us (19%)
  local copies, waits for them, and re-layouts  40.2 us (13%)
  Pallas kernels  37 us (12%)
  other arithmetic  16.4 us (5%)
  matrix products  12.8 us (4%)
    ppermute x65, waiting for transfers between devices, send(): return lax.ppermute(value, AXES, pairs)  147 us
    ppermute x65, starting transfers between devices, send(): return lax.ppermute(value, AXES, pairs)  58.9 us
    unnamed x153, local copies, waits for them, and re-layouts  21.4 us
    pallas_call x8, Pallas kernels, simple(): pl.pallas_call(kernel, in_specs=[vmem] * len(ins), out_specs=[vmem] * len...  18.1 us
    pallas_call x3, Pallas kernels, scatter(): pl.pallas_call(kernel, in_specs=[vmem] * inputs, out_specs=[vmem] * (2 *...  9.64 us
    pallas_call x3, Pallas kernels, gather(): pl.pallas_call(kernel, in_specs=[pl.BlockSpec(memory_space=pl.ANY)] * len...  6.72 us
  transfers between devices with their start and end apart: 65, of which 24 were waited for; matrix products, arithmetic and copies ran while one was open for 13% of the time, Pallas kernels for 8%

commit v1 on v0

--- a/solution.py
+++ b/solution.py
@@ -106,12 +106,16 @@
         return self.send(value, lambda z, x, y, k: (z + 2, x, y, k) if k == 0 else (z + 3, x, y, k))
 
 
-def gather(grid, shard, widths):
-    rows, _ = shard.shape
+def gather_z(grid, shard):
     core = grid.here()[3]
     other = grid.core(shard)
     pair = jnp.where(core == 0, jnp.stack([shard, other]), jnp.stack([other, shard]))
-    base = jnp.stack([grid.z_far(pair), grid.z_near(pair)])
+    return grid.z_far(pair), grid.z_near(pair)
+
+
+def gather(grid, lines, widths):
+    base = jnp.stack(lines)
+    rows = base.shape[2]
     reached = {}
     for i in range(grid.x):
         reached[i, 0] = base if i == 0 else grid.first(base, i)
@@ -152,9 +156,9 @@
         kernel,
         in_specs=[pl.BlockSpec(memory_space=pl.ANY)] * len(parts),
         out_specs=[pl.BlockSpec(memory_space=pltpu.VMEM)] * len(widths),
-        out_shape=[jax.ShapeDtypeStruct((grid.n // 2, 2, rows, width), shard.dtype) for width in widths],
+        out_shape=[jax.ShapeDtypeStruct((grid.n // 2, 2, rows, width), base.dtype) for width in widths],
         scratch_shapes=[pltpu.SemaphoreType.DMA((len(parts) * 2 * len(widths),))],
-        compiler_params=pltpu.CompilerParams(vmem_limit_bytes=16 * 1024 * 1024),
+        compiler_params=pltpu.CompilerParams(vmem_limit_bytes=12 * 1024 * 1024),
     )(*parts)
     return [item.reshape(grid.n * rows, width) for item, width in zip(whole, widths)]
 
@@ -280,14 +284,15 @@
     return lax.dot_general(left, right, (dims, ((), ())), preferred_element_type=F32)
 
 
-def simple(kernel, ins, outs):
+def simple(kernel, ins, outs, scratch=()):
     vmem = pl.BlockSpec(memory_space=pltpu.VMEM)
     return pl.pallas_call(
         kernel,
         in_specs=[vmem] * len(ins),
         out_specs=[vmem] * len(outs),
         out_shape=[jax.ShapeDtypeStruct(shape, kind) for shape, kind in outs],
-        compiler_params=pltpu.CompilerParams(vmem_limit_bytes=24 * 1024 * 1024),
+        scratch_shapes=scratch,
+        compiler_params=pltpu.CompilerParams(vmem_limit_bytes=12 * 1024 * 1024),
     )(*ins)
 
 
@@ -433,6 +438,37 @@
     return simple(kernel, [grad_q, own, *came], [((step, 3 * group), BF)] * Z)
 
 
+def unpack_lines(extra, used, rows):
+    spare = used - 8
+    n = extra.shape[0] // rows
+
+    def kernel(extra_ref, lines_ref, up_ref, joint_ref, turned):
+        turned[...] = extra_ref[...].astype(F32).T
+        lines_ref[...] = turned[:8]
+        joint_ref[:, :D] = turned[2:3]
+        joint_ref[:, D : 2 * D] = jnp.zeros((1, D), F32)
+        joint_ref[:, 2 * D :] = turned[3:4]
+        for at in range(n):
+            for part in range(spare):
+                low = (at * spare + part) * rows
+                up_ref[:, low : low + rows] = turned[8 + part : 9 + part, at * rows : (at + 1) * rows]
+
+    outs = [((8, D), F32), ((1, spare * D), F32), ((1, 3 * D), F32)]
+    return simple(kernel, [extra], outs, [pltpu.VMEM((EXT, D), F32)])
+
+
+def fold_lines(vector, spare, rows):
+    n = D // rows
+
+    def kernel(vector_ref, out_ref):
+        for at in range(n):
+            for part in range(spare):
+                low = (at * spare + part) * rows
+                out_ref[part : part + 1, at * rows : (at + 1) * rows] = vector_ref[:, low : low + rows]
+
+    return simple(kernel, [vector], [((spare, D), F32)])[0]
+
+
 def pack_first(w_qkv, lines, spare, rows):
     width = w_qkv.shape[1]
     used = len(lines) + spare.shape[1] // rows
@@ -479,12 +515,13 @@
     rows = w_qkv.shape[1]
     small = [attn_gain, attn_shift, query_bias, value_bias, out_bias, mlp_gain, mlp_shift, proj_bias]
     used = 8 + fc_bias.shape[1] // rows
-    w_joint, extra = gather(grid, pack_first(w_qkv[0], small, fc_bias, rows), [3 * D, EXT])
-    w_mix, w_up = gather(grid, jnp.concatenate([w_out[0], w_fc[0]], axis=1), [D, w_fc.shape[2]])
-    (w_down,) = gather(grid, w_proj[0], [D])
-    extra = extra[:, :used].T
-    gain_one, shift_one, bias_query, bias_value, bias_mix, gain_two, shift_two, bias_down = [extra[i] for i in range(8)]
-    bias_up = jnp.transpose(extra[8:].reshape(used - 8, grid.n, rows), (1, 0, 2)).reshape(-1)
+    first_z = gather_z(grid, pack_first(w_qkv[0], small, fc_bias, rows))
+    mid_z = gather_z(grid, jnp.concatenate([w_out[0], w_fc[0]], axis=1))
+    last_z = gather_z(grid, w_proj[0])
+    w_joint, extra = gather(grid, first_z, [3 * D, EXT])
+    w_mix, w_up = gather(grid, mid_z, [D, w_fc.shape[2]])
+    lines, bias_up, joint_bias = unpack_lines(extra, used, rows)
+    gain_one, shift_one, _, _, bias_mix, gain_two, shift_two, bias_down = [lines[i : i + 1] for i in range(8)]
 
     def positions(dz, dx):
         owner = (z - dz + Z) % Z * X + (x - dx + X) % X
@@ -503,11 +540,12 @@
     normed_in, normed_one, inverse_one = norm_forward(state, gain_one, shift_one)
     first = normed_in.astype(BF)
     joint = jnp.dot(first, w_joint, preferred_element_type=F32)
-    joint_bias = jnp.concatenate([bias_query, jnp.zeros_like(bias_query), bias_value]).astype(F32)[None]
     packed = spread(split_groups(grid, joint, joint_bias, 3))
     own_keys = jnp.concatenate([piece[:, group:] for piece in packed])
     all_keys = [own_keys] + [grid.along_x(own_keys, dx) for dx in range(1, X)]
     mixed_local, log_total, mixed_send = attend(packed, all_keys, query_pos, key_pos, heads)
+    log_total, *last_z = lax.optimization_barrier((log_total, *last_z))
+    (w_down,) = gather(grid, last_z, [D])
     mixed_round, _ = join_groups(grid, collect(mixed_send), 1)
 
     middle = state + jnp.dot(mixed_round, w_mix, preferred_element_type=F32) + bias_mix.astype(F32)
@@ -559,7 +597,7 @@
         grad_proj_bias,
     ]
     vectors = [item.reshape(1, D) for item in vectors]
-    vectors.append(jnp.transpose(grad_fc_bias.reshape(grid.n, used - 8, rows), (1, 0, 2)).reshape(used - 8, D))
+    vectors.append(fold_lines(grad_fc_bias.reshape(1, -1), used - 8, rows))
     shard_first = scatter(grid, [(first, grad_joint)], vectors)
     shard_qkv, ends = shard_first[:, : 3 * D], shard_first[:, 3 * D :]
     small = [ends[:, i][None] for i in range(8)]

time: 316 us -> 281 us (0.89)
  local copies, waits for them, and re-layouts: 40.2 us -> 19.7 us
  starting transfers between devices: 58.9 us -> 50.6 us
  waiting for transfers between devices: 147 us -> 155 us
  other arithmetic: 16.4 us -> 10.6 us
  Pallas kernels: 37 us -> 32.3 us
  matrix products: 12.8 us -> 9.53 us
    ppermute x65, starting transfers between devices: 58.9 us -> 50.6 us  [send(): return lax.ppermute(value, AXES, pairs)]
    ppermute x65, waiting for transfers between devices: 147 us -> 155 us  [send(): return lax.ppermute(value, AXES, pairs)]
    unnamed x153 -> x90, local copies, waits for them, and re-layouts: 21.4 us -> 13.5 us
    convert_element_type x3 -> x0, local copies, waits for them, and re-layouts: 4.46 us -> none  [local_step(): bias_up.astype(F32)]
    slice x4, local copies, waits for them, and re-layouts: 4.06 us -> 0.38 us  [local_step(): own_keys = jnp.concatenate([piece[:, group:] for piece in packed])]
    pallas_call x8 -> x10, Pallas kernels: 18.1 us -> 15.1 us  [simple(): pl.pallas_call(kernel, in_specs=[vmem] * len(ins), out_specs=[vmem] * len...]
  transfers between devices with their start and end apart: 65 -> 65, of which waited for: 24 -> 26; matrix products, arithmetic and copies ran while one was open for 13% -> 9% of each run, Pallas kernels for 8% -> 11%
where the time goes in v1:
time: 281 us; the launch traced here: 280 us
  waiting for transfers between devices  155 us (55%)
  starting transfers between devices  50.6 us (18%)
  Pallas kernels  32.3 us (11%)
  local copies, waits for them, and re-layouts  19.7 us (7%)
  other arithmetic  10.6 us (4%)
  matrix products  9.53 us (3%)
    ppermute x65, waiting for transfers between devices, send(): return lax.ppermute(value, AXES, pairs)  155 us
    ppermute x65, starting transfers between devices, send(): return lax.ppermute(value, AXES, pairs)  50.6 us
    pallas_call x10, Pallas kernels, simple(): pl.pallas_call(kernel, in_specs=[vmem] * len(ins), out_specs=[vmem] * len...  15.1 us
    unnamed x90, local copies, waits for them, and re-layouts  13.5 us
    pallas_call x3, Pallas kernels, scatter(): pl.pallas_call(kernel, in_specs=[vmem] * inputs, out_specs=[vmem] * (2 *...  9.68 us
  transfers between devices with their start and end apart: 65, of which 26 were waited for; matrix products, arithmetic and copies ran while one was open for 9% of the time, Pallas kernels for 11%

profile of v1, /device:TPU:0, one launch (start us, length us, event | category | flops | bytes accessed | tf_op | source)
XLA Modules:
  0.0 280.1 jit_solution(12050645649261575747)
XLA Ops:
  10.5 4.0 %collective-permute-start.2 = (bf16[2,24,2432]{2,1,0:T(8,128)(2,1)S(1)}, bf16[2,24,2432]{2,1,0:T(8,128)(2,1)S(1)}, u32[]{:S(2)}, u32[]{:S(2)}) collective-permute-start(bf16[2,24,2432]{2,1,0:T(8,128)(2,1)S(1)} %maximum_select_fusion.2), channel_id=1, source_target_pairs={{0,16},{1,25},{2,18},{3,27},{4,20},{5,29},{6,22},{7,31},{8,24},{9,... | collective-permute-start | bytes 700424 | tf_op jit(solution)/shard_map/ppermute | solution.py:85
  15.8 9.8 %collective-permute-done.2 = bf16[2,24,2432]{2,1,0:T(8,128)(2,1)S(1)} collective-permute-done((bf16[2,24,2432]{2,1,0:T(8,128)(2,1)S(1)}, bf16[2,24,2432]{2,1,0:T(8,128)(2,1)S(1)}, u32[]{:S(2)}, u32[]{:S(2)}) %collective-permute-start.2) | collective-permute-done | bytes 233504 | tf_op jit(solution)/shard_map/ppermute | solution.py:85
  29.1 10.2 %collective-permute-done.4.refs_2_ = bf16[2,2,24,2432]{3,2,1,0:T(8,128)(2,1)S(1)} collective-permute-done((bf16[2,2,24,2432]{3,2,1,0:T(8,128)(2,1)S(1)}, bf16[2,2,24,2432]{3,2,1,0:T(8,128)(2,1)S(1)}, u32[]{:S(2)}, u32[]{:S(2)}) %collective-permute-start.4) | collective-permute-done | bytes 466976 | tf_op jit(solution)/shard_map/ppermute | solution.py:85
  41.5 17.6 %collective-permute-done.19 = bf16[2,24,3840]{2,1,0:T(8,128)(2,1)S(1)} collective-permute-done((bf16[2,24,3840]{2,1,0:T(8,128)(2,1)S(1)}, bf16[2,24,3840]{2,1,0:T(8,128)(2,1)S(1)}, u32[]{:S(2)}, u32[]{:S(2)}) %collective-permute-start.19) | collective-permute-done | bytes 368672 | tf_op jit(solution)/shard_map/ppermute | solution.py:85
  67.2 8.6 %collective-permute-done.21.refs_2_ = bf16[2,2,24,3840]{3,2,1,0:T(8,128)(2,1)} collective-permute-done((bf16[2,2,24,3840]{3,2,1,0:T(8,128)(2,1)}, bf16[2,2,24,3840]{3,2,1,0:T(8,128)(2,1)}, u32[]{:S(2)}, u32[]{:S(2)}) %collective-permute-start.21) | collective-permute-done | bytes 737312 | tf_op jit(solution)/shard_map/ppermute | solution.py:85
  78.1 6.6 %collective-permute-done.11.refs_2_ = bf16[128,576]{1,0:T(8,128)(2,1)S(1)} collective-permute-done((bf16[128,576]{1,0:T(8,128)(2,1)S(1)}, bf16[128,576]{1,0:T(8,128)(2,1)S(1)}, u32[]{:S(2)}, u32[]{:S(2)}) %collective-permute-start.11) | collective-permute-done | bytes 147488 | tf_op jit(solution)/shard_map/ppermute | solution.py:85
  90.3 3.7 %collective-permute-start.28 = (bf16[2,96,768]{2,1,0:T(8,128)(2,1)}, bf16[2,96,768]{2,1,0:T(8,128)(2,1)}, u32[]{:S(2)}, u32[]{:S(2)}) collective-permute-start(bf16[2,96,768]{2,1,0:T(8,128)(2,1)} %maximum_select_fusion.1), channel_id=1, source_target_pairs={{0,0},{1,9},{2,2},{3,11},{4,4},{5,13},{6,6},{7,15},{8,8},{9,17},{1... | collective-permute-start | bytes 884744 | tf_op jit(solution)/shard_map/ppermute | solution.py:85
  101.7 5.8 %shard_map.275 = (f32[512,192]{1,0:T(8,128)S(1)}, f32[512,3]{1,0:T(8,128)S(1)}, bf16[128,192]{1,0:T(8,128)(2,1)S(1)}, bf16[128,192]{1,0:T(8,128)(2,1)S(1)}, bf16...) custom-call(bf16[128,576]{1,0:T(8,128)(2,1)S(1)} %copy-done.3, bf16[128,576]{1,0:T(8,128)(2,1)S(1)} %copy-done.6, ...), custom_call_target="tpu_custom_call" | custom-call | tf_op jit(solution)/shard_map/pallas_call | solution.py:289
  107.5 3.2 %collective-permute-start.14 = (bf16[128,192]{1,0:T(8,128)(2,1)S(1)}, bf16[128,192]{1,0:T(8,128)(2,1)S(1)}, u32[]{:S(2)}, u32[]{:S(2)}) collective-permute-start(bf16[128,192]{1,0:T(8,128)(2,1)S(1)} %get-tuple-element.70), channel_id=1, source_target_pairs={{0,24},{1,25},{2,26},{3,27},{4,28},{5,29},{6,30},{7,31},{8,0},{9,1... | collective-permute-start | bytes 147464 | tf_op jit(solution)/shard_map/ppermute | solution.py:85
  117.3 5.0 %collective-permute-done.16.refs_3_ = bf16[128,192]{1,0:T(8,128)(2,1)S(1)} collective-permute-done((bf16[128,192]{1,0:T(8,128)(2,1)S(1)}, bf16[128,192]{1,0:T(8,128)(2,1)S(1)}, u32[]{:S(2)}, u32[]{:S(2)}) %collective-permute-start.16) | collective-permute-done | bytes 49184 | tf_op jit(solution)/shard_map/ppermute | solution.py:85
  126.9 10.4 %collective-permute-done.31.refs_2_ = bf16[2,2,96,768]{3,2,1,0:T(8,128)(2,1)S(1)} collective-permute-done((bf16[2,2,96,768]{3,2,1,0:T(8,128)(2,1)S(1)}, bf16[2,2,96,768]{3,2,1,0:T(8,128)(2,1)S(1)}, u32[]{:S(2)}, u32[]{:S(2)}) %collective-permute-start.31) | collective-permute-done | bytes 589856 | tf_op jit(solution)/shard_map/ppermute | solution.py:85
  139.2 8.0 %collective-permute-done.32.refs_3_ = bf16[2,2,96,768]{3,2,1,0:T(8,128)(2,1)S(1)} collective-permute-done((bf16[2,2,96,768]{3,2,1,0:T(8,128)(2,1)S(1)}, bf16[2,2,96,768]{3,2,1,0:T(8,128)(2,1)S(1)}, u32[]{:S(2)}, u32[]{:S(2)}) %collective-permute-start.32) | collective-permute-done | bytes 589856 | tf_op jit(solution)/shard_map/ppermute | solution.py:85
  148.7 3.2 %shard_map.294 = (bf16[2,4,96,768]{3,2,1,0:T(8,128)(2,1)S(1)}, bf16[2,4,96,768]{3,2,1,0:T(8,128)(2,1)S(1)}, bf16[2,4,96,768]{3,2,1,0:T(8,128)(2,1)S(1)}, bf16[2,4,96,768]{3,2,1,0:T(8,128)(2,1)S(1)}) custom-call(bf16[128,3072]{1,0:T(8,128)(2,1)S(1)} %get-tuple-element.158.refs_0_, bf16[128,768]{1,0:T(8,128)(2,1)S(1)} %get-tuple-element.149.refs_1_), custom_call_target="tpu_custom_call" | custom-call | tf_op jit(solution)/shard_map/pallas_call | solution.py:250
  158.8 3.6 %collective-permute-start.39 = (bf16[128,192]{1,0:T(8,128)(2,1)S(1)}, bf16[128,192]{1,0:T(8,128)(2,1)S(1)}, u32[]{:S(2)}, u32[]{:S(2)}) collective-permute-start(bf16[128,192]{1,0:T(8,128)(2,1)S(1)} %get-tuple-element.85), channel_id=1, source_target_pairs={{0,24},{1,25},{2,26},{3,27},{4,28},{5,29},{6,30},{7,31},{8,0},{9,1... | collective-permute-start | bytes 147464 | tf_op jit(solution)/shard_map/ppermute | solution.py:85
  162.4 3.0 %collective-permute-done.37.refs_11_ = bf16[128,192]{1,0:T(8,128)(2,1)S(1)} collective-permute-done((bf16[128,192]{1,0:T(8,128)(2,1)S(1)}, bf16[128,192]{1,0:T(8,128)(2,1)S(1)}, u32[]{:S(2)}, u32[]{:S(2)}) %collective-permute-start.37) | collective-permute-done | bytes 49184 | tf_op jit(solution)/shard_map/ppermute | solution.py:85
  167.2 7.1 %shard_map.280 = (bf16[512,192]{1,0:T(8,128)(2,1)S(1)}, f32[512,384]{1,0:T(8,128)S(1)}, bf16[512,384]{1,0:T(8,128)(2,1)S(1)}) custom-call(bf16[128,576]{1,0:T(8,128)(2,1)S(1)} %copy-done.4, bf16[128,576]{1,0:T(8,128)(2,1)S(1)} %copy-done.7, bf16[128,576]{1,0:T(8,128)(2,1)S(1)} %copy-done.10, bf16[128,576]{1,0:T(8,128)(2,1)S(1)} %copy-done.13, ...), custom_call_target="tpu_custom_call" | custom-call | tf_op jit(solution)/shard_map/pallas_call | solution.py:289
  174.4 9.5 %collective-permute-done.40.refs_2_ = bf16[512,384]{1,0:T(8,128)(2,1)S(1)} collective-permute-done((bf16[512,384]{1,0:T(8,128)(2,1)S(1)}, bf16[512,384]{1,0:T(8,128)(2,1)S(1)}, u32[]{:S(2)}, u32[]{:S(2)}) %collective-permute-start.40) | collective-permute-done | bytes 393248 | tf_op jit(solution)/shard_map/ppermute | solution.py:85
  188.7 3.6 %shard_map.289 = (bf16[2,4,24,3840]{3,2,1,0:T(8,128)(2,1)S(1)}, bf16[2,4,24,3840]{3,2,1,0:T(8,128)(2,1)S(1)}, bf16[2,4,24,3840]{3,2,1,0:T(8,128)(2,1)S(1)}, bf16[2,4,24,3840]{3,2,1,0:T(8,128)(2,1)S(1)}) custom-call(bf16[128,768]{1,0:T(8,128)(2,1)S(1)} %get-tuple-element.73.refs_0_, bf16[128,768]{1,0:T(8,128)(2,1)S(1)} %add_convert_fusion.refs_1_, ...), custom_call_target="tpu_custom_call" | custom-call | tf_op jit(solution)/shard_map/pallas_call | solution.py:250
  193.3 8.0 %collective-permute-done.42.refs_2_ = bf16[128,576]{1,0:T(8,128)(2,1)S(1)} collective-permute-done((bf16[128,576]{1,0:T(8,128)(2,1)S(1)}, bf16[128,576]{1,0:T(8,128)(2,1)S(1)}, u32[]{:S(2)}, u32[]{:S(2)}) %collective-permute-start.42) | collective-permute-done | bytes 147488 | tf_op jit(solution)/shard_map/ppermute | solution.py:85
  213.6 12.1 %collective-permute-done.61.refs_3_ = bf16[1,4,96,768]{3,2,1,0:T(8,128)(2,1)S(1)} collective-permute-done((bf16[1,4,96,768]{3,2,1,0:T(8,128)(2,1)S(1)}, bf16[1,4,96,768]{3,2,1,0:T(8,128)(2,1)S(1)}, u32[]{:S(2)}, u32[]{:S(2)}) %collective-permute-start.61) | collective-permute-done | bytes 589856 | tf_op jit(solution)/shard_map/ppermute | solution.py:85
  230.4 9.3 %collective-permute-done.63 = bf16[2,96,768]{2,1,0:T(8,128)(2,1)S(1)} collective-permute-done((bf16[2,96,768]{2,1,0:T(8,128)(2,1)S(1)}, bf16[2,96,768]{2,1,0:T(8,128)(2,1)S(1)}, u32[]{:S(2)}, u32[]{:S(2)}) %collective-permute-start.63) | collective-permute-done | bytes 294944 | tf_op jit(solution)/shard_map/ppermute | solution.py:85
  250.4 4.5 %collective-permute-done.49 = bf16[2,24,2432]{2,1,0:T(8,128)(2,1)S(1)} collective-permute-done((bf16[2,24,2432]{2,1,0:T(8,128)(2,1)S(1)}, bf16[2,24,2432]{2,1,0:T(8,128)(2,1)S(1)}, u32[]{:S(2)}, u32[]{:S(2)}) %collective-permute-start.49) | collective-permute-done | bytes 233504 | tf_op jit(solution)/shard_map/ppermute | solution.py:85
  256.4 4.8 %collective-permute-done.54.refs_3_ = bf16[1,4,24,3840]{3,2,1,0:T(8,128)(2,1)S(1)} collective-permute-done((bf16[1,4,24,3840]{3,2,1,0:T(8,128)(2,1)S(1)}, bf16[1,4,24,3840]{3,2,1,0:T(8,128)(2,1)S(1)}, u32[]{:S(2)}, u32[]{:S(2)}) %collective-permute-start.54) | collective-permute-done | bytes 737312 | tf_op jit(solution)/shard_map/ppermute | solution.py:85
  263.4 13.5 %collective-permute-done.56 = bf16[2,24,3840]{2,1,0:T(8,128)(2,1)S(1)} collective-permute-done((bf16[2,24,3840]{2,1,0:T(8,128)(2,1)S(1)}, bf16[2,24,3840]{2,1,0:T(8,128)(2,1)S(1)}, u32[]{:S(2)}, u32[]{:S(2)}) %collective-permute-start.56) | collective-permute-done | bytes 368672 | tf_op jit(solution)/shard_map/ppermute | solution.py:85
  (300 shorter events, 103.2 us)
Async XLA Ops:
  9.1 31.3 %collective-permute-start.17 = (bf16[24,3840]{1,0:T(8,128)(2,1)S(1)}, bf16[24,3840]{1,0:T(8,128)(2,1)S(1)}, u32[]{:S(2)}, u32[]{:S(2)}) collective-permute-start(bf16[24,3840]{1,0:T(8,128)(2,1)S(1)} %get-tuple-element.153), channel_id=1, source_target_pairs={{0,1},{1,0},{2,3},{3,2},{4,5},{5,4},{6,7},{7,6},{8,9},{9,8},{10,11... | collective-permute-start | bytes 552968 | tf_op jit(solution)/shard_map/ppermute | solution.py:85
  10.5 15.2 %collective-permute-start.2 = (bf16[2,24,2432]{2,1,0:T(8,128)(2,1)S(1)}, bf16[2,24,2432]{2,1,0:T(8,128)(2,1)S(1)}, u32[]{:S(2)}, u32[]{:S(2)}) collective-permute-start(bf16[2,24,2432]{2,1,0:T(8,128)(2,1)S(1)} %maximum_select_fusion.2), channel_id=1, source_target_pairs={{0,16},{1,25},{2,18},{3,27},{4,20},{5,29},{6,22},{7,31},{8,24},{9,... | collective-permute-start | bytes 700424 | tf_op jit(solution)/shard_map/ppermute | solution.py:85
  27.5 31.6 %collective-permute-start.3 = (bf16[2,2,24,2432]{3,2,1,0:T(8,128)(2,1)S(1)}, bf16[2,2,24,2432]{3,2,1,0:T(8,128)(2,1)S(1)}, u32[]{:S(2)}, u32[]{:S(2)}) collective-permute-start(bf16[2,2,24,2432]{3,2,1,0:T(8,128)(2,1)S(1)} %pad_maximum_fusion.2.refs_0_), channel_id=1, source_target_pairs={{0,2},{1,5},{2,0},{3,7},{4,6},{5,1},{6,4},{7,3},{8,10},{9,13},{10,... | collective-permute-start | bytes 1400840 | tf_op jit(solution)/shard_map/ppermute | solution.py:85
  39.4 20.2 %collective-permute-start.5 = (bf16[2,2,24,2432]{3,2,1,0:T(8,128)(2,1)S(1)}, bf16[2,2,24,2432]{3,2,1,0:T(8,128)(2,1)S(1)}, u32[]{:S(2)}, u32[]{:S(2)}) collective-permute-start(bf16[2,2,24,2432]{3,2,1,0:T(8,128)(2,1)S(1)} %collective-permute-done.4.refs_2_), channel_id=1, source_target_pairs={{0,2},{1,5},{2,0},{3,7},{4,6},{5,1},{6,4},{7,3},{8,10},{9,13},{10,... | collective-permute-start | bytes 1400840 | tf_op jit(solution)/shard_map/ppermute | solution.py:85
  40.4 18.7 %collective-permute-start.19 = (bf16[2,24,3840]{2,1,0:T(8,128)(2,1)S(1)}, bf16[2,24,3840]{2,1,0:T(8,128)(2,1)S(1)}, u32[]{:S(2)}, u32[]{:S(2)}) collective-permute-start(bf16[2,24,3840]{2,1,0:T(8,128)(2,1)S(1)} %maximum_select_fusion), channel_id=1, source_target_pairs={{0,16},{1,25},{2,18},{3,27},{4,20},{5,29},{6,22},{7,31},{8,24},{9,... | collective-permute-start | bytes 1105928 | tf_op jit(solution)/shard_map/ppermute | solution.py:85
  40.5 19.2 %collective-permute-start.18 = (bf16[2,24,3840]{2,1,0:T(8,128)(2,1)S(1)}, bf16[2,24,3840]{2,1,0:T(8,128)(2,1)S(1)}, u32[]{:S(2)}, u32[]{:S(2)}) collective-permute-start(bf16[2,24,3840]{2,1,0:T(8,128)(2,1)S(1)} %maximum_select_fusion), channel_id=1, source_target_pairs={{0,0},{1,9},{2,2},{3,11},{4,4},{5,13},{6,6},{7,15},{8,8},{9,17},{1... | collective-permute-start | bytes 1105928 | tf_op jit(solution)/shard_map/ppermute | solution.py:85
  41.2 20.8 %collective-permute-start.6 = (bf16[2,2,24,2432]{3,2,1,0:T(8,128)(2,1)S(1)}, bf16[2,2,24,2432]{3,2,1,0:T(8,128)(2,1)S(1)}, u32[]{:S(2)}, u32[]{:S(2)}) collective-permute-start(bf16[2,2,24,2432]{3,2,1,0:T(8,128)(2,1)S(1)} %pad_maximum_fusion.2.refs_0_), channel_id=1, source_target_pairs={{0,1},{1,0},{2,3},{3,2},{4,5},{5,4},{6,7},{7,6},{8,9},{9,8},{10,11... | collective-permute-start | bytes 1400840 | tf_op jit(solution)/shard_map/ppermute | solution.py:85
  60.6 15.1 %collective-permute-start.21 = (bf16[2,2,24,3840]{3,2,1,0:T(8,128)(2,1)}, bf16[2,2,24,3840]{3,2,1,0:T(8,128)(2,1)}, u32[]{:S(2)}, u32[]{:S(2)}) collective-permute-start(bf16[2,2,24,3840]{3,2,1,0:T(8,128)(2,1)} %pad_maximum_fusion.refs_0_), channel_id=1, source_target_pairs={{0,4},{1,3},{2,6},{3,1},{4,0},{5,7},{6,2},{7,5},{8,12},{9,11},{10,... | collective-permute-start | bytes 2211848 | tf_op jit(solution)/shard_map/ppermute | solution.py:85
  62.1 26.9 %collective-permute-start.27 = (bf16[96,768]{1,0:T(8,128)(2,1)S(1)}, bf16[96,768]{1,0:T(8,128)(2,1)S(1)}, u32[]{:S(2)}, u32[]{:S(2)}) collective-permute-start(bf16[96,768]{1,0:T(8,128)(2,1)S(1)} %bitcast.167), channel_id=1, source_target_pairs={{0,1},{1,0},{2,3},{3,2},{4,5},{5,4},{6,7},{7,6},{8,9},{9,8},{10,11... | collective-permute-start | bytes 442376 | tf_op jit(solution)/shard_map/ppermute | solution.py:85
  65.6 46.7 %collective-permute-start.20 = (bf16[2,2,24,3840]{3,2,1,0:T(8,128)(2,1)}, bf16[2,2,24,3840]{3,2,1,0:T(8,128)(2,1)}, u32[]{:S(2)}, u32[]{:S(2)}) collective-permute-start(bf16[2,2,24,3840]{3,2,1,0:T(8,128)(2,1)} %pad_maximum_fusion.refs_0_), channel_id=1, source_target_pairs={{0,2},{1,5},{2,0},{3,7},{4,6},{5,1},{6,4},{7,3},{8,10},{9,13},{10,... | collective-permute-start | bytes 2211848 | tf_op jit(solution)/shard_map/ppermute | solution.py:85
  75.8 37.0 %collective-permute-start.22 = (bf16[2,2,24,3840]{3,2,1,0:T(8,128)(2,1)}, bf16[2,2,24,3840]{3,2,1,0:T(8,128)(2,1)}, u32[]{:S(2)}, u32[]{:S(2)}) collective-permute-start(bf16[2,2,24,3840]{3,2,1,0:T(8,128)(2,1)} %collective-permute-done.21.refs_2_), channel_id=1, source_target_pairs={{0,2},{1,5},{2,0},{3,7},{4,6},{5,1},{6,4},{7,3},{8,10},{9,13},{10,... | collective-permute-start | bytes 2211848 | tf_op jit(solution)/shard_map/ppermute | solution.py:85
  89.8 20.9 %collective-permute-start.29 = (bf16[2,96,768]{2,1,0:T(8,128)(2,1)}, bf16[2,96,768]{2,1,0:T(8,128)(2,1)}, u32[]{:S(2)}, u32[]{:S(2)}) collective-permute-start(bf16[2,96,768]{2,1,0:T(8,128)(2,1)} %maximum_select_fusion.1), channel_id=1, source_target_pairs={{0,16},{1,25},{2,18},{3,27},{4,20},{5,29},{6,22},{7,31},{8,24},{9,... | collective-permute-start | bytes 884744 | tf_op jit(solution)/shard_map/ppermute | solution.py:85
  90.3 22.0 %collective-permute-start.28 = (bf16[2,96,768]{2,1,0:T(8,128)(2,1)}, bf16[2,96,768]{2,1,0:T(8,128)(2,1)}, u32[]{:S(2)}, u32[]{:S(2)}) collective-permute-start(bf16[2,96,768]{2,1,0:T(8,128)(2,1)} %maximum_select_fusion.1), channel_id=1, source_target_pairs={{0,0},{1,9},{2,2},{3,11},{4,4},{5,13},{6,6},{7,15},{8,8},{9,17},{1... | collective-permute-start | bytes 884744 | tf_op jit(solution)/shard_map/ppermute | solution.py:85
  123.9 28.5 %collective-permute-start.33 = (bf16[2,2,96,768]{3,2,1,0:T(8,128)(2,1)S(1)}, bf16[2,2,96,768]{3,2,1,0:T(8,128)(2,1)S(1)}, u32[]{:S(2)}, u32[]{:S(2)}) collective-permute-start(bf16[2,2,96,768]{3,2,1,0:T(8,128)(2,1)S(1)} %pad_maximum_fusion.1.refs_0_), channel_id=1, source_target_pairs={{0,1},{1,0},{2,3},{3,2},{4,5},{5,4},{6,7},{7,6},{8,9},{9,8},{10,11... | collective-permute-start | bytes 1769480 | tf_op jit(solution)/shard_map/ppermute | solution.py:85
  151.9 36.1 %collective-permute-start.59 = (bf16[2,4,96,768]{3,2,1,0:T(8,128)(2,1)S(1)}, bf16[2,4,96,768]{3,2,1,0:T(8,128)(2,1)S(1)}, u32[]{:S(2)}, u32[]{:S(2)}) collective-permute-start(bf16[2,4,96,768]{3,2,1,0:T(8,128)(2,1)S(1)} %get-tuple-element.106), channel_id=1, source_target_pairs={{0,1},{1,0},{2,3},{3,2},{4,5},{5,4},{6,7},{7,6},{8,9},{9,8},{10,11... | collective-permute-start | bytes 3538952 | tf_op jit(solution)/shard_map/ppermute | solution.py:85
  188.0 21.2 %collective-permute-start.58 = (bf16[2,4,96,768]{3,2,1,0:T(8,128)(2,1)S(1)}, bf16[2,4,96,768]{3,2,1,0:T(8,128)(2,1)S(1)}, u32[]{:S(2)}, u32[]{:S(2)}) collective-permute-start(bf16[2,4,96,768]{3,2,1,0:T(8,128)(2,1)S(1)} %get-tuple-element.104), channel_id=1, source_target_pairs={{0,1},{1,0},{2,3},{3,2},{4,5},{5,4},{6,7},{7,6},{8,9},{9,8},{10,11... | collective-permute-start | bytes 3538952 | tf_op jit(solution)/shard_map/ppermute | solution.py:85
  188.4 20.8 %collective-permute-start.60 = (bf16[2,4,96,768]{3,2,1,0:T(8,128)(2,1)S(1)}, bf16[2,4,96,768]{3,2,1,0:T(8,128)(2,1)S(1)}, u32[]{:S(2)}, u32[]{:S(2)}) collective-permute-start(bf16[2,4,96,768]{3,2,1,0:T(8,128)(2,1)S(1)} %shard_map.295), channel_id=1, source_target_pairs={{0,4},{1,3},{2,6},{3,1},{4,0},{5,7},{6,2},{7,5},{8,12},{9,11},{10,... | collective-permute-start | bytes 3538952 | tf_op jit(solution)/shard_map/ppermute | solution.py:85
  192.6 18.3 %collective-permute-start.52 = (bf16[2,4,24,3840]{3,2,1,0:T(8,128)(2,1)S(1)}, bf16[2,4,24,3840]{3,2,1,0:T(8,128)(2,1)S(1)}, u32[]{:S(2)}, u32[]{:S(2)}) collective-permute-start(bf16[2,4,24,3840]{3,2,1,0:T(8,128)(2,1)S(1)} %get-tuple-element.102), channel_id=1, source_target_pairs={{0,1},{1,0},{2,3},{3,2},{4,5},{5,4},{6,7},{7,6},{8,9},{9,8},{10,11... | collective-permute-start | bytes 4423688 | tf_op jit(solution)/shard_map/ppermute | solution.py:85
  205.9 20.9 %collective-permute-start.44 = (bf16[2,4,24,2432]{3,2,1,0:T(8,128)(2,1)S(1)}, bf16[2,4,24,2432]{3,2,1,0:T(8,128)(2,1)S(1)}, u32[]{:S(2)}, u32[]{:S(2)}) collective-permute-start(bf16[2,4,24,2432]{3,2,1,0:T(8,128)(2,1)S(1)} %get-tuple-element.96), channel_id=1, source_target_pairs={{0,1},{1,0},{2,3},{3,2},{4,5},{5,4},{6,7},{7,6},{8,9},{9,8},{10,11... | collective-permute-start | bytes 2801672 | tf_op jit(solution)/shard_map/ppermute | solution.py:85
  208.6 20.0 %collective-permute-start.46 = (bf16[2,4,24,2432]{3,2,1,0:T(8,128)(2,1)S(1)}, bf16[2,4,24,2432]{3,2,1,0:T(8,128)(2,1)S(1)}, u32[]{:S(2)}, u32[]{:S(2)}) collective-permute-start(bf16[2,4,24,2432]{3,2,1,0:T(8,128)(2,1)S(1)} %shard_map.285), channel_id=1, source_target_pairs={{0,4},{1,3},{2,6},{3,1},{4,0},{5,7},{6,2},{7,5},{8,12},{9,11},{10,... | collective-permute-start | bytes 2801672 | tf_op jit(solution)/shard_map/ppermute | solution.py:85
  209.2 37.4 %collective-permute-start.51 = (bf16[2,4,24,3840]{3,2,1,0:T(8,128)(2,1)S(1)}, bf16[2,4,24,3840]{3,2,1,0:T(8,128)(2,1)S(1)}, u32[]{:S(2)}, u32[]{:S(2)}) collective-permute-start(bf16[2,4,24,3840]{3,2,1,0:T(8,128)(2,1)S(1)} %get-tuple-element.100), channel_id=1, source_target_pairs={{0,1},{1,0},{2,3},{3,2},{4,5},{5,4},{6,7},{7,6},{8,9},{9,8},{10,11... | collective-permute-start | bytes 4423688 | tf_op jit(solution)/shard_map/ppermute | solution.py:85
  209.4 16.3 %collective-permute-start.61 = (bf16[1,4,96,768]{3,2,1,0:T(8,128)(2,1)S(1)}, bf16[1,4,96,768]{3,2,1,0:T(8,128)(2,1)S(1)}, u32[]{:S(2)}, u32[]{:S(2)}) collective-permute-start(bf16[1,4,96,768]{3,2,1,0:T(8,128)(2,1)S(1)} %bitcast.146), channel_id=1, source_target_pairs={{0,2},{1,5},{2,0},{3,7},{4,6},{5,1},{6,4},{7,3},{8,10},{9,13},{10,... | collective-permute-start | bytes 1769480 | tf_op jit(solution)/shard_map/ppermute | solution.py:85
  211.2 38.1 %collective-permute-start.53 = (bf16[2,4,24,3840]{3,2,1,0:T(8,128)(2,1)S(1)}, bf16[2,4,24,3840]{3,2,1,0:T(8,128)(2,1)S(1)}, u32[]{:S(2)}, u32[]{:S(2)}) collective-permute-start(bf16[2,4,24,3840]{3,2,1,0:T(8,128)(2,1)S(1)} %shard_map.290), channel_id=1, source_target_pairs={{0,4},{1,3},{2,6},{3,1},{4,0},{5,7},{6,2},{7,5},{8,12},{9,11},{10,... | collective-permute-start | bytes 4423688 | tf_op jit(solution)/shard_map/ppermute | solution.py:85
  261.4 15.5 %collective-permute-start.56 = (bf16[2,24,3840]{2,1,0:T(8,128)(2,1)S(1)}, bf16[2,24,3840]{2,1,0:T(8,128)(2,1)S(1)}, u32[]{:S(2)}, u32[]{:S(2)}) collective-permute-start(bf16[2,24,3840]{2,1,0:T(8,128)(2,1)S(1)} %bitcast.149), channel_id=1, source_target_pairs={{0,16},{1,25},{2,18},{3,27},{4,20},{5,29},{6,22},{7,31},{8,24},{9,... | collective-permute-start | bytes 1105928 | tf_op jit(solution)/shard_map/ppermute | solution.py:85
  (86 other events, 755.8 us)

commit v2 on v1

--- a/solution.py
+++ b/solution.py
@@ -273,8 +273,9 @@
         two = add_parts([(item, pick(j)) for item in held], 2, 2).reshape(1, 4, rows, total)
         final.append((grid.second(two, j), 0))
     half = [add_parts([(item, lambda g, near=near: (0, near, 0, 0)) for item, _ in final], 2, 1)[0] for near in range(2)]
-    four = grid.z_far(half[0]).astype(F32) + grid.z_near(half[1]).astype(F32)
+    four = [grid.z_far(half[0]), grid.z_near(half[1])]
     core = grid.here()[3]
+    four = four[0].astype(F32) + four[1].astype(F32)
     kept = jnp.where(core == 0, four[0], four[1])
     sent = jnp.where(core == 0, four[1], four[0]).astype(BF)
     return kept + grid.core(sent).astype(F32)
@@ -284,11 +285,15 @@
     return lax.dot_general(left, right, (dims, ((), ())), preferred_element_type=F32)
 
 
-def simple(kernel, ins, outs, scratch=()):
+def simple(kernel, ins, outs, scratch=(), fetch=False):
     vmem = pl.BlockSpec(memory_space=pltpu.VMEM)
+    specs = [vmem] * len(ins)
+    if fetch:
+        specs = [pl.BlockSpec(item.shape, lambda g, item=item: (0,) * item.ndim) for item in ins]
     return pl.pallas_call(
         kernel,
-        in_specs=[vmem] * len(ins),
+        grid=(1,) if fetch else (),
+        in_specs=specs,
         out_specs=[vmem] * len(outs),
         out_shape=[jax.ShapeDtypeStruct(shape, kind) for shape, kind in outs],
         scratch_shapes=scratch,
@@ -370,7 +375,7 @@
                 lse_ref[rows, head : head + 1] = top + jnp.log(total)
 
     outs = [((Z * step, group), F32), ((Z * step, heads), F32)] + [((step, group), BF)] * Z
-    made = simple(kernel, [*pieces, *keys, query_pos[:, None], key_pos[None]], outs)
+    made = simple(kernel, [*pieces, *keys, query_pos[:, None], key_pos[None]], outs, fetch=True)
     return made[0], made[1], made[2:]
 
 
@@ -482,7 +487,7 @@
         across = lax.broadcasted_iota(jnp.int32, (rows, rows), 0) == lax.broadcasted_iota(jnp.int32, (rows, rows), 1)
         out[:, width:] = product(across.astype(BF), stacked.astype(BF), ((1,), (1,))).astype(BF)
 
-    return simple(kernel, [w_qkv, spare, *lines], [((rows, width + EXT), BF)])[0]
+    return simple(kernel, [w_qkv, spare, *lines], [((rows, width + EXT), BF)], fetch=True)[0]
 
 
 def local_step(

time: 281 us -> 281 us (level)
  no operation moved by 1% of the time
where the time goes in v2:
time: 281 us; the launch traced here: 280 us
  waiting for transfers between devices  155 us (55%)
  starting transfers between devices  50.6 us (18%)
  Pallas kernels  32.3 us (11%)
  local copies, waits for them, and re-layouts  19.7 us (7%)
  other arithmetic  10.6 us (4%)
  matrix products  9.53 us (3%)
    ppermute x65, waiting for transfers between devices, send(): return lax.ppermute(value, AXES, pairs)  155 us
    ppermute x65, starting transfers between devices, send(): return lax.ppermute(value, AXES, pairs)  50.6 us
    pallas_call x10, Pallas kernels, simple(): pl.pallas_call(kernel, grid=(1,) if fetch else (), in_specs=specs, out_sp...  15.1 us
    unnamed x90, local copies, waits for them, and re-layouts  13.5 us
    pallas_call x3, Pallas kernels, scatter(): pl.pallas_call(kernel, in_specs=[vmem] * inputs, out_specs=[vmem] * (2 *...  9.68 us
  transfers between devices with their start and end apart: 65, of which 26 were waited for; matrix products, arithmetic and copies ran while one was open for 9% of the time, Pallas kernels for 11%

profile of v2, /device:TPU:0, one launch (start us, length us, event | category | flops | bytes accessed | tf_op | source)
XLA Modules:
  0.0 280.1 jit_solution(12050645649261575747)
XLA Ops:
  10.5 4.0 %collective-permute-start.2 = (bf16[2,24,2432]{2,1,0:T(8,128)(2,1)S(1)}, bf16[2,24,2432]{2,1,0:T(8,128)(2,1)S(1)}, u32[]{:S(2)}, u32[]{:S(2)}) collective-permute-start(bf16[2,24,2432]{2,1,0:T(8,128)(2,1)S(1)} %maximum_select_fusion.2), channel_id=1, source_target_pairs={{0,16},{1,25},{2,18},{3,27},{4,20},{5,29},{6,22},{7,31},{8,24},{9,... | collective-permute-start | bytes 700424 | tf_op jit(solution)/shard_map/ppermute | solution.py:85
  15.8 9.8 %collective-permute-done.2 = bf16[2,24,2432]{2,1,0:T(8,128)(2,1)S(1)} collective-permute-done((bf16[2,24,2432]{2,1,0:T(8,128)(2,1)S(1)}, bf16[2,24,2432]{2,1,0:T(8,128)(2,1)S(1)}, u32[]{:S(2)}, u32[]{:S(2)}) %collective-permute-start.2) | collective-permute-done | bytes 233504 | tf_op jit(solution)/shard_map/ppermute | solution.py:85
  29.1 10.2 %collective-permute-done.4.refs_2_ = bf16[2,2,24,2432]{3,2,1,0:T(8,128)(2,1)S(1)} collective-permute-done((bf16[2,2,24,2432]{3,2,1,0:T(8,128)(2,1)S(1)}, bf16[2,2,24,2432]{3,2,1,0:T(8,128)(2,1)S(1)}, u32[]{:S(2)}, u32[]{:S(2)}) %collective-permute-start.4) | collective-permute-done | bytes 466976 | tf_op jit(solution)/shard_map/ppermute | solution.py:85
  41.5 17.6 %collective-permute-done.19 = bf16[2,24,3840]{2,1,0:T(8,128)(2,1)S(1)} collective-permute-done((bf16[2,24,3840]{2,1,0:T(8,128)(2,1)S(1)}, bf16[2,24,3840]{2,1,0:T(8,128)(2,1)S(1)}, u32[]{:S(2)}, u32[]{:S(2)}) %collective-permute-start.19) | collective-permute-done | bytes 368672 | tf_op jit(solution)/shard_map/ppermute | solution.py:85
  67.2 8.6 %collective-permute-done.21.refs_2_ = bf16[2,2,24,3840]{3,2,1,0:T(8,128)(2,1)} collective-permute-done((bf16[2,2,24,3840]{3,2,1,0:T(8,128)(2,1)}, bf16[2,2,24,3840]{3,2,1,0:T(8,128)(2,1)}, u32[]{:S(2)}, u32[]{:S(2)}) %collective-permute-start.21) | collective-permute-done | bytes 737312 | tf_op jit(solution)/shard_map/ppermute | solution.py:85
  78.1 6.6 %collective-permute-done.11.refs_2_ = bf16[128,576]{1,0:T(8,128)(2,1)S(1)} collective-permute-done((bf16[128,576]{1,0:T(8,128)(2,1)S(1)}, bf16[128,576]{1,0:T(8,128)(2,1)S(1)}, u32[]{:S(2)}, u32[]{:S(2)}) %collective-permute-start.11) | collective-permute-done | bytes 147488 | tf_op jit(solution)/shard_map/ppermute | solution.py:85
  90.3 3.7 %collective-permute-start.28 = (bf16[2,96,768]{2,1,0:T(8,128)(2,1)}, bf16[2,96,768]{2,1,0:T(8,128)(2,1)}, u32[]{:S(2)}, u32[]{:S(2)}) collective-permute-start(bf16[2,96,768]{2,1,0:T(8,128)(2,1)} %maximum_select_fusion.1), channel_id=1, source_target_pairs={{0,0},{1,9},{2,2},{3,11},{4,4},{5,13},{6,6},{7,15},{8,8},{9,17},{1... | collective-permute-start | bytes 884744 | tf_op jit(solution)/shard_map/ppermute | solution.py:85
  101.7 5.8 %shard_map.275 = (f32[512,192]{1,0:T(8,128)S(1)}, f32[512,3]{1,0:T(8,128)S(1)}, bf16[128,192]{1,0:T(8,128)(2,1)S(1)}, bf16[128,192]{1,0:T(8,128)(2,1)S(1)}, bf16...) custom-call(bf16[128,576]{1,0:T(8,128)(2,1)S(1)} %copy-done.3, bf16[128,576]{1,0:T(8,128)(2,1)S(1)} %copy-done.6, ...), custom_call_target="tpu_custom_call" | custom-call | tf_op jit(solution)/shard_map/pallas_call | solution.py:293
  107.5 3.2 %collective-permute-start.14 = (bf16[128,192]{1,0:T(8,128)(2,1)S(1)}, bf16[128,192]{1,0:T(8,128)(2,1)S(1)}, u32[]{:S(2)}, u32[]{:S(2)}) collective-permute-start(bf16[128,192]{1,0:T(8,128)(2,1)S(1)} %get-tuple-element.70), channel_id=1, source_target_pairs={{0,24},{1,25},{2,26},{3,27},{4,28},{5,29},{6,30},{7,31},{8,0},{9,1... | collective-permute-start | bytes 147464 | tf_op jit(solution)/shard_map/ppermute | solution.py:85
  117.3 5.0 %collective-permute-done.16.refs_3_ = bf16[128,192]{1,0:T(8,128)(2,1)S(1)} collective-permute-done((bf16[128,192]{1,0:T(8,128)(2,1)S(1)}, bf16[128,192]{1,0:T(8,128)(2,1)S(1)}, u32[]{:S(2)}, u32[]{:S(2)}) %collective-permute-start.16) | collective-permute-done | bytes 49184 | tf_op jit(solution)/shard_map/ppermute | solution.py:85
  126.9 10.4 %collective-permute-done.31.refs_2_ = bf16[2,2,96,768]{3,2,1,0:T(8,128)(2,1)S(1)} collective-permute-done((bf16[2,2,96,768]{3,2,1,0:T(8,128)(2,1)S(1)}, bf16[2,2,96,768]{3,2,1,0:T(8,128)(2,1)S(1)}, u32[]{:S(2)}, u32[]{:S(2)}) %collective-permute-start.31) | collective-permute-done | bytes 589856 | tf_op jit(solution)/shard_map/ppermute | solution.py:85
  139.2 8.0 %collective-permute-done.32.refs_3_ = bf16[2,2,96,768]{3,2,1,0:T(8,128)(2,1)S(1)} collective-permute-done((bf16[2,2,96,768]{3,2,1,0:T(8,128)(2,1)S(1)}, bf16[2,2,96,768]{3,2,1,0:T(8,128)(2,1)S(1)}, u32[]{:S(2)}, u32[]{:S(2)}) %collective-permute-start.32) | collective-permute-done | bytes 589856 | tf_op jit(solution)/shard_map/ppermute | solution.py:85
  148.7 3.2 %shard_map.294 = (bf16[2,4,96,768]{3,2,1,0:T(8,128)(2,1)S(1)}, bf16[2,4,96,768]{3,2,1,0:T(8,128)(2,1)S(1)}, bf16[2,4,96,768]{3,2,1,0:T(8,128)(2,1)S(1)}, bf16[2,4,96,768]{3,2,1,0:T(8,128)(2,1)S(1)}) custom-call(bf16[128,3072]{1,0:T(8,128)(2,1)S(1)} %get-tuple-element.158.refs_0_, bf16[128,768]{1,0:T(8,128)(2,1)S(1)} %get-tuple-element.149.refs_1_), custom_call_target="tpu_custom_call" | custom-call | tf_op jit(solution)/shard_map/pallas_call | solution.py:250
  158.8 3.6 %collective-permute-start.39 = (bf16[128,192]{1,0:T(8,128)(2,1)S(1)}, bf16[128,192]{1,0:T(8,128)(2,1)S(1)}, u32[]{:S(2)}, u32[]{:S(2)}) collective-permute-start(bf16[128,192]{1,0:T(8,128)(2,1)S(1)} %get-tuple-element.85), channel_id=1, source_target_pairs={{0,24},{1,25},{2,26},{3,27},{4,28},{5,29},{6,30},{7,31},{8,0},{9,1... | collective-permute-start | bytes 147464 | tf_op jit(solution)/shard_map/ppermute | solution.py:85
  162.4 3.0 %collective-permute-done.37.refs_11_ = bf16[128,192]{1,0:T(8,128)(2,1)S(1)} collective-permute-done((bf16[128,192]{1,0:T(8,128)(2,1)S(1)}, bf16[128,192]{1,0:T(8,128)(2,1)S(1)}, u32[]{:S(2)}, u32[]{:S(2)}) %collective-permute-start.37) | collective-permute-done | bytes 49184 | tf_op jit(solution)/shard_map/ppermute | solution.py:85
  167.2 7.1 %shard_map.280 = (bf16[512,192]{1,0:T(8,128)(2,1)S(1)}, f32[512,384]{1,0:T(8,128)S(1)}, bf16[512,384]{1,0:T(8,128)(2,1)S(1)}) custom-call(bf16[128,576]{1,0:T(8,128)(2,1)S(1)} %copy-done.4, bf16[128,576]{1,0:T(8,128)(2,1)S(1)} %copy-done.7, bf16[128,576]{1,0:T(8,128)(2,1)S(1)} %copy-done.10, bf16[128,576]{1,0:T(8,128)(2,1)S(1)} %copy-done.13, ...), custom_call_target="tpu_custom_call" | custom-call | tf_op jit(solution)/shard_map/pallas_call | solution.py:293
  174.4 9.5 %collective-permute-done.40.refs_2_ = bf16[512,384]{1,0:T(8,128)(2,1)S(1)} collective-permute-done((bf16[512,384]{1,0:T(8,128)(2,1)S(1)}, bf16[512,384]{1,0:T(8,128)(2,1)S(1)}, u32[]{:S(2)}, u32[]{:S(2)}) %collective-permute-start.40) | collective-permute-done | bytes 393248 | tf_op jit(solution)/shard_map/ppermute | solution.py:85
  188.7 3.6 %shard_map.289 = (bf16[2,4,24,3840]{3,2,1,0:T(8,128)(2,1)S(1)}, bf16[2,4,24,3840]{3,2,1,0:T(8,128)(2,1)S(1)}, bf16[2,4,24,3840]{3,2,1,0:T(8,128)(2,1)S(1)}, bf16[2,4,24,3840]{3,2,1,0:T(8,128)(2,1)S(1)}) custom-call(bf16[128,768]{1,0:T(8,128)(2,1)S(1)} %get-tuple-element.73.refs_0_, bf16[128,768]{1,0:T(8,128)(2,1)S(1)} %add_convert_fusion.refs_1_, ...), custom_call_target="tpu_custom_call" | custom-call | tf_op jit(solution)/shard_map/pallas_call | solution.py:250
  193.3 8.0 %collective-permute-done.42.refs_2_ = bf16[128,576]{1,0:T(8,128)(2,1)S(1)} collective-permute-done((bf16[128,576]{1,0:T(8,128)(2,1)S(1)}, bf16[128,576]{1,0:T(8,128)(2,1)S(1)}, u32[]{:S(2)}, u32[]{:S(2)}) %collective-permute-start.42) | collective-permute-done | bytes 147488 | tf_op jit(solution)/shard_map/ppermute | solution.py:85
  213.6 12.1 %collective-permute-done.61.refs_3_ = bf16[1,4,96,768]{3,2,1,0:T(8,128)(2,1)S(1)} collective-permute-done((bf16[1,4,96,768]{3,2,1,0:T(8,128)(2,1)S(1)}, bf16[1,4,96,768]{3,2,1,0:T(8,128)(2,1)S(1)}, u32[]{:S(2)}, u32[]{:S(2)}) %collective-permute-start.61) | collective-permute-done | bytes 589856 | tf_op jit(solution)/shard_map/ppermute | solution.py:85
  230.4 9.3 %collective-permute-done.63 = bf16[2,96,768]{2,1,0:T(8,128)(2,1)S(1)} collective-permute-done((bf16[2,96,768]{2,1,0:T(8,128)(2,1)S(1)}, bf16[2,96,768]{2,1,0:T(8,128)(2,1)S(1)}, u32[]{:S(2)}, u32[]{:S(2)}) %collective-permute-start.63) | collective-permute-done | bytes 294944 | tf_op jit(solution)/shard_map/ppermute | solution.py:85
  250.4 4.5 %collective-permute-done.49 = bf16[2,24,2432]{2,1,0:T(8,128)(2,1)S(1)} collective-permute-done((bf16[2,24,2432]{2,1,0:T(8,128)(2,1)S(1)}, bf16[2,24,2432]{2,1,0:T(8,128)(2,1)S(1)}, u32[]{:S(2)}, u32[]{:S(2)}) %collective-permute-start.49) | collective-permute-done | bytes 233504 | tf_op jit(solution)/shard_map/ppermute | solution.py:85
  256.4 4.8 %collective-permute-done.54.refs_3_ = bf16[1,4,24,3840]{3,2,1,0:T(8,128)(2,1)S(1)} collective-permute-done((bf16[1,4,24,3840]{3,2,1,0:T(8,128)(2,1)S(1)}, bf16[1,4,24,3840]{3,2,1,0:T(8,128)(2,1)S(1)}, u32[]{:S(2)}, u32[]{:S(2)}) %collective-permute-start.54) | collective-permute-done | bytes 737312 | tf_op jit(solution)/shard_map/ppermute | solution.py:85
  263.4 13.5 %collective-permute-done.56 = bf16[2,24,3840]{2,1,0:T(8,128)(2,1)S(1)} collective-permute-done((bf16[2,24,3840]{2,1,0:T(8,128)(2,1)S(1)}, bf16[2,24,3840]{2,1,0:T(8,128)(2,1)S(1)}, u32[]{:S(2)}, u32[]{:S(2)}) %collective-permute-start.56) | collective-permute-done | bytes 368672 | tf_op jit(solution)/shard_map/ppermute | solution.py:85
  (300 shorter events, 103.2 us)
Async XLA Ops:
  9.1 31.3 %collective-permute-start.17 = (bf16[24,3840]{1,0:T(8,128)(2,1)S(1)}, bf16[24,3840]{1,0:T(8,128)(2,1)S(1)}, u32[]{:S(2)}, u32[]{:S(2)}) collective-permute-start(bf16[24,3840]{1,0:T(8,128)(2,1)S(1)} %get-tuple-element.153), channel_id=1, source_target_pairs={{0,1},{1,0},{2,3},{3,2},{4,5},{5,4},{6,7},{7,6},{8,9},{9,8},{10,11... | collective-permute-start | bytes 552968 | tf_op jit(solution)/shard_map/ppermute | solution.py:85
  10.5 15.2 %collective-permute-start.2 = (bf16[2,24,2432]{2,1,0:T(8,128)(2,1)S(1)}, bf16[2,24,2432]{2,1,0:T(8,128)(2,1)S(1)}, u32[]{:S(2)}, u32[]{:S(2)}) collective-permute-start(bf16[2,24,2432]{2,1,0:T(8,128)(2,1)S(1)} %maximum_select_fusion.2), channel_id=1, source_target_pairs={{0,16},{1,25},{2,18},{3,27},{4,20},{5,29},{6,22},{7,31},{8,24},{9,... | collective-permute-start | bytes 700424 | tf_op jit(solution)/shard_map/ppermute | solution.py:85
  27.5 31.6 %collective-permute-start.3 = (bf16[2,2,24,2432]{3,2,1,0:T(8,128)(2,1)S(1)}, bf16[2,2,24,2432]{3,2,1,0:T(8,128)(2,1)S(1)}, u32[]{:S(2)}, u32[]{:S(2)}) collective-permute-start(bf16[2,2,24,2432]{3,2,1,0:T(8,128)(2,1)S(1)} %pad_maximum_fusion.2.refs_0_), channel_id=1, source_target_pairs={{0,2},{1,5},{2,0},{3,7},{4,6},{5,1},{6,4},{7,3},{8,10},{9,13},{10,... | collective-permute-start | bytes 1400840 | tf_op jit(solution)/shard_map/ppermute | solution.py:85
  39.4 20.2 %collective-permute-start.5 = (bf16[2,2,24,2432]{3,2,1,0:T(8,128)(2,1)S(1)}, bf16[2,2,24,2432]{3,2,1,0:T(8,128)(2,1)S(1)}, u32[]{:S(2)}, u32[]{:S(2)}) collective-permute-start(bf16[2,2,24,2432]{3,2,1,0:T(8,128)(2,1)S(1)} %collective-permute-done.4.refs_2_), channel_id=1, source_target_pairs={{0,2},{1,5},{2,0},{3,7},{4,6},{5,1},{6,4},{7,3},{8,10},{9,13},{10,... | collective-permute-start | bytes 1400840 | tf_op jit(solution)/shard_map/ppermute | solution.py:85
  40.4 18.7 %collective-permute-start.19 = (bf16[2,24,3840]{2,1,0:T(8,128)(2,1)S(1)}, bf16[2,24,3840]{2,1,0:T(8,128)(2,1)S(1)}, u32[]{:S(2)}, u32[]{:S(2)}) collective-permute-start(bf16[2,24,3840]{2,1,0:T(8,128)(2,1)S(1)} %maximum_select_fusion), channel_id=1, source_target_pairs={{0,16},{1,25},{2,18},{3,27},{4,20},{5,29},{6,22},{7,31},{8,24},{9,... | collective-permute-start | bytes 1105928 | tf_op jit(solution)/shard_map/ppermute | solution.py:85
  40.5 19.2 %collective-permute-start.18 = (bf16[2,24,3840]{2,1,0:T(8,128)(2,1)S(1)}, bf16[2,24,3840]{2,1,0:T(8,128)(2,1)S(1)}, u32[]{:S(2)}, u32[]{:S(2)}) collective-permute-start(bf16[2,24,3840]{2,1,0:T(8,128)(2,1)S(1)} %maximum_select_fusion), channel_id=1, source_target_pairs={{0,0},{1,9},{2,2},{3,11},{4,4},{5,13},{6,6},{7,15},{8,8},{9,17},{1... | collective-permute-start | bytes 1105928 | tf_op jit(solution)/shard_map/ppermute | solution.py:85
  41.2 20.8 %collective-permute-start.6 = (bf16[2,2,24,2432]{3,2,1,0:T(8,128)(2,1)S(1)}, bf16[2,2,24,2432]{3,2,1,0:T(8,128)(2,1)S(1)}, u32[]{:S(2)}, u32[]{:S(2)}) collective-permute-start(bf16[2,2,24,2432]{3,2,1,0:T(8,128)(2,1)S(1)} %pad_maximum_fusion.2.refs_0_), channel_id=1, source_target_pairs={{0,1},{1,0},{2,3},{3,2},{4,5},{5,4},{6,7},{7,6},{8,9},{9,8},{10,11... | collective-permute-start | bytes 1400840 | tf_op jit(solution)/shard_map/ppermute | solution.py:85
  60.6 15.1 %collective-permute-start.21 = (bf16[2,2,24,3840]{3,2,1,0:T(8,128)(2,1)}, bf16[2,2,24,3840]{3,2,1,0:T(8,128)(2,1)}, u32[]{:S(2)}, u32[]{:S(2)}) collective-permute-start(bf16[2,2,24,3840]{3,2,1,0:T(8,128)(2,1)} %pad_maximum_fusion.refs_0_), channel_id=1, source_target_pairs={{0,4},{1,3},{2,6},{3,1},{4,0},{5,7},{6,2},{7,5},{8,12},{9,11},{10,... | collective-permute-start | bytes 2211848 | tf_op jit(solution)/shard_map/ppermute | solution.py:85
  62.1 26.9 %collective-permute-start.27 = (bf16[96,768]{1,0:T(8,128)(2,1)S(1)}, bf16[96,768]{1,0:T(8,128)(2,1)S(1)}, u32[]{:S(2)}, u32[]{:S(2)}) collective-permute-start(bf16[96,768]{1,0:T(8,128)(2,1)S(1)} %bitcast.167), channel_id=1, source_target_pairs={{0,1},{1,0},{2,3},{3,2},{4,5},{5,4},{6,7},{7,6},{8,9},{9,8},{10,11... | collective-permute-start | bytes 442376 | tf_op jit(solution)/shard_map/ppermute | solution.py:85
  65.6 46.7 %collective-permute-start.20 = (bf16[2,2,24,3840]{3,2,1,0:T(8,128)(2,1)}, bf16[2,2,24,3840]{3,2,1,0:T(8,128)(2,1)}, u32[]{:S(2)}, u32[]{:S(2)}) collective-permute-start(bf16[2,2,24,3840]{3,2,1,0:T(8,128)(2,1)} %pad_maximum_fusion.refs_0_), channel_id=1, source_target_pairs={{0,2},{1,5},{2,0},{3,7},{4,6},{5,1},{6,4},{7,3},{8,10},{9,13},{10,... | collective-permute-start | bytes 2211848 | tf_op jit(solution)/shard_map/ppermute | solution.py:85
  75.8 37.0 %collective-permute-start.22 = (bf16[2,2,24,3840]{3,2,1,0:T(8,128)(2,1)}, bf16[2,2,24,3840]{3,2,1,0:T(8,128)(2,1)}, u32[]{:S(2)}, u32[]{:S(2)}) collective-permute-start(bf16[2,2,24,3840]{3,2,1,0:T(8,128)(2,1)} %collective-permute-done.21.refs_2_), channel_id=1, source_target_pairs={{0,2},{1,5},{2,0},{3,7},{4,6},{5,1},{6,4},{7,3},{8,10},{9,13},{10,... | collective-permute-start | bytes 2211848 | tf_op jit(solution)/shard_map/ppermute | solution.py:85
  89.8 20.9 %collective-permute-start.29 = (bf16[2,96,768]{2,1,0:T(8,128)(2,1)}, bf16[2,96,768]{2,1,0:T(8,128)(2,1)}, u32[]{:S(2)}, u32[]{:S(2)}) collective-permute-start(bf16[2,96,768]{2,1,0:T(8,128)(2,1)} %maximum_select_fusion.1), channel_id=1, source_target_pairs={{0,16},{1,25},{2,18},{3,27},{4,20},{5,29},{6,22},{7,31},{8,24},{9,... | collective-permute-start | bytes 884744 | tf_op jit(solution)/shard_map/ppermute | solution.py:85
  90.3 22.0 %collective-permute-start.28 = (bf16[2,96,768]{2,1,0:T(8,128)(2,1)}, bf16[2,96,768]{2,1,0:T(8,128)(2,1)}, u32[]{:S(2)}, u32[]{:S(2)}) collective-permute-start(bf16[2,96,768]{2,1,0:T(8,128)(2,1)} %maximum_select_fusion.1), channel_id=1, source_target_pairs={{0,0},{1,9},{2,2},{3,11},{4,4},{5,13},{6,6},{7,15},{8,8},{9,17},{1... | collective-permute-start | bytes 884744 | tf_op jit(solution)/shard_map/ppermute | solution.py:85
  123.9 28.5 %collective-permute-start.33 = (bf16[2,2,96,768]{3,2,1,0:T(8,128)(2,1)S(1)}, bf16[2,2,96,768]{3,2,1,0:T(8,128)(2,1)S(1)}, u32[]{:S(2)}, u32[]{:S(2)}) collective-permute-start(bf16[2,2,96,768]{3,2,1,0:T(8,128)(2,1)S(1)} %pad_maximum_fusion.1.refs_0_), channel_id=1, source_target_pairs={{0,1},{1,0},{2,3},{3,2},{4,5},{5,4},{6,7},{7,6},{8,9},{9,8},{10,11... | collective-permute-start | bytes 1769480 | tf_op jit(solution)/shard_map/ppermute | solution.py:85
  151.9 36.1 %collective-permute-start.59 = (bf16[2,4,96,768]{3,2,1,0:T(8,128)(2,1)S(1)}, bf16[2,4,96,768]{3,2,1,0:T(8,128)(2,1)S(1)}, u32[]{:S(2)}, u32[]{:S(2)}) collective-permute-start(bf16[2,4,96,768]{3,2,1,0:T(8,128)(2,1)S(1)} %get-tuple-element.106), channel_id=1, source_target_pairs={{0,1},{1,0},{2,3},{3,2},{4,5},{5,4},{6,7},{7,6},{8,9},{9,8},{10,11... | collective-permute-start | bytes 3538952 | tf_op jit(solution)/shard_map/ppermute | solution.py:85
  188.0 21.2 %collective-permute-start.58 = (bf16[2,4,96,768]{3,2,1,0:T(8,128)(2,1)S(1)}, bf16[2,4,96,768]{3,2,1,0:T(8,128)(2,1)S(1)}, u32[]{:S(2)}, u32[]{:S(2)}) collective-permute-start(bf16[2,4,96,768]{3,2,1,0:T(8,128)(2,1)S(1)} %get-tuple-element.104), channel_id=1, source_target_pairs={{0,1},{1,0},{2,3},{3,2},{4,5},{5,4},{6,7},{7,6},{8,9},{9,8},{10,11... | collective-permute-start | bytes 3538952 | tf_op jit(solution)/shard_map/ppermute | solution.py:85
  188.4 20.8 %collective-permute-start.60 = (bf16[2,4,96,768]{3,2,1,0:T(8,128)(2,1)S(1)}, bf16[2,4,96,768]{3,2,1,0:T(8,128)(2,1)S(1)}, u32[]{:S(2)}, u32[]{:S(2)}) collective-permute-start(bf16[2,4,96,768]{3,2,1,0:T(8,128)(2,1)S(1)} %shard_map.295), channel_id=1, source_target_pairs={{0,4},{1,3},{2,6},{3,1},{4,0},{5,7},{6,2},{7,5},{8,12},{9,11},{10,... | collective-permute-start | bytes 3538952 | tf_op jit(solution)/shard_map/ppermute | solution.py:85
  192.6 18.3 %collective-permute-start.52 = (bf16[2,4,24,3840]{3,2,1,0:T(8,128)(2,1)S(1)}, bf16[2,4,24,3840]{3,2,1,0:T(8,128)(2,1)S(1)}, u32[]{:S(2)}, u32[]{:S(2)}) collective-permute-start(bf16[2,4,24,3840]{3,2,1,0:T(8,128)(2,1)S(1)} %get-tuple-element.102), channel_id=1, source_target_pairs={{0,1},{1,0},{2,3},{3,2},{4,5},{5,4},{6,7},{7,6},{8,9},{9,8},{10,11... | collective-permute-start | bytes 4423688 | tf_op jit(solution)/shard_map/ppermute | solution.py:85
  205.9 20.9 %collective-permute-start.44 = (bf16[2,4,24,2432]{3,2,1,0:T(8,128)(2,1)S(1)}, bf16[2,4,24,2432]{3,2,1,0:T(8,128)(2,1)S(1)}, u32[]{:S(2)}, u32[]{:S(2)}) collective-permute-start(bf16[2,4,24,2432]{3,2,1,0:T(8,128)(2,1)S(1)} %get-tuple-element.96), channel_id=1, source_target_pairs={{0,1},{1,0},{2,3},{3,2},{4,5},{5,4},{6,7},{7,6},{8,9},{9,8},{10,11... | collective-permute-start | bytes 2801672 | tf_op jit(solution)/shard_map/ppermute | solution.py:85
  208.6 20.0 %collective-permute-start.46 = (bf16[2,4,24,2432]{3,2,1,0:T(8,128)(2,1)S(1)}, bf16[2,4,24,2432]{3,2,1,0:T(8,128)(2,1)S(1)}, u32[]{:S(2)}, u32[]{:S(2)}) collective-permute-start(bf16[2,4,24,2432]{3,2,1,0:T(8,128)(2,1)S(1)} %shard_map.285), channel_id=1, source_target_pairs={{0,4},{1,3},{2,6},{3,1},{4,0},{5,7},{6,2},{7,5},{8,12},{9,11},{10,... | collective-permute-start | bytes 2801672 | tf_op jit(solution)/shard_map/ppermute | solution.py:85
  209.2 37.4 %collective-permute-start.51 = (bf16[2,4,24,3840]{3,2,1,0:T(8,128)(2,1)S(1)}, bf16[2,4,24,3840]{3,2,1,0:T(8,128)(2,1)S(1)}, u32[]{:S(2)}, u32[]{:S(2)}) collective-permute-start(bf16[2,4,24,3840]{3,2,1,0:T(8,128)(2,1)S(1)} %get-tuple-element.100), channel_id=1, source_target_pairs={{0,1},{1,0},{2,3},{3,2},{4,5},{5,4},{6,7},{7,6},{8,9},{9,8},{10,11... | collective-permute-start | bytes 4423688 | tf_op jit(solution)/shard_map/ppermute | solution.py:85
  209.4 16.3 %collective-permute-start.61 = (bf16[1,4,96,768]{3,2,1,0:T(8,128)(2,1)S(1)}, bf16[1,4,96,768]{3,2,1,0:T(8,128)(2,1)S(1)}, u32[]{:S(2)}, u32[]{:S(2)}) collective-permute-start(bf16[1,4,96,768]{3,2,1,0:T(8,128)(2,1)S(1)} %bitcast.146), channel_id=1, source_target_pairs={{0,2},{1,5},{2,0},{3,7},{4,6},{5,1},{6,4},{7,3},{8,10},{9,13},{10,... | collective-permute-start | bytes 1769480 | tf_op jit(solution)/shard_map/ppermute | solution.py:85
  211.2 38.1 %collective-permute-start.53 = (bf16[2,4,24,3840]{3,2,1,0:T(8,128)(2,1)S(1)}, bf16[2,4,24,3840]{3,2,1,0:T(8,128)(2,1)S(1)}, u32[]{:S(2)}, u32[]{:S(2)}) collective-permute-start(bf16[2,4,24,3840]{3,2,1,0:T(8,128)(2,1)S(1)} %shard_map.290), channel_id=1, source_target_pairs={{0,4},{1,3},{2,6},{3,1},{4,0},{5,7},{6,2},{7,5},{8,12},{9,11},{10,... | collective-permute-start | bytes 4423688 | tf_op jit(solution)/shard_map/ppermute | solution.py:85
  261.4 15.5 %collective-permute-start.56 = (bf16[2,24,3840]{2,1,0:T(8,128)(2,1)S(1)}, bf16[2,24,3840]{2,1,0:T(8,128)(2,1)S(1)}, u32[]{:S(2)}, u32[]{:S(2)}) collective-permute-start(bf16[2,24,3840]{2,1,0:T(8,128)(2,1)S(1)} %bitcast.149), channel_id=1, source_target_pairs={{0,16},{1,25},{2,18},{3,27},{4,20},{5,29},{6,22},{7,31},{8,24},{9,... | collective-permute-start | bytes 1105928 | tf_op jit(solution)/shard_map/ppermute | solution.py:85
  (86 other events, 755.8 us)

commit v3 on v1

--- a/solution.py
+++ b/solution.py
@@ -273,8 +273,9 @@
         two = add_parts([(item, pick(j)) for item in held], 2, 2).reshape(1, 4, rows, total)
         final.append((grid.second(two, j), 0))
     half = [add_parts([(item, lambda g, near=near: (0, near, 0, 0)) for item, _ in final], 2, 1)[0] for near in range(2)]
-    four = grid.z_far(half[0]).astype(F32) + grid.z_near(half[1]).astype(F32)
+    four = [grid.z_far(half[0]), grid.z_near(half[1])]
     core = grid.here()[3]
+    four = four[0].astype(F32) + four[1].astype(F32)
     kept = jnp.where(core == 0, four[0], four[1])
     sent = jnp.where(core == 0, four[1], four[0]).astype(BF)
     return kept + grid.core(sent).astype(F32)
@@ -284,14 +285,27 @@
     return lax.dot_general(left, right, (dims, ((), ())), preferred_element_type=F32)
 
 
-def simple(kernel, ins, outs, scratch=()):
+def simple(kernel, ins, outs, scratch=(), fetch=0):
     vmem = pl.BlockSpec(memory_space=pltpu.VMEM)
+    held = [pltpu.VMEM(item.shape, item.dtype) for item in ins[:fetch]]
+
+    def fetched(*refs):
+        body = refs[: len(refs) - fetch - 1]
+        slots, sem = refs[len(body) : -1], refs[-1]
+        copies = [pltpu.make_async_copy(ref, slot, sem.at[at]) for at, (ref, slot) in enumerate(zip(body, slots))]
+        for copy in copies:
+            copy.start()
+        for copy in copies:
+            copy.wait()
+        kernel(*slots, *body[fetch:])
+
+    extra = held + [pltpu.SemaphoreType.DMA((fetch,))] if fetch else []
     return pl.pallas_call(
-        kernel,
-        in_specs=[vmem] * len(ins),
+        fetched if fetch else kernel,
+        in_specs=[pl.BlockSpec(memory_space=pltpu.HBM)] * fetch + [vmem] * (len(ins) - fetch),
         out_specs=[vmem] * len(outs),
         out_shape=[jax.ShapeDtypeStruct(shape, kind) for shape, kind in outs],
-        scratch_shapes=scratch,
+        scratch_shapes=list(scratch) + extra,
         compiler_params=pltpu.CompilerParams(vmem_limit_bytes=12 * 1024 * 1024),
     )(*ins)
 
@@ -348,8 +362,8 @@
     scale = HEAD_DIM ** (-0.5)
 
     def kernel(*refs):
-        piece_refs, key_refs = refs[:Z], refs[Z : Z + len(keys)]
-        row_ref, col_ref, mixed_ref, lse_ref = refs[Z + len(keys) : Z + len(keys) + 4]
+        piece_refs, row_ref, key_refs = refs[:Z], refs[Z], refs[Z + 1 : Z + 1 + len(keys)]
+        col_ref, mixed_ref, lse_ref = refs[Z + 1 + len(keys) : Z + len(keys) + 4]
         sent = refs[Z + len(keys) + 4 :]
         for head in range(heads):
             low = head * HEAD_DIM
@@ -370,7 +384,7 @@
                 lse_ref[rows, head : head + 1] = top + jnp.log(total)
 
     outs = [((Z * step, group), F32), ((Z * step, heads), F32)] + [((step, group), BF)] * Z
-    made = simple(kernel, [*pieces, *keys, query_pos[:, None], key_pos[None]], outs)
+    made = simple(kernel, [*pieces, query_pos[:, None], *keys, key_pos[None]], outs, fetch=Z + 1)
     return made[0], made[1], made[2:]
 
 
@@ -482,7 +496,7 @@
         across = lax.broadcasted_iota(jnp.int32, (rows, rows), 0) == lax.broadcasted_iota(jnp.int32, (rows, rows), 1)
         out[:, width:] = product(across.astype(BF), stacked.astype(BF), ((1,), (1,))).astype(BF)
 
-    return simple(kernel, [w_qkv, spare, *lines], [((rows, width + EXT), BF)])[0]
+    return simple(kernel, [w_qkv, spare, *lines], [((rows, width + EXT), BF)], fetch=len(lines) + 2)[0]
 
 
 def local_step(
@@ -544,7 +558,6 @@
     own_keys = jnp.concatenate([piece[:, group:] for piece in packed])
     all_keys = [own_keys] + [grid.along_x(own_keys, dx) for dx in range(1, X)]
     mixed_local, log_total, mixed_send = attend(packed, all_keys, query_pos, key_pos, heads)
-    log_total, *last_z = lax.optimization_barrier((log_total, *last_z))
     (w_down,) = gather(grid, last_z, [D])
     mixed_round, _ = join_groups(grid, collect(mixed_send), 1)
 

time: 281 us -> 311 us (1.11)
  waiting for transfers between devices: 155 us -> 177 us
  starting transfers between devices: 50.6 us -> 58.2 us
    ppermute x65, waiting for transfers between devices: 155 us -> 177 us  [send(): return lax.ppermute(value, AXES, pairs)]
    ppermute x65, starting transfers between devices: 50.6 us -> 58.2 us  [send(): return lax.ppermute(value, AXES, pairs)]
    unnamed x90 -> x108, local copies, waits for them, and re-layouts: 13.5 us -> 14.5 us
  transfers between devices with their start and end apart: 65 -> 65, of which waited for: 26 -> 25; matrix products, arithmetic and copies ran while one was open for 9% -> 5% of each run, Pallas kernels for 11% -> 8%
where the time goes in v3:
time: 311 us
  waiting for transfers between devices  177 us (57%)
  starting transfers between devices  58.2 us (19%)
  Pallas kernels  33.9 us (11%)
  local copies, waits for them, and re-layouts  20.7 us (7%)
  matrix products  9.45 us (3%)
  other arithmetic  9.1 us (3%)
    ppermute x65, waiting for transfers between devices, send(): return lax.ppermute(value, AXES, pairs)  177 us
    ppermute x65, starting transfers between devices, send(): return lax.ppermute(value, AXES, pairs)  58.2 us
    pallas_call x10, Pallas kernels, simple(): pl.pallas_call(fetched if fetch else kernel, in_specs=[pl.BlockSpec(memor...  16.3 us
    unnamed x108, local copies, waits for them, and re-layouts  14.5 us
    pallas_call x3, Pallas kernels, scatter(): pl.pallas_call(kernel, in_specs=[vmem] * inputs, out_specs=[vmem] * (2 *...  9.68 us
  transfers between devices with their start and end apart: 65, of which 25 were waited for; matrix products, arithmetic and copies ran while one was open for 5% of the time, Pallas kernels for 8%

profile of v3, /device:TPU:0, one launch (start us, length us, event | category | flops | bytes accessed | tf_op | source)
XLA Modules:
  0.0 310.5 jit_solution(16897229246523608884)
XLA Ops:
  10.1 3.8 %collective-permute-start.2 = (bf16[2,24,2432]{2,1,0:T(8,128)(2,1)S(1)}, bf16[2,24,2432]{2,1,0:T(8,128)(2,1)S(1)}, u32[]{:S(2)}, u32[]{:S(2)}) collective-permute-start(bf16[2,24,2432]{2,1,0:T(8,128)(2,1)S(1)} %maximum_select_fusion.2), channel_id=1, source_target_pairs={{0,16},{1,25},{2,18},{3,27},{4,20},{5,29},{6,22},{7,31},{8,24},{9,... | collective-permute-start | bytes 700424 | tf_op jit(solution)/shard_map/ppermute | solution.py:85
  14.7 10.6 %collective-permute-done.2 = bf16[2,24,2432]{2,1,0:T(8,128)(2,1)S(1)} collective-permute-done((bf16[2,24,2432]{2,1,0:T(8,128)(2,1)S(1)}, bf16[2,24,2432]{2,1,0:T(8,128)(2,1)S(1)}, u32[]{:S(2)}, u32[]{:S(2)}) %collective-permute-start.2) | collective-permute-done | bytes 233504 | tf_op jit(solution)/shard_map/ppermute | solution.py:85
  28.8 10.2 %collective-permute-done.4.refs_2_ = bf16[2,2,24,2432]{3,2,1,0:T(8,128)(2,1)S(1)} collective-permute-done((bf16[2,2,24,2432]{3,2,1,0:T(8,128)(2,1)S(1)}, bf16[2,2,24,2432]{3,2,1,0:T(8,128)(2,1)S(1)}, u32[]{:S(2)}, u32[]{:S(2)}) %collective-permute-start.4) | collective-permute-done | bytes 466976 | tf_op jit(solution)/shard_map/ppermute | solution.py:85
  40.9 3.0 collective-permute-start.29
  44.5 26.4 %collective-permute-done.29 = bf16[2,96,768]{2,1,0:T(8,128)(2,1)S(1)} collective-permute-done((bf16[2,96,768]{2,1,0:T(8,128)(2,1)S(1)}, bf16[2,96,768]{2,1,0:T(8,128)(2,1)S(1)}, u32[]{:S(2)}, u32[]{:S(2)}) %collective-permute-start.29) | collective-permute-done | bytes 294944 | tf_op jit(solution)/shard_map/ppermute | solution.py:85
  83.3 19.2 %collective-permute-done.31.refs_2_ = bf16[2,2,96,768]{3,2,1,0:T(8,128)(2,1)} collective-permute-done((bf16[2,2,96,768]{3,2,1,0:T(8,128)(2,1)S(1)}, bf16[2,2,96,768]{3,2,1,0:T(8,128)(2,1)}, u32[]{:S(2)}, u32[]{:S(2)}) %collective-permute-start.31) | collective-permute-done | bytes 589856 | tf_op jit(solution)/shard_map/ppermute | solution.py:85
  102.6 8.9 %collective-permute-done.10.refs_1_ = bf16[128,576]{1,0:T(8,128)(2,1)S(1)} collective-permute-done((bf16[128,576]{1,0:T(8,128)(2,1)S(1)}, bf16[128,576]{1,0:T(8,128)(2,1)S(1)}, u32[]{:S(2)}, u32[]{:S(2)}) %collective-permute-start.10) | collective-permute-done | bytes 147488 | tf_op jit(solution)/shard_map/ppermute | solution.py:85
  112.2 5.0 %collective-permute-done.11.refs_2_ = bf16[128,576]{1,0:T(8,128)(2,1)S(1)} collective-permute-done((bf16[128,576]{1,0:T(8,128)(2,1)S(1)}, bf16[128,576]{1,0:T(8,128)(2,1)S(1)}, u32[]{:S(2)}, u32[]{:S(2)}) %collective-permute-start.11) | collective-permute-done | bytes 147488 | tf_op jit(solution)/shard_map/ppermute | solution.py:85
  117.6 5.9 %collective-permute-done.12.refs_3_ = bf16[128,576]{1,0:T(8,128)(2,1)S(1)} collective-permute-done((bf16[128,576]{1,0:T(8,128)(2,1)S(1)}, bf16[128,576]{1,0:T(8,128)(2,1)S(1)}, u32[]{:S(2)}, u32[]{:S(2)}) %collective-permute-start.12) | collective-permute-done | bytes 147488 | tf_op jit(solution)/shard_map/ppermute | solution.py:85
  148.3 6.7 %shard_map.275 = (f32[512,192]{1,0:T(8,128)S(1)}, f32[512,3]{1,0:T(8,128)S(1)}, bf16[128,192]{1,0:T(8,128)(2,1)S(1)}, bf16[128,192]{1,0:T(8,128)(2,1)S(1)}, bf16...) custom-call(bf16[128,576]{1,0:T(8,128)(2,1)S(1)} %copy-done.9, bf16[128,576]{1,0:T(8,128)(2,1)S(1)} %copy-done.12, ...), custom_call_target="tpu_custom_call" | custom-call | tf_op jit(solution)/shard_map/pallas_call | solution.py:303
  160.0 4.5 %collective-permute-done.15.refs_2_ = bf16[128,192]{1,0:T(8,128)(2,1)S(1)} collective-permute-done((bf16[128,192]{1,0:T(8,128)(2,1)S(1)}, bf16[128,192]{1,0:T(8,128)(2,1)S(1)}, u32[]{:S(2)}, u32[]{:S(2)}) %collective-permute-start.15) | collective-permute-done | bytes 49184 | tf_op jit(solution)/shard_map/ppermute | solution.py:85
  187.5 7.1 %shard_map.280 = (bf16[512,192]{1,0:T(8,128)(2,1)S(1)}, f32[512,384]{1,0:T(8,128)S(1)}, bf16[512,384]{1,0:T(8,128)(2,1)S(1)}) custom-call(bf16[128,576]{1,0:T(8,128)(2,1)S(1)} %copy-done.10, bf16[128,576]{1,0:T(8,128)(2,1)S(1)} %copy-done.13, bf16[128,576]{1,0:T(8,128)(2,1)S(1)} %copy-done.16, bf16[128,576]{1,0:T(8,128)(2,1)S(1)} %copy-done.19, ...), custom_call_target="tpu_custom_call" | custom-call | tf_op jit(solution)/shard_map/pallas_call | solution.py:303
  195.8 6.7 %collective-permute-done.40.refs_2_ = bf16[512,384]{1,0:T(8,128)(2,1)S(1)} collective-permute-done((bf16[512,384]{1,0:T(8,128)(2,1)S(1)}, bf16[512,384]{1,0:T(8,128)(2,1)S(1)}, u32[]{:S(2)}, u32[]{:S(2)}) %collective-permute-start.40) | collective-permute-done | bytes 393248 | tf_op jit(solution)/shard_map/ppermute | solution.py:85
  202.7 3.5 %collective-permute-start.41 = (bf16[128,576]{1,0:T(8,128)(2,1)S(1)}, bf16[128,576]{1,0:T(8,128)(2,1)S(1)}, u32[]{:S(2)}, u32[]{:S(2)}) collective-permute-start(bf16[128,576]{1,0:T(8,128)(2,1)S(1)} %get-tuple-element.84), channel_id=1, source_target_pairs={{0,24},{1,25},{2,26},{3,27},{4,28},{5,29},{6,30},{7,31},{8,0},{9,1... | collective-permute-start | bytes 442376 | tf_op jit(solution)/shard_map/ppermute | solution.py:85
  207.1 3.2 %shard_map.294 = (bf16[2,4,96,768]{3,2,1,0:T(8,128)(2,1)S(1)}, bf16[2,4,96,768]{3,2,1,0:T(8,128)(2,1)S(1)}, bf16[2,4,96,768]{3,2,1,0:T(8,128)(2,1)S(1)}, bf16[2,4,96,768]{3,2,1,0:T(8,128)(2,1)S(1)}) custom-call(bf16[128,3072]{1,0:T(8,128)(2,1)S(1)} %get-tuple-element.152.refs_0_, bf16[128,768]{1,0:T(8,128)(2,1)S(1)} %get-tuple-element.143.refs_1_), custom_call_target="tpu_custom_call" | custom-call | tf_op jit(solution)/shard_map/pallas_call | solution.py:250
  210.4 5.3 %collective-permute-done.42.refs_2_ = bf16[128,576]{1,0:T(8,128)(2,1)S(1)} collective-permute-done((bf16[128,576]{1,0:T(8,128)(2,1)S(1)}, bf16[128,576]{1,0:T(8,128)(2,1)S(1)}, u32[]{:S(2)}, u32[]{:S(2)}) %collective-permute-start.42) | collective-permute-done | bytes 147488 | tf_op jit(solution)/shard_map/ppermute | solution.py:85
  217.4 2.9 shard_map.284
  220.3 3.6 %shard_map.289 = (bf16[2,4,24,3840]{3,2,1,0:T(8,128)(2,1)S(1)}, bf16[2,4,24,3840]{3,2,1,0:T(8,128)(2,1)S(1)}, bf16[2,4,24,3840]{3,2,1,0:T(8,128)(2,1)S(1)}, bf16[2,4,24,3840]{3,2,1,0:T(8,128)(2,1)S(1)}) custom-call(bf16[128,768]{1,0:T(8,128)(2,1)S(1)} %get-tuple-element.70.refs_0_, bf16[128,768]{1,0:T(8,128)(2,1)S(1)} %add_convert_fusion.refs_1_, ...), custom_call_target="tpu_custom_call" | custom-call | tf_op jit(solution)/shard_map/pallas_call | solution.py:250
  229.8 8.6 %collective-permute-done.46.refs_2_ = bf16[2,4,24,2432]{3,2,1,0:T(8,128)(2,1)S(1)} collective-permute-done((bf16[2,4,24,2432]{3,2,1,0:T(8,128)(2,1)S(1)}, bf16[2,4,24,2432]{3,2,1,0:T(8,128)(2,1)S(1)}, u32[]{:S(2)}, u32[]{:S(2)}) %collective-permute-start.46) | collective-permute-done | bytes 933920 | tf_op jit(solution)/shard_map/ppermute | solution.py:85
  241.0 15.1 %collective-permute-done.60.refs_2_ = bf16[2,4,96,768]{3,2,1,0:T(8,128)(2,1)S(1)} collective-permute-done((bf16[2,4,96,768]{3,2,1,0:T(8,128)(2,1)S(1)}, bf16[2,4,96,768]{3,2,1,0:T(8,128)(2,1)S(1)}, u32[]{:S(2)}, u32[]{:S(2)}) %collective-permute-start.60) | collective-permute-done | bytes 1179680 | tf_op jit(solution)/shard_map/ppermute | solution.py:85
  261.0 11.7 %collective-permute-done.61.refs_3_ = bf16[1,4,96,768]{3,2,1,0:T(8,128)(2,1)S(1)} collective-permute-done((bf16[1,4,96,768]{3,2,1,0:T(8,128)(2,1)S(1)}, bf16[1,4,96,768]{3,2,1,0:T(8,128)(2,1)S(1)}, u32[]{:S(2)}, u32[]{:S(2)}) %collective-permute-start.61) | collective-permute-done | bytes 589856 | tf_op jit(solution)/shard_map/ppermute | solution.py:85
  279.6 7.3 %collective-permute-done.63 = bf16[2,96,768]{2,1,0:T(8,128)(2,1)S(1)} collective-permute-done((bf16[2,96,768]{2,1,0:T(8,128)(2,1)S(1)}, bf16[2,96,768]{2,1,0:T(8,128)(2,1)S(1)}, u32[]{:S(2)}, u32[]{:S(2)}) %collective-permute-start.63) | collective-permute-done | bytes 294944 | tf_op jit(solution)/shard_map/ppermute | solution.py:85
  287.1 3.0 collective-permute-done.54.refs_3_
  295.3 12.2 %collective-permute-done.56 = bf16[2,24,3840]{2,1,0:T(8,128)(2,1)S(1)} collective-permute-done((bf16[2,24,3840]{2,1,0:T(8,128)(2,1)S(1)}, bf16[2,24,3840]{2,1,0:T(8,128)(2,1)S(1)}, u32[]{:S(2)}, u32[]{:S(2)}) %collective-permute-start.56) | collective-permute-done | bytes 368672 | tf_op jit(solution)/shard_map/ppermute | solution.py:85
  (318 shorter events, 114.5 us)
Async XLA Ops:
  8.4 32.4 %collective-permute-start.27 = (bf16[96,768]{1,0:T(8,128)(2,1)}, bf16[96,768]{1,0:T(8,128)(2,1)S(1)}, u32[]{:S(2)}, u32[]{:S(2)}) collective-permute-start(bf16[96,768]{1,0:T(8,128)(2,1)} %bitcast.169), channel_id=1, source_target_pairs={{0,1},{1,0},{2,3},{3,2},{4,5},{5,4},{6,7},{7,6},{8,9},{9,8},{10,11... | collective-permute-start | bytes 442376 | tf_op jit(solution)/shard_map/ppermute | solution.py:85
  9.5 30.5 %collective-permute-start.17 = (bf16[24,3840]{1,0:T(8,128)(2,1)S(1)}, bf16[24,3840]{1,0:T(8,128)(2,1)S(1)}, u32[]{:S(2)}, u32[]{:S(2)}) collective-permute-start(bf16[24,3840]{1,0:T(8,128)(2,1)S(1)} %get-tuple-element.147), channel_id=1, source_target_pairs={{0,1},{1,0},{2,3},{3,2},{4,5},{5,4},{6,7},{7,6},{8,9},{9,8},{10,11... | collective-permute-start | bytes 552968 | tf_op jit(solution)/shard_map/ppermute | solution.py:85
  27.2 45.0 %collective-permute-start.3 = (bf16[2,2,24,2432]{3,2,1,0:T(8,128)(2,1)S(1)}, bf16[2,2,24,2432]{3,2,1,0:T(8,128)(2,1)S(1)}, u32[]{:S(2)}, u32[]{:S(2)}) collective-permute-start(bf16[2,2,24,2432]{3,2,1,0:T(8,128)(2,1)S(1)} %pad_maximum_fusion.2.refs_0_), channel_id=1, source_target_pairs={{0,2},{1,5},{2,0},{3,7},{4,6},{5,1},{6,4},{7,3},{8,10},{9,13},{10,... | collective-permute-start | bytes 1400840 | tf_op jit(solution)/shard_map/ppermute | solution.py:85
  39.0 33.2 %collective-permute-start.5 = (bf16[2,2,24,2432]{3,2,1,0:T(8,128)(2,1)S(1)}, bf16[2,2,24,2432]{3,2,1,0:T(8,128)(2,1)S(1)}, u32[]{:S(2)}, u32[]{:S(2)}) collective-permute-start(bf16[2,2,24,2432]{3,2,1,0:T(8,128)(2,1)S(1)} %collective-permute-done.4.refs_2_), channel_id=1, source_target_pairs={{0,2},{1,5},{2,0},{3,7},{4,6},{5,1},{6,4},{7,3},{8,10},{9,13},{10,... | collective-permute-start | bytes 1400840 | tf_op jit(solution)/shard_map/ppermute | solution.py:85
  40.1 31.5 %collective-permute-start.19 = (bf16[2,24,3840]{2,1,0:T(8,128)(2,1)S(1)}, bf16[2,24,3840]{2,1,0:T(8,128)(2,1)S(1)}, u32[]{:S(2)}, u32[]{:S(2)}) collective-permute-start(bf16[2,24,3840]{2,1,0:T(8,128)(2,1)S(1)} %maximum_select_fusion), channel_id=1, source_target_pairs={{0,16},{1,25},{2,18},{3,27},{4,20},{5,29},{6,22},{7,31},{8,24},{9,... | collective-permute-start | bytes 1105928 | tf_op jit(solution)/shard_map/ppermute | solution.py:85
  40.1 31.5 %collective-permute-start.18 = (bf16[2,24,3840]{2,1,0:T(8,128)(2,1)S(1)}, bf16[2,24,3840]{2,1,0:T(8,128)(2,1)S(1)}, u32[]{:S(2)}, u32[]{:S(2)}) collective-permute-start(bf16[2,24,3840]{2,1,0:T(8,128)(2,1)S(1)} %maximum_select_fusion), channel_id=1, source_target_pairs={{0,0},{1,9},{2,2},{3,11},{4,4},{5,13},{6,6},{7,15},{8,8},{9,17},{1... | collective-permute-start | bytes 1105928 | tf_op jit(solution)/shard_map/ppermute | solution.py:85
  40.9 30.0 %collective-permute-start.29 = (bf16[2,96,768]{2,1,0:T(8,128)(2,1)S(1)}, bf16[2,96,768]{2,1,0:T(8,128)(2,1)S(1)}, u32[]{:S(2)}, u32[]{:S(2)}) collective-permute-start(bf16[2,96,768]{2,1,0:T(8,128)(2,1)S(1)} %maximum_select_fusion.1), channel_id=1, source_target_pairs={{0,16},{1,25},{2,18},{3,27},{4,20},{5,29},{6,22},{7,31},{8,24},{9,... | collective-permute-start | bytes 884744 | tf_op jit(solution)/shard_map/ppermute | solution.py:85
  72.7 29.8 %collective-permute-start.21 = (bf16[2,2,24,3840]{3,2,1,0:T(8,128)(2,1)S(1)}, bf16[2,2,24,3840]{3,2,1,0:T(8,128)(2,1)}, u32[]{:S(2)}, u32[]{:S(2)}) collective-permute-start(bf16[2,2,24,3840]{3,2,1,0:T(8,128)(2,1)S(1)} %pad_maximum_fusion.refs_0_), channel_id=1, source_target_pairs={{0,4},{1,3},{2,6},{3,1},{4,0},{5,7},{6,2},{7,5},{8,12},{9,11},{10,... | collective-permute-start | bytes 2211848 | tf_op jit(solution)/shard_map/ppermute | solution.py:85
  74.2 28.3 %collective-permute-start.31 = (bf16[2,2,96,768]{3,2,1,0:T(8,128)(2,1)S(1)}, bf16[2,2,96,768]{3,2,1,0:T(8,128)(2,1)}, u32[]{:S(2)}, u32[]{:S(2)}) collective-permute-start(bf16[2,2,96,768]{3,2,1,0:T(8,128)(2,1)S(1)} %pad_maximum_fusion.1.refs_0_), channel_id=1, source_target_pairs={{0,4},{1,3},{2,6},{3,1},{4,0},{5,7},{6,2},{7,5},{8,12},{9,11},{10,... | collective-permute-start | bytes 1769480 | tf_op jit(solution)/shard_map/ppermute | solution.py:85
  75.0 48.6 %collective-permute-start.33 = (bf16[2,2,96,768]{3,2,1,0:T(8,128)(2,1)S(1)}, bf16[2,2,96,768]{3,2,1,0:T(8,128)(2,1)S(1)}, u32[]{:S(2)}, u32[]{:S(2)}) collective-permute-start(bf16[2,2,96,768]{3,2,1,0:T(8,128)(2,1)S(1)} %pad_maximum_fusion.1.refs_0_), channel_id=1, source_target_pairs={{0,1},{1,0},{2,3},{3,2},{4,5},{5,4},{6,7},{7,6},{8,9},{9,8},{10,11... | collective-permute-start | bytes 1769480 | tf_op jit(solution)/shard_map/ppermute | solution.py:85
  76.0 48.4 %collective-permute-start.30 = (bf16[2,2,96,768]{3,2,1,0:T(8,128)(2,1)S(1)}, bf16[2,2,96,768]{3,2,1,0:T(8,128)(2,1)}, u32[]{:S(2)}, u32[]{:S(2)}) collective-permute-start(bf16[2,2,96,768]{3,2,1,0:T(8,128)(2,1)S(1)} %pad_maximum_fusion.1.refs_0_), channel_id=1, source_target_pairs={{0,2},{1,5},{2,0},{3,7},{4,6},{5,1},{6,4},{7,3},{8,10},{9,13},{10,... | collective-permute-start | bytes 1769480 | tf_op jit(solution)/shard_map/ppermute | solution.py:85
  77.2 48.7 %collective-permute-start.20 = (bf16[2,2,24,3840]{3,2,1,0:T(8,128)(2,1)S(1)}, bf16[2,2,24,3840]{3,2,1,0:T(8,128)(2,1)S(1)}, u32[]{:S(2)}, u32[]{:S(2)}) collective-permute-start(bf16[2,2,24,3840]{3,2,1,0:T(8,128)(2,1)S(1)} %pad_maximum_fusion.refs_0_), channel_id=1, source_target_pairs={{0,2},{1,5},{2,0},{3,7},{4,6},{5,1},{6,4},{7,3},{8,10},{9,13},{10,... | collective-permute-start | bytes 2211848 | tf_op jit(solution)/shard_map/ppermute | solution.py:85
  111.5 24.8 %collective-permute-start.22 = (bf16[2,2,24,3840]{3,2,1,0:T(8,128)(2,1)}, bf16[2,2,24,3840]{3,2,1,0:T(8,128)(2,1)}, u32[]{:S(2)}, u32[]{:S(2)}) collective-permute-start(bf16[2,2,24,3840]{3,2,1,0:T(8,128)(2,1)} %collective-permute-done.21.refs_2_), channel_id=1, source_target_pairs={{0,2},{1,5},{2,0},{3,7},{4,6},{5,1},{6,4},{7,3},{8,10},{9,13},{10,... | collective-permute-start | bytes 2211848 | tf_op jit(solution)/shard_map/ppermute | solution.py:85
  130.8 41.0 %collective-permute-start.23 = (bf16[2,2,24,3840]{3,2,1,0:T(8,128)(2,1)}, bf16[2,2,24,3840]{3,2,1,0:T(8,128)(2,1)S(1)}, u32[]{:S(2)}, u32[]{:S(2)}) collective-permute-start(bf16[2,2,24,3840]{3,2,1,0:T(8,128)(2,1)} %copy-done), channel_id=1, source_target_pairs={{0,1},{1,0},{2,3},{3,2},{4,5},{5,4},{6,7},{7,6},{8,9},{9,8},{10,11... | collective-permute-start | bytes 2211848 | tf_op jit(solution)/shard_map/ppermute | solution.py:85
  133.9 37.9 %collective-permute-start.25 = (bf16[2,2,24,3840]{3,2,1,0:T(8,128)(2,1)}, bf16[2,2,24,3840]{3,2,1,0:T(8,128)(2,1)S(1)}, u32[]{:S(2)}, u32[]{:S(2)}) collective-permute-start(bf16[2,2,24,3840]{3,2,1,0:T(8,128)(2,1)} %collective-permute-done.21.refs_2_), channel_id=1, source_target_pairs={{0,1},{1,0},{2,3},{3,2},{4,5},{5,4},{6,7},{7,6},{8,9},{9,8},{10,11... | collective-permute-start | bytes 2211848 | tf_op jit(solution)/shard_map/ppermute | solution.py:85
  136.3 35.5 %collective-permute-start.24 = (bf16[2,2,24,3840]{3,2,1,0:T(8,128)(2,1)}, bf16[2,2,24,3840]{3,2,1,0:T(8,128)(2,1)S(1)}, u32[]{:S(2)}, u32[]{:S(2)}) collective-permute-start(bf16[2,2,24,3840]{3,2,1,0:T(8,128)(2,1)} %copy-done.20), channel_id=1, source_target_pairs={{0,1},{1,0},{2,3},{3,2},{4,5},{5,4},{6,7},{7,6},{8,9},{9,8},{10,11... | collective-permute-start | bytes 2211848 | tf_op jit(solution)/shard_map/ppermute | solution.py:85
  136.3 18.7 %collective-permute-start.36 = (bf16[2,2,96,768]{3,2,1,0:T(8,128)(2,1)}, bf16[2,2,96,768]{3,2,1,0:T(8,128)(2,1)S(1)}, u32[]{:S(2)}, u32[]{:S(2)}) collective-permute-start(bf16[2,2,96,768]{3,2,1,0:T(8,128)(2,1)} %collective-permute-done.32.refs_3_), channel_id=1, source_target_pairs={{0,1},{1,0},{2,3},{3,2},{4,5},{5,4},{6,7},{7,6},{8,9},{9,8},{10,11... | collective-permute-start | bytes 1769480 | tf_op jit(solution)/shard_map/ppermute | solution.py:85
  139.1 32.7 %collective-permute-start.26 = (bf16[2,2,24,3840]{3,2,1,0:T(8,128)(2,1)}, bf16[2,2,24,3840]{3,2,1,0:T(8,128)(2,1)S(1)}, u32[]{:S(2)}, u32[]{:S(2)}) collective-permute-start(bf16[2,2,24,3840]{3,2,1,0:T(8,128)(2,1)} %collective-permute-done.22.refs_3_), channel_id=1, source_target_pairs={{0,1},{1,0},{2,3},{3,2},{4,5},{5,4},{6,7},{7,6},{8,9},{9,8},{10,11... | collective-permute-start | bytes 2211848 | tf_op jit(solution)/shard_map/ppermute | solution.py:85
  226.3 29.8 %collective-permute-start.60 = (bf16[2,4,96,768]{3,2,1,0:T(8,128)(2,1)S(1)}, bf16[2,4,96,768]{3,2,1,0:T(8,128)(2,1)S(1)}, u32[]{:S(2)}, u32[]{:S(2)}) collective-permute-start(bf16[2,4,96,768]{3,2,1,0:T(8,128)(2,1)S(1)} %shard_map.295), channel_id=1, source_target_pairs={{0,4},{1,3},{2,6},{3,1},{4,0},{5,7},{6,2},{7,5},{8,12},{9,11},{10,... | collective-permute-start | bytes 3538952 | tf_op jit(solution)/shard_map/ppermute | solution.py:85
  228.0 46.8 %collective-permute-start.51 = (bf16[2,4,24,3840]{3,2,1,0:T(8,128)(2,1)S(1)}, bf16[2,4,24,3840]{3,2,1,0:T(8,128)(2,1)S(1)}, u32[]{:S(2)}, u32[]{:S(2)}) collective-permute-start(bf16[2,4,24,3840]{3,2,1,0:T(8,128)(2,1)S(1)} %get-tuple-element.94), channel_id=1, source_target_pairs={{0,1},{1,0},{2,3},{3,2},{4,5},{5,4},{6,7},{7,6},{8,9},{9,8},{10,11... | collective-permute-start | bytes 4423688 | tf_op jit(solution)/shard_map/ppermute | solution.py:85
  228.7 49.5 %collective-permute-start.53 = (bf16[2,4,24,3840]{3,2,1,0:T(8,128)(2,1)S(1)}, bf16[2,4,24,3840]{3,2,1,0:T(8,128)(2,1)S(1)}, u32[]{:S(2)}, u32[]{:S(2)}) collective-permute-start(bf16[2,4,24,3840]{3,2,1,0:T(8,128)(2,1)S(1)} %shard_map.290), channel_id=1, source_target_pairs={{0,4},{1,3},{2,6},{3,1},{4,0},{5,7},{6,2},{7,5},{8,12},{9,11},{10,... | collective-permute-start | bytes 4423688 | tf_op jit(solution)/shard_map/ppermute | solution.py:85
  257.4 22.0 %collective-permute-start.49 = (bf16[2,24,2432]{2,1,0:T(8,128)(2,1)S(1)}, bf16[2,24,2432]{2,1,0:T(8,128)(2,1)S(1)}, u32[]{:S(2)}, u32[]{:S(2)}) collective-permute-start(bf16[2,24,2432]{2,1,0:T(8,128)(2,1)S(1)} %bitcast.153), channel_id=1, source_target_pairs={{0,16},{1,25},{2,18},{3,27},{4,20},{5,29},{6,22},{7,31},{8,24},{9,... | collective-permute-start | bytes 700424 | tf_op jit(solution)/shard_map/ppermute | solution.py:85
  259.4 20.0 %collective-permute-start.48 = (bf16[2,24,2432]{2,1,0:T(8,128)(2,1)S(1)}, bf16[2,24,2432]{2,1,0:T(8,128)(2,1)S(1)}, u32[]{:S(2)}, u32[]{:S(2)}) collective-permute-start(bf16[2,24,2432]{2,1,0:T(8,128)(2,1)S(1)} %bitcast.154), channel_id=1, source_target_pairs={{0,0},{1,9},{2,2},{3,11},{4,4},{5,13},{6,6},{7,15},{8,8},{9,17},{1... | collective-permute-start | bytes 700424 | tf_op jit(solution)/shard_map/ppermute | solution.py:85
  287.0 20.7 %collective-permute-start.64 = (bf16[96,768]{1,0:T(8,128)(2,1)S(1)}, bf16[96,768]{1,0:T(8,128)(2,1)S(1)}, u32[]{:S(2)}, u32[]{:S(2)}) collective-permute-start(bf16[96,768]{1,0:T(8,128)(2,1)S(1)} %fusion.41), channel_id=1, source_target_pairs={{0,1},{1,0},{2,3},{3,2},{4,5},{5,4},{6,7},{7,6},{8,9},{9,8},{10,11... | collective-permute-start | bytes 442376 | tf_op jit(solution)/shard_map/ppermute | solution.py:85
  (95 other events, 863.2 us)

commit v4 on v3

--- a/solution.py
+++ b/solution.py
@@ -485,18 +485,29 @@
 
 def pack_first(w_qkv, lines, spare, rows):
     width = w_qkv.shape[1]
-    used = len(lines) + spare.shape[1] // rows
+    count = lines.shape[0]
+    used = count + spare.shape[1] // rows
 
     def kernel(*refs):
         out = refs[-1]
         out[:, :width] = refs[0][...]
-        items = [ref[...] for ref in refs[2:-1]]
-        items += [refs[1][:, at * rows : (at + 1) * rows] for at in range(used - len(lines))]
+        items = [refs[2][...]]
+        items += [refs[1][:, at * rows : (at + 1) * rows] for at in range(used - count)]
         stacked = jnp.concatenate([item.astype(F32) for item in items] + [jnp.zeros((EXT - used, rows), F32)], axis=0)
         across = lax.broadcasted_iota(jnp.int32, (rows, rows), 0) == lax.broadcasted_iota(jnp.int32, (rows, rows), 1)
         out[:, width:] = product(across.astype(BF), stacked.astype(BF), ((1,), (1,))).astype(BF)
 
-    return simple(kernel, [w_qkv, spare, *lines], [((rows, width + EXT), BF)], fetch=len(lines) + 2)[0]
+    return simple(kernel, [w_qkv, spare, lines], [((rows, width + EXT), BF)])[0]
+
+
+def pack_keys(pieces):
+    step, group = pieces[0].shape[0], pieces[0].shape[1] // 3
+
+    def kernel(*refs):
+        for at, ref in enumerate(refs[:-1]):
+            refs[-1][at * step : (at + 1) * step, :] = ref[:, group:]
+
+    return simple(kernel, pieces, [((len(pieces) * step, 2 * group), BF)], fetch=len(pieces))[0]
 
 
 def local_step(
@@ -523,13 +534,12 @@
     order = block_order[0]
     Z, X = grid.z, grid.x
     z, x, _, _ = grid.here()
-    group = D // Z
     heads = HEADS // Z
 
     rows = w_qkv.shape[1]
     small = [attn_gain, attn_shift, query_bias, value_bias, out_bias, mlp_gain, mlp_shift, proj_bias]
     used = 8 + fc_bias.shape[1] // rows
-    first_z = gather_z(grid, pack_first(w_qkv[0], small, fc_bias, rows))
+    first_z = gather_z(grid, pack_first(w_qkv[0], jnp.concatenate(small), fc_bias, rows))
     mid_z = gather_z(grid, jnp.concatenate([w_out[0], w_fc[0]], axis=1))
     last_z = gather_z(grid, w_proj[0])
     w_joint, extra = gather(grid, first_z, [3 * D, EXT])
@@ -555,7 +565,7 @@
     first = normed_in.astype(BF)
     joint = jnp.dot(first, w_joint, preferred_element_type=F32)
     packed = spread(split_groups(grid, joint, joint_bias, 3))
-    own_keys = jnp.concatenate([piece[:, group:] for piece in packed])
+    own_keys = pack_keys(packed)
     all_keys = [own_keys] + [grid.along_x(own_keys, dx) for dx in range(1, X)]
     mixed_local, log_total, mixed_send = attend(packed, all_keys, query_pos, key_pos, heads)
     (w_down,) = gather(grid, last_z, [D])

time: 311 us -> 285 us (0.916)
  waiting for transfers between devices: 177 us -> 151 us
    ppermute x65, waiting for transfers between devices: 177 us -> 151 us  [send(): return lax.ppermute(value, AXES, pairs)]
    unnamed x108, local copies, waits for them, and re-layouts: 14.5 us -> 11 us
    pallas_call x10 -> x11, Pallas kernels: 16.3 us -> 17.9 us  [simple(): pl.pallas_call(fetched if fetch else kernel, in_specs=[pl.BlockSpec(memor...]
  transfers between devices with their start and end apart: 65 -> 65, of which waited for: 25 -> 25; matrix products, arithmetic and copies ran while one was open for 5% -> 6% of each run, Pallas kernels for 8% -> 9%
where the time goes in v4:
time: 285 us; the launch traced here: 284 us
  waiting for transfers between devices  151 us (53%)
  starting transfers between devices  57.9 us (20%)
  Pallas kernels  35.6 us (12%)
  local copies, waits for them, and re-layouts  17.7 us (6%)
  other arithmetic  10.3 us (4%)
  matrix products  9.45 us (3%)
    ppermute x65, waiting for transfers between devices, send(): return lax.ppermute(value, AXES, pairs)  151 us
    ppermute x65, starting transfers between devices, send(): return lax.ppermute(value, AXES, pairs)  57.9 us
    pallas_call x11, Pallas kernels, simple(): pl.pallas_call(fetched if fetch else kernel, in_specs=[pl.BlockSpec(memor...  17.9 us
    unnamed x108, local copies, waits for them, and re-layouts  11 us
    pallas_call x3, Pallas kernels, scatter(): pl.pallas_call(kernel, in_specs=[vmem] * inputs, out_specs=[vmem] * (2 *...  9.64 us
  transfers between devices with their start and end apart: 65, of which 25 were waited for; matrix products, arithmetic and copies ran while one was open for 6% of the time, Pallas kernels for 9%

profile of v4, /device:TPU:0, one launch (start us, length us, event | category | flops | bytes accessed | tf_op | source)
XLA Modules:
  0.0 284.0 jit_solution(9247369486662744240)
XLA Ops:
  6.4 3.6 %collective-permute-start.2 = (bf16[2,24,2432]{2,1,0:T(8,128)(2,1)S(1)}, bf16[2,24,2432]{2,1,0:T(8,128)(2,1)S(1)}, u32[]{:S(2)}, u32[]{:S(2)}) collective-permute-start(bf16[2,24,2432]{2,1,0:T(8,128)(2,1)S(1)} %maximum_select_fusion.2), channel_id=1, source_target_pairs={{0,16},{1,25},{2,18},{3,27},{4,20},{5,29},{6,22},{7,31},{8,24},{9,... | collective-permute-start | bytes 700424 | tf_op jit(solution)/shard_map/ppermute | solution.py:85
  10.8 10.8 %collective-permute-done.2 = bf16[2,24,2432]{2,1,0:T(8,128)(2,1)S(1)} collective-permute-done((bf16[2,24,2432]{2,1,0:T(8,128)(2,1)S(1)}, bf16[2,24,2432]{2,1,0:T(8,128)(2,1)S(1)}, u32[]{:S(2)}, u32[]{:S(2)}) %collective-permute-start.2) | collective-permute-done | bytes 233504 | tf_op jit(solution)/shard_map/ppermute | solution.py:85
  26.5 5.3 %collective-permute-done.4.refs_2_ = bf16[2,2,24,2432]{3,2,1,0:T(8,128)(2,1)S(1)} collective-permute-done((bf16[2,2,24,2432]{3,2,1,0:T(8,128)(2,1)S(1)}, bf16[2,2,24,2432]{3,2,1,0:T(8,128)(2,1)S(1)}, u32[]{:S(2)}, u32[]{:S(2)}) %collective-permute-start.4) | collective-permute-done | bytes 466976 | tf_op jit(solution)/shard_map/ppermute | solution.py:85
  34.4 6.6 %collective-permute-done.29 = bf16[2,96,768]{2,1,0:T(8,128)(2,1)} collective-permute-done((bf16[2,96,768]{2,1,0:T(8,128)(2,1)S(1)}, bf16[2,96,768]{2,1,0:T(8,128)(2,1)}, u32[]{:S(2)}, u32[]{:S(2)}) %collective-permute-start.29) | collective-permute-done | bytes 294944 | tf_op jit(solution)/shard_map/ppermute | solution.py:85
  43.5 11.9 %collective-permute-done.19 = bf16[2,24,3840]{2,1,0:T(8,128)(2,1)S(1)} collective-permute-done((bf16[2,24,3840]{2,1,0:T(8,128)(2,1)S(1)}, bf16[2,24,3840]{2,1,0:T(8,128)(2,1)S(1)}, u32[]{:S(2)}, u32[]{:S(2)}) %collective-permute-start.19) | collective-permute-done | bytes 368672 | tf_op jit(solution)/shard_map/ppermute | solution.py:85
  68.9 4.8 %collective-permute-done.31.refs_2_ = bf16[2,2,96,768]{3,2,1,0:T(8,128)(2,1)} collective-permute-done((bf16[2,2,96,768]{3,2,1,0:T(8,128)(2,1)S(1)}, bf16[2,2,96,768]{3,2,1,0:T(8,128)(2,1)}, u32[]{:S(2)}, u32[]{:S(2)}) %collective-permute-start.31) | collective-permute-done | bytes 589856 | tf_op jit(solution)/shard_map/ppermute | solution.py:85
  76.2 13.2 %collective-permute-done.21.refs_2_ = bf16[2,2,24,3840]{3,2,1,0:T(8,128)(2,1)} collective-permute-done((bf16[2,2,24,3840]{3,2,1,0:T(8,128)(2,1)S(1)}, bf16[2,2,24,3840]{3,2,1,0:T(8,128)(2,1)}, u32[]{:S(2)}, u32[]{:S(2)}) %collective-permute-start.21) | collective-permute-done | bytes 737312 | tf_op jit(solution)/shard_map/ppermute | solution.py:85
  100.9 6.6 %collective-permute-done.22.refs_3_ = bf16[2,2,24,3840]{3,2,1,0:T(8,128)(2,1)} collective-permute-done((bf16[2,2,24,3840]{3,2,1,0:T(8,128)(2,1)}, bf16[2,2,24,3840]{3,2,1,0:T(8,128)(2,1)}, u32[]{:S(2)}, u32[]{:S(2)}) %collective-permute-start.22) | collective-permute-done | bytes 737312 | tf_op jit(solution)/shard_map/ppermute | solution.py:85
  107.5 3.5 %collective-permute-start.36 = (bf16[2,2,96,768]{3,2,1,0:T(8,128)(2,1)}, bf16[2,2,96,768]{3,2,1,0:T(8,128)(2,1)S(1)}, u32[]{:S(2)}, u32[]{:S(2)}) collective-permute-start(bf16[2,2,96,768]{3,2,1,0:T(8,128)(2,1)} %collective-permute-done.32.refs_3_), channel_id=1, source_target_pairs={{0,1},{1,0},{2,3},{3,2},{4,5},{5,4},{6,7},{7,6},{8,9},{9,8},{10,11... | collective-permute-start | bytes 1769480 | tf_op jit(solution)/shard_map/ppermute | solution.py:85
  111.0 4.2 %collective-permute-start.26 = (bf16[2,2,24,3840]{3,2,1,0:T(8,128)(2,1)}, bf16[2,2,24,3840]{3,2,1,0:T(8,128)(2,1)S(1)}, u32[]{:S(2)}, u32[]{:S(2)}) collective-permute-start(bf16[2,2,24,3840]{3,2,1,0:T(8,128)(2,1)} %collective-permute-done.22.refs_3_), channel_id=1, source_target_pairs={{0,1},{1,0},{2,3},{3,2},{4,5},{5,4},{6,7},{7,6},{8,9},{9,8},{10,11... | collective-permute-start | bytes 2211848 | tf_op jit(solution)/shard_map/ppermute | solution.py:85
  121.9 6.7 %shard_map.276 = (f32[512,192]{1,0:T(8,128)S(1)}, f32[512,3]{1,0:T(8,128)S(1)}, bf16[128,192]{1,0:T(8,128)(2,1)S(1)}, bf16[128,192]{1,0:T(8,128)(2,1)S(1)}, bf16...) custom-call(bf16[128,576]{1,0:T(8,128)(2,1)S(1)} %copy-done.9, bf16[128,576]{1,0:T(8,128)(2,1)S(1)} %copy-done.12, ...), custom_call_target="tpu_custom_call" | custom-call | tf_op jit(solution)/shard_map/pallas_call | solution.py:303
  129.7 3.2 %collective-permute-done.14.refs_1_ = bf16[128,192]{1,0:T(8,128)(2,1)S(1)} collective-permute-done((bf16[128,192]{1,0:T(8,128)(2,1)S(1)}, bf16[128,192]{1,0:T(8,128)(2,1)S(1)}, u32[]{:S(2)}, u32[]{:S(2)}) %collective-permute-start.14) | collective-permute-done | bytes 49184 | tf_op jit(solution)/shard_map/ppermute | solution.py:85
  132.9 5.8 %collective-permute-done.15.refs_2_ = bf16[128,192]{1,0:T(8,128)(2,1)S(1)} collective-permute-done((bf16[128,192]{1,0:T(8,128)(2,1)S(1)}, bf16[128,192]{1,0:T(8,128)(2,1)S(1)}, u32[]{:S(2)}, u32[]{:S(2)}) %collective-permute-start.15) | collective-permute-done | bytes 49184 | tf_op jit(solution)/shard_map/ppermute | solution.py:85
  141.0 3.8 %collective-permute-done.16.refs_3_ = bf16[128,192]{1,0:T(8,128)(2,1)S(1)} collective-permute-done((bf16[128,192]{1,0:T(8,128)(2,1)S(1)}, bf16[128,192]{1,0:T(8,128)(2,1)S(1)}, u32[]{:S(2)}, u32[]{:S(2)}) %collective-permute-start.16) | collective-permute-done | bytes 49184 | tf_op jit(solution)/shard_map/ppermute | solution.py:85
  161.3 7.1 %shard_map.281 = (bf16[512,192]{1,0:T(8,128)(2,1)S(1)}, f32[512,384]{1,0:T(8,128)S(1)}, bf16[512,384]{1,0:T(8,128)(2,1)S(1)}) custom-call(bf16[128,576]{1,0:T(8,128)(2,1)S(1)} %copy-done.10, bf16[128,576]{1,0:T(8,128)(2,1)S(1)} %copy-done.13, bf16[128,576]{1,0:T(8,128)(2,1)S(1)} %copy-done.16, bf16[128,576]{1,0:T(8,128)(2,1)S(1)} %copy-done.19, ...), custom_call_target="tpu_custom_call" | custom-call | tf_op jit(solution)/shard_map/pallas_call | solution.py:303
  169.9 6.3 %collective-permute-done.40.refs_2_ = bf16[512,384]{1,0:T(8,128)(2,1)S(1)} collective-permute-done((bf16[512,384]{1,0:T(8,128)(2,1)S(1)}, bf16[512,384]{1,0:T(8,128)(2,1)S(1)}, u32[]{:S(2)}, u32[]{:S(2)}) %collective-permute-start.40) | collective-permute-done | bytes 393248 | tf_op jit(solution)/shard_map/ppermute | solution.py:85
  176.5 3.4 %collective-permute-start.41 = (bf16[128,576]{1,0:T(8,128)(2,1)S(1)}, bf16[128,576]{1,0:T(8,128)(2,1)S(1)}, u32[]{:S(2)}, u32[]{:S(2)}) collective-permute-start(bf16[128,576]{1,0:T(8,128)(2,1)S(1)} %get-tuple-element.84), channel_id=1, source_target_pairs={{0,24},{1,25},{2,26},{3,27},{4,28},{5,29},{6,30},{7,31},{8,0},{9,1... | collective-permute-start | bytes 442376 | tf_op jit(solution)/shard_map/ppermute | solution.py:85
  184.1 5.1 %collective-permute-done.42.refs_2_ = bf16[128,576]{1,0:T(8,128)(2,1)S(1)} collective-permute-done((bf16[128,576]{1,0:T(8,128)(2,1)S(1)}, bf16[128,576]{1,0:T(8,128)(2,1)S(1)}, u32[]{:S(2)}, u32[]{:S(2)}) %collective-permute-start.42) | collective-permute-done | bytes 147488 | tf_op jit(solution)/shard_map/ppermute | solution.py:85
  193.8 3.6 %shard_map.290 = (bf16[2,4,24,3840]{3,2,1,0:T(8,128)(2,1)S(1)}, bf16[2,4,24,3840]{3,2,1,0:T(8,128)(2,1)S(1)}, bf16[2,4,24,3840]{3,2,1,0:T(8,128)(2,1)S(1)}, bf16[2,4,24,3840]{3,2,1,0:T(8,128)(2,1)S(1)}) custom-call(bf16[128,768]{1,0:T(8,128)(2,1)S(1)} %get-tuple-element.70.refs_0_, bf16[128,768]{1,0:T(8,128)(2,1)S(1)} %add_convert_fusion.refs_1_, ...), custom_call_target="tpu_custom_call" | custom-call | tf_op jit(solution)/shard_map/pallas_call | solution.py:250
  203.9 8.1 %collective-permute-done.46.refs_2_ = bf16[2,4,24,2432]{3,2,1,0:T(8,128)(2,1)S(1)} collective-permute-done((bf16[2,4,24,2432]{3,2,1,0:T(8,128)(2,1)S(1)}, bf16[2,4,24,2432]{3,2,1,0:T(8,128)(2,1)S(1)}, u32[]{:S(2)}, u32[]{:S(2)}) %collective-permute-start.46) | collective-permute-done | bytes 933920 | tf_op jit(solution)/shard_map/ppermute | solution.py:85
  214.2 15.4 %collective-permute-done.60.refs_2_ = bf16[2,4,96,768]{3,2,1,0:T(8,128)(2,1)S(1)} collective-permute-done((bf16[2,4,96,768]{3,2,1,0:T(8,128)(2,1)S(1)}, bf16[2,4,96,768]{3,2,1,0:T(8,128)(2,1)S(1)}, u32[]{:S(2)}, u32[]{:S(2)}) %collective-permute-start.60) | collective-permute-done | bytes 1179680 | tf_op jit(solution)/shard_map/ppermute | solution.py:85
  234.1 12.0 %collective-permute-done.61.refs_3_ = bf16[1,4,96,768]{3,2,1,0:T(8,128)(2,1)S(1)} collective-permute-done((bf16[1,4,96,768]{3,2,1,0:T(8,128)(2,1)S(1)}, bf16[1,4,96,768]{3,2,1,0:T(8,128)(2,1)S(1)}, u32[]{:S(2)}, u32[]{:S(2)}) %collective-permute-start.61) | collective-permute-done | bytes 589856 | tf_op jit(solution)/shard_map/ppermute | solution.py:85
  253.2 7.2 %collective-permute-done.63 = bf16[2,96,768]{2,1,0:T(8,128)(2,1)S(1)} collective-permute-done((bf16[2,96,768]{2,1,0:T(8,128)(2,1)S(1)}, bf16[2,96,768]{2,1,0:T(8,128)(2,1)S(1)}, u32[]{:S(2)}, u32[]{:S(2)}) %collective-permute-start.63) | collective-permute-done | bytes 294944 | tf_op jit(solution)/shard_map/ppermute | solution.py:85
  268.7 12.2 %collective-permute-done.56 = bf16[2,24,3840]{2,1,0:T(8,128)(2,1)S(1)} collective-permute-done((bf16[2,24,3840]{2,1,0:T(8,128)(2,1)S(1)}, bf16[2,24,3840]{2,1,0:T(8,128)(2,1)S(1)}, u32[]{:S(2)}, u32[]{:S(2)}) %collective-permute-start.56) | collective-permute-done | bytes 368672 | tf_op jit(solution)/shard_map/ppermute | solution.py:85
  (315 shorter events, 111.8 us)
Async XLA Ops:
  3.7 19.8 %collective-permute-start.27 = (bf16[96,768]{1,0:T(8,128)(2,1)}, bf16[96,768]{1,0:T(8,128)(2,1)S(1)}, u32[]{:S(2)}, u32[]{:S(2)}) collective-permute-start(bf16[96,768]{1,0:T(8,128)(2,1)} %bitcast.167), channel_id=1, source_target_pairs={{0,1},{1,0},{2,3},{3,2},{4,5},{5,4},{6,7},{7,6},{8,9},{9,8},{10,11... | collective-permute-start | bytes 442376 | tf_op jit(solution)/shard_map/ppermute | solution.py:85
  4.6 29.6 %collective-permute-start.17 = (bf16[24,3840]{1,0:T(8,128)(2,1)S(1)}, bf16[24,3840]{1,0:T(8,128)(2,1)S(1)}, u32[]{:S(2)}, u32[]{:S(2)}) collective-permute-start(bf16[24,3840]{1,0:T(8,128)(2,1)S(1)} %get-tuple-element.147), channel_id=1, source_target_pairs={{0,1},{1,0},{2,3},{3,2},{4,5},{5,4},{6,7},{7,6},{8,9},{9,8},{10,11... | collective-permute-start | bytes 552968 | tf_op jit(solution)/shard_map/ppermute | solution.py:85
  23.5 17.4 %collective-permute-start.29 = (bf16[2,96,768]{2,1,0:T(8,128)(2,1)S(1)}, bf16[2,96,768]{2,1,0:T(8,128)(2,1)}, u32[]{:S(2)}, u32[]{:S(2)}) collective-permute-start(bf16[2,96,768]{2,1,0:T(8,128)(2,1)S(1)} %maximum_select_fusion.1), channel_id=1, source_target_pairs={{0,16},{1,25},{2,18},{3,27},{4,20},{5,29},{6,22},{7,31},{8,24},{9,... | collective-permute-start | bytes 884744 | tf_op jit(solution)/shard_map/ppermute | solution.py:85
  23.6 18.7 %collective-permute-start.28 = (bf16[2,96,768]{2,1,0:T(8,128)(2,1)S(1)}, bf16[2,96,768]{2,1,0:T(8,128)(2,1)}, u32[]{:S(2)}, u32[]{:S(2)}) collective-permute-start(bf16[2,96,768]{2,1,0:T(8,128)(2,1)S(1)} %maximum_select_fusion.1), channel_id=1, source_target_pairs={{0,0},{1,9},{2,2},{3,11},{4,4},{5,13},{6,6},{7,15},{8,8},{9,17},{1... | collective-permute-start | bytes 884744 | tf_op jit(solution)/shard_map/ppermute | solution.py:85
  25.0 30.9 %collective-permute-start.3 = (bf16[2,2,24,2432]{3,2,1,0:T(8,128)(2,1)S(1)}, bf16[2,2,24,2432]{3,2,1,0:T(8,128)(2,1)S(1)}, u32[]{:S(2)}, u32[]{:S(2)}) collective-permute-start(bf16[2,2,24,2432]{3,2,1,0:T(8,128)(2,1)S(1)} %pad_maximum_fusion.2.refs_0_), channel_id=1, source_target_pairs={{0,2},{1,5},{2,0},{3,7},{4,6},{5,1},{6,4},{7,3},{8,10},{9,13},{10,... | collective-permute-start | bytes 1400840 | tf_op jit(solution)/shard_map/ppermute | solution.py:85
  31.8 24.2 %collective-permute-start.5 = (bf16[2,2,24,2432]{3,2,1,0:T(8,128)(2,1)S(1)}, bf16[2,2,24,2432]{3,2,1,0:T(8,128)(2,1)S(1)}, u32[]{:S(2)}, u32[]{:S(2)}) collective-permute-start(bf16[2,2,24,2432]{3,2,1,0:T(8,128)(2,1)S(1)} %collective-permute-done.4.refs_2_), channel_id=1, source_target_pairs={{0,2},{1,5},{2,0},{3,7},{4,6},{5,1},{6,4},{7,3},{8,10},{9,13},{10,... | collective-permute-start | bytes 1400840 | tf_op jit(solution)/shard_map/ppermute | solution.py:85
  34.3 21.1 %collective-permute-start.19 = (bf16[2,24,3840]{2,1,0:T(8,128)(2,1)S(1)}, bf16[2,24,3840]{2,1,0:T(8,128)(2,1)S(1)}, u32[]{:S(2)}, u32[]{:S(2)}) collective-permute-start(bf16[2,24,3840]{2,1,0:T(8,128)(2,1)S(1)} %maximum_select_fusion), channel_id=1, source_target_pairs={{0,16},{1,25},{2,18},{3,27},{4,20},{5,29},{6,22},{7,31},{8,24},{9,... | collective-permute-start | bytes 1105928 | tf_op jit(solution)/shard_map/ppermute | solution.py:85
  59.4 29.9 %collective-permute-start.21 = (bf16[2,2,24,3840]{3,2,1,0:T(8,128)(2,1)S(1)}, bf16[2,2,24,3840]{3,2,1,0:T(8,128)(2,1)}, u32[]{:S(2)}, u32[]{:S(2)}) collective-permute-start(bf16[2,2,24,3840]{3,2,1,0:T(8,128)(2,1)S(1)} %pad_maximum_fusion.refs_0_), channel_id=1, source_target_pairs={{0,4},{1,3},{2,6},{3,1},{4,0},{5,7},{6,2},{7,5},{8,12},{9,11},{10,... | collective-permute-start | bytes 2211848 | tf_op jit(solution)/shard_map/ppermute | solution.py:85
  60.3 33.1 %collective-permute-start.20 = (bf16[2,2,24,3840]{3,2,1,0:T(8,128)(2,1)S(1)}, bf16[2,2,24,3840]{3,2,1,0:T(8,128)(2,1)S(1)}, u32[]{:S(2)}, u32[]{:S(2)}) collective-permute-start(bf16[2,2,24,3840]{3,2,1,0:T(8,128)(2,1)S(1)} %pad_maximum_fusion.refs_0_), channel_id=1, source_target_pairs={{0,2},{1,5},{2,0},{3,7},{4,6},{5,1},{6,4},{7,3},{8,10},{9,13},{10,... | collective-permute-start | bytes 2211848 | tf_op jit(solution)/shard_map/ppermute | solution.py:85
  68.9 20.4 %collective-permute-start.10 = (bf16[128,576]{1,0:T(8,128)(2,1)S(1)}, bf16[128,576]{1,0:T(8,128)(2,1)S(1)}, u32[]{:S(2)}, u32[]{:S(2)}) collective-permute-start(bf16[128,576]{1,0:T(8,128)(2,1)S(1)} %get-tuple-element.63), channel_id=1, source_target_pairs={{0,8},{1,9},{2,10},{3,11},{4,12},{5,13},{6,14},{7,15},{8,16},{9,17... | collective-permute-start | bytes 442376 | tf_op jit(solution)/shard_map/ppermute | solution.py:85
  93.4 17.6 %collective-permute-start.13 = (bf16[512,384]{1,0:T(8,128)(2,1)}, bf16[512,384]{1,0:T(8,128)(2,1)}, u32[]{:S(2)}, u32[]{:S(2)}) collective-permute-start(bf16[512,384]{1,0:T(8,128)(2,1)} %shard_map.275.refs_5_.refs_4_), channel_id=1, source_target_pairs={{0,4},{1,5},{2,6},{3,7},{4,0},{5,1},{6,2},{7,3},{8,12},{9,13},{10,... | collective-permute-start | bytes 1179656 | tf_op jit(solution)/shard_map/ppermute | solution.py:85
  97.9 47.7 %collective-permute-start.23 = (bf16[2,2,24,3840]{3,2,1,0:T(8,128)(2,1)}, bf16[2,2,24,3840]{3,2,1,0:T(8,128)(2,1)S(1)}, u32[]{:S(2)}, u32[]{:S(2)}) collective-permute-start(bf16[2,2,24,3840]{3,2,1,0:T(8,128)(2,1)} %copy-done), channel_id=1, source_target_pairs={{0,1},{1,0},{2,3},{3,2},{4,5},{5,4},{6,7},{7,6},{8,9},{9,8},{10,11... | collective-permute-start | bytes 2211848 | tf_op jit(solution)/shard_map/ppermute | solution.py:85
  99.6 46.0 %collective-permute-start.25 = (bf16[2,2,24,3840]{3,2,1,0:T(8,128)(2,1)}, bf16[2,2,24,3840]{3,2,1,0:T(8,128)(2,1)S(1)}, u32[]{:S(2)}, u32[]{:S(2)}) collective-permute-start(bf16[2,2,24,3840]{3,2,1,0:T(8,128)(2,1)} %collective-permute-done.21.refs_2_), channel_id=1, source_target_pairs={{0,1},{1,0},{2,3},{3,2},{4,5},{5,4},{6,7},{7,6},{8,9},{9,8},{10,11... | collective-permute-start | bytes 2211848 | tf_op jit(solution)/shard_map/ppermute | solution.py:85
  100.9 44.7 %collective-permute-start.24 = (bf16[2,2,24,3840]{3,2,1,0:T(8,128)(2,1)}, bf16[2,2,24,3840]{3,2,1,0:T(8,128)(2,1)S(1)}, u32[]{:S(2)}, u32[]{:S(2)}) collective-permute-start(bf16[2,2,24,3840]{3,2,1,0:T(8,128)(2,1)} %copy-done.20), channel_id=1, source_target_pairs={{0,1},{1,0},{2,3},{3,2},{4,5},{5,4},{6,7},{7,6},{8,9},{9,8},{10,11... | collective-permute-start | bytes 2211848 | tf_op jit(solution)/shard_map/ppermute | solution.py:85
  107.5 21.0 %collective-permute-start.36 = (bf16[2,2,96,768]{3,2,1,0:T(8,128)(2,1)}, bf16[2,2,96,768]{3,2,1,0:T(8,128)(2,1)S(1)}, u32[]{:S(2)}, u32[]{:S(2)}) collective-permute-start(bf16[2,2,96,768]{3,2,1,0:T(8,128)(2,1)} %collective-permute-done.32.refs_3_), channel_id=1, source_target_pairs={{0,1},{1,0},{2,3},{3,2},{4,5},{5,4},{6,7},{7,6},{8,9},{9,8},{10,11... | collective-permute-start | bytes 1769480 | tf_op jit(solution)/shard_map/ppermute | solution.py:85
  111.0 34.6 %collective-permute-start.26 = (bf16[2,2,24,3840]{3,2,1,0:T(8,128)(2,1)}, bf16[2,2,24,3840]{3,2,1,0:T(8,128)(2,1)S(1)}, u32[]{:S(2)}, u32[]{:S(2)}) collective-permute-start(bf16[2,2,24,3840]{3,2,1,0:T(8,128)(2,1)} %collective-permute-done.22.refs_3_), channel_id=1, source_target_pairs={{0,1},{1,0},{2,3},{3,2},{4,5},{5,4},{6,7},{7,6},{8,9},{9,8},{10,11... | collective-permute-start | bytes 2211848 | tf_op jit(solution)/shard_map/ppermute | solution.py:85
  200.3 29.3 %collective-permute-start.60 = (bf16[2,4,96,768]{3,2,1,0:T(8,128)(2,1)S(1)}, bf16[2,4,96,768]{3,2,1,0:T(8,128)(2,1)S(1)}, u32[]{:S(2)}, u32[]{:S(2)}) collective-permute-start(bf16[2,4,96,768]{3,2,1,0:T(8,128)(2,1)S(1)} %shard_map.296), channel_id=1, source_target_pairs={{0,4},{1,3},{2,6},{3,1},{4,0},{5,7},{6,2},{7,5},{8,12},{9,11},{10,... | collective-permute-start | bytes 3538952 | tf_op jit(solution)/shard_map/ppermute | solution.py:85
  200.9 47.4 %collective-permute-start.51 = (bf16[2,4,24,3840]{3,2,1,0:T(8,128)(2,1)S(1)}, bf16[2,4,24,3840]{3,2,1,0:T(8,128)(2,1)S(1)}, u32[]{:S(2)}, u32[]{:S(2)}) collective-permute-start(bf16[2,4,24,3840]{3,2,1,0:T(8,128)(2,1)S(1)} %get-tuple-element.94), channel_id=1, source_target_pairs={{0,1},{1,0},{2,3},{3,2},{4,5},{5,4},{6,7},{7,6},{8,9},{9,8},{10,11... | collective-permute-start | bytes 4423688 | tf_op jit(solution)/shard_map/ppermute | solution.py:85
  202.2 49.5 %collective-permute-start.53 = (bf16[2,4,24,3840]{3,2,1,0:T(8,128)(2,1)S(1)}, bf16[2,4,24,3840]{3,2,1,0:T(8,128)(2,1)S(1)}, u32[]{:S(2)}, u32[]{:S(2)}) collective-permute-start(bf16[2,4,24,3840]{3,2,1,0:T(8,128)(2,1)S(1)} %shard_map.291), channel_id=1, source_target_pairs={{0,4},{1,3},{2,6},{3,1},{4,0},{5,7},{6,2},{7,5},{8,12},{9,11},{10,... | collective-permute-start | bytes 4423688 | tf_op jit(solution)/shard_map/ppermute | solution.py:85
  212.2 18.2 %collective-permute-start.47 = (bf16[1,4,24,2432]{3,2,1,0:T(8,128)(2,1)S(1)}, bf16[1,4,24,2432]{3,2,1,0:T(8,128)(2,1)S(1)}, u32[]{:S(2)}, u32[]{:S(2)}) collective-permute-start(bf16[1,4,24,2432]{3,2,1,0:T(8,128)(2,1)S(1)} %bitcast.147), channel_id=1, source_target_pairs={{0,2},{1,5},{2,0},{3,7},{4,6},{5,1},{6,4},{7,3},{8,10},{9,13},{10,... | collective-permute-start | bytes 1400840 | tf_op jit(solution)/shard_map/ppermute | solution.py:85
  230.5 22.0 %collective-permute-start.49 = (bf16[2,24,2432]{2,1,0:T(8,128)(2,1)S(1)}, bf16[2,24,2432]{2,1,0:T(8,128)(2,1)S(1)}, u32[]{:S(2)}, u32[]{:S(2)}) collective-permute-start(bf16[2,24,2432]{2,1,0:T(8,128)(2,1)S(1)} %bitcast.153), channel_id=1, source_target_pairs={{0,16},{1,25},{2,18},{3,27},{4,20},{5,29},{6,22},{7,31},{8,24},{9,... | collective-permute-start | bytes 700424 | tf_op jit(solution)/shard_map/ppermute | solution.py:85
  232.5 20.1 %collective-permute-start.48 = (bf16[2,24,2432]{2,1,0:T(8,128)(2,1)S(1)}, bf16[2,24,2432]{2,1,0:T(8,128)(2,1)S(1)}, u32[]{:S(2)}, u32[]{:S(2)}) collective-permute-start(bf16[2,24,2432]{2,1,0:T(8,128)(2,1)S(1)} %bitcast.154), channel_id=1, source_target_pairs={{0,0},{1,9},{2,2},{3,11},{4,4},{5,13},{6,6},{7,15},{8,8},{9,17},{1... | collective-permute-start | bytes 700424 | tf_op jit(solution)/shard_map/ppermute | solution.py:85
  260.4 20.7 %collective-permute-start.64 = (bf16[96,768]{1,0:T(8,128)(2,1)S(1)}, bf16[96,768]{1,0:T(8,128)(2,1)S(1)}, u32[]{:S(2)}, u32[]{:S(2)}) collective-permute-start(bf16[96,768]{1,0:T(8,128)(2,1)S(1)} %fusion.41), channel_id=1, source_target_pairs={{0,1},{1,0},{2,3},{3,2},{4,5},{5,4},{6,7},{7,6},{8,9},{9,8},{10,11... | collective-permute-start | bytes 442376 | tf_op jit(solution)/shard_map/ppermute | solution.py:85
  263.7 17.2 %collective-permute-start.56 = (bf16[2,24,3840]{2,1,0:T(8,128)(2,1)S(1)}, bf16[2,24,3840]{2,1,0:T(8,128)(2,1)S(1)}, u32[]{:S(2)}, u32[]{:S(2)}) collective-permute-start(bf16[2,24,3840]{2,1,0:T(8,128)(2,1)S(1)} %bitcast.149), channel_id=1, source_target_pairs={{0,16},{1,25},{2,18},{3,27},{4,20},{5,29},{6,22},{7,31},{8,24},{9,... | collective-permute-start | bytes 1105928 | tf_op jit(solution)/shard_map/ppermute | solution.py:85
  (95 other events, 897.7 us)
